TPU v7x, 128 devices: a whole 4x4x4 slice. The times are simulated.
128 devices in a mesh: ctx: 32 (over y, z, core), head: 4 (over x).
Axes of the slice: x: 4, y: 4, z: 4, core: 2. Of those that a mesh axis runs over, the one named last changes fastest.
Arguments:
- query_rows: bfloat16 [8192, 4096], P('ctx', 'head'), may hold values from -6 to 6
- key_rows: bfloat16 [8192, 4096], P('ctx', 'head')
- value_rows: bfloat16 [8192, 4096], P('ctx', 'head'), may hold values from -6 to 6
- beta: float32 [8192, 32], P('ctx', 'head'), may hold values from 0 to 2
- norm_gain: float32 [128], replicated, may hold values from 0.1 to 1.9
- out_cotangent: bfloat16 [8192, 4096], P('ctx', 'head'), may hold values from -0.125 to 0.125
Outputs:
- attended: bfloat16 [8192, 4096], P('ctx', 'head')
- weight_grad: float32 [4096, 4096], P('ctx', 'head')
All inputs are finite; a program needn't handle non-finite values.
Results may differ from a plain program's by a relative error of at most 0.0029.
Values may be sent and summed in bfloat16 or wider, within the bound.
No kernel may reach another device: no remote copies, remote signals or barrier semaphores. Data moves between devices by JAX's collectives and lax.ppermute only.
A program may use at most 128 MiB of HBM per device.

v0:
```python
import jax
import jax.numpy as jnp
from jax import lax
from jax.experimental import pallas as pl
from jax.experimental.pallas import tpu as pltpu
from jax.sharding import Mesh, PartitionSpec as P

F = 128
TOK = 256
HEADS = 8
EPS = 1e-06
f32 = jnp.float32
bf16 = jnp.bfloat16


def split(x):
    h = x.astype(bf16)
    return h, (x - h.astype(f32)).astype(bf16)


def dot(a, b):
    return jnp.dot(a, b, preferred_element_type=f32)


def dot_nt(a, b):
    return lax.dot_general(a, b, (((1,), (1,)), ((), ())), preferred_element_type=f32)


def dot_tn(a, b):
    return lax.dot_general(a, b, (((0,), (0,)), ((), ())), preferred_element_type=f32)


def lhs_of(s):
    return jnp.concatenate(s, axis=1)


def rhs_of(s):
    y = jnp.concatenate(s, axis=1)
    return jnp.concatenate([y, y], axis=0)


def mm(a, b):
    o = dot(lhs_of(a), rhs_of(b))
    return o[:, :F] + o[:, F:]


def mm_all(pairs):
    return [mm(a, b) for a, b in pairs]


def map_product(p, r):
    ph, pl_ = split(p)
    rh, rl = split(r)
    return dot(jnp.concatenate([ph, pl_], axis=1), jnp.concatenate([rh, rh], axis=0)) + dot(ph, rl)


HB = 2


def local_kernel(k_ref, v_ref, b_ref, map_ref, xh_ref, xl_ref, r_ref):
    g = pl.program_id(0)
    beta_all = b_ref[...]
    lane8 = lax.broadcasted_iota(jnp.int32, (TOK, HEADS), 1)
    lane = lax.broadcasted_iota(jnp.int32, (TOK, F), 1)
    row = lax.broadcasted_iota(jnp.int32, (F, F), 0)
    col = lax.broadcasted_iota(jnp.int32, (F, F), 1)
    eye = (row == col).astype(f32)
    strict = row > col
    in16 = jnp.logical_and(strict, (row // 16) == (col // 16))
    in64 = jnp.logical_and((row // 64) == (col // 64), (row // 16) > (col // 16))
    in128 = (row // 64) > (col // 64)

    stat = jnp.zeros((TOK, F), f32)
    ks, rs, bs, kraw = [], [], [], []
    for i in range(HB):
        k = k_ref[:, i * F:(i + 1) * F]
        kf = k.astype(f32)
        r = lax.rsqrt(jnp.sum(kf * kf, axis=-1, keepdims=True) + EPS)
        kf = jnp.where(r > 0.0, kf, 0.0)
        b = jnp.sum(jnp.where(lane8 == g * HB + i, beta_all, 0.0), axis=-1, keepdims=True)
        ks.append(kf)
        kraw.append(kf.astype(bf16))
        rs.append(r)
        bs.append(b)
        stat = jnp.where(lane == 2 * i, r, stat)
        stat = jnp.where(lane == 2 * i + 1, b, stat)
    stat_t = jnp.transpose(stat)
    r_ref[0] = stat_t[0:8, :]

    tiles = []
    cross = []
    for i in range(HB):
        r_row = stat_t[2 * i:2 * i + 1, :]
        br = bs[i] * rs[i]
        k1, k2 = kraw[i][:F], kraw[i][F:]
        g11 = dot_nt(k1, k1)
        g2 = dot_nt(k2, kraw[i])
        a11 = g11 * br[:F] * r_row[:, :F]
        a2 = g2 * br[F:] * r_row
        tiles += [a11, a2[:, F:]]
        cross.append(a2[:, :F])
    n = [jnp.where(in16, a, 0.0) for a in tiles]
    ns = [split(a) for a in n]
    n2 = mm_all(zip(ns, ns))
    n2s = [split(a) for a in n2]
    n4 = mm_all(zip(n2s, n2s))
    q1 = mm_all(zip(ns, n2s))
    n4s = [split(a) for a in n4]
    r1 = [eye - a + b - c for a, b, c in zip(n, n2, q1)]
    n8 = mm_all(zip(n4s, n4s))
    q2 = mm_all(zip([split(a) for a in r1], n4s))
    r2 = [a + b for a, b in zip(r1, q2)]
    q3 = mm_all(zip([split(a) for a in r2], [split(a) for a in n8]))
    d = [a + b for a, b in zip(r2, q3)]
    ds = [split(a) for a in d]
    m = mm_all(zip(ds, [split(jnp.where(in64, a, 0.0)) for a in tiles]))
    ms = [split(a) for a in m]
    m2 = mm_all(zip(ms, ms))
    e = [a + b for a, b in zip(d, mm_all(zip([split(a) for a in m2], ds)))]
    t = [a - b for a, b in zip(e, mm_all(zip(ms, [split(a) for a in e])))]
    ts = [split(a) for a in t]
    u = mm_all(zip([split(jnp.where(in128, a, 0.0)) for a in tiles], ts))
    t = [a - b for a, b in zip(t, mm_all(zip(ts, [split(a) for a in u])))]
    ts = [split(a) for a in t]
    c1 = mm_all(zip([split(a) for a in cross], ts[0::2]))
    t21 = [-a for a in mm_all(zip(ts[1::2], [split(a) for a in c1]))]

    for i in range(HB):
        b_row = stat_t[2 * i + 1:2 * i + 2, :]
        t11h, t11l = split(t[2 * i] * b_row[:, :F])
        t2h, t2l = split(jnp.concatenate([t21[i], t[2 * i + 1]], axis=1) * b_row)
        kn = ks[i] * rs[i]
        knh, knl = split(kn)
        v = v_ref[:, i * F:(i + 1) * F]
        bh = jnp.concatenate([knh, v], axis=1)
        bh1 = bh[:F]
        x1 = dot(jnp.concatenate([t11h, t11l], axis=1), jnp.concatenate([bh1, bh1], axis=0))
        x2 = dot(t2h, bh) + dot(t2l, bh)
        y1 = dot(t11h, knl[:F])
        y2 = dot(t2h, knl)
        x = jnp.concatenate([x1, x2], axis=0)
        y = jnp.concatenate([y1, y2], axis=0)
        x = jnp.concatenate([x[:, :F] + y, x[:, F:]], axis=1)
        xh, xl = split(x)
        xh_ref[i] = xh
        xl_ref[i] = xl
        zh, zl = split(x * rs[i])
        pw = dot_tn(kraw[i], zh) + dot_tn(kraw[i], zl)
        map_ref[i] = jnp.concatenate([eye - pw[:, :F], pw[:, F:]], axis=1)


def local_maps(k, v, beta):
    steps = HEADS // HB
    return pl.pallas_call(
        local_kernel,
        grid=(steps,),
        in_specs=[
            pl.BlockSpec((TOK, HB * F), lambda g: (0, g)),
            pl.BlockSpec((TOK, HB * F), lambda g: (0, g)),
            pl.BlockSpec((TOK, HEADS), lambda g: (0, 0)),
        ],
        out_specs=[
            pl.BlockSpec((HB, F, 2 * F), lambda g: (g, 0, 0)),
            pl.BlockSpec((HB, TOK, 2 * F), lambda g: (g, 0, 0)),
            pl.BlockSpec((HB, TOK, 2 * F), lambda g: (g, 0, 0)),
            pl.BlockSpec((1, 8, TOK), lambda g: (g, 0, 0)),
        ],
        out_shape=[
            jax.ShapeDtypeStruct((HEADS, F, 2 * F), f32),
            jax.ShapeDtypeStruct((HEADS, TOK, 2 * F), bf16),
            jax.ShapeDtypeStruct((HEADS, TOK, 2 * F), bf16),
            jax.ShapeDtypeStruct((steps, 8, TOK), f32),
        ],
        name="local_maps",
    )(k, v, beta)


def reads_kernel(q_ref, k_ref, xh_ref, xl_ref, r_ref, qh_ref, ql_ref, y_ref):
    row = lax.broadcasted_iota(jnp.int32, (TOK, TOK), 0)
    col = lax.broadcasted_iota(jnp.int32, (TOK, TOK), 1)
    causal = row >= col
    for i in range(HB):
        q = q_ref[:, i * F:(i + 1) * F]
        k = k_ref[:, i * F:(i + 1) * F]
        r_row = r_ref[0, 2 * i:2 * i + 1, :]
        s = dot_nt(q, k) * r_row
        s = jnp.where(jnp.logical_and(causal, r_row > 0.0), s, 0.0)
        sh, sl = split(s)
        xh, xl = xh_ref[i], xl_ref[i]
        o = dot(sh, xh) + (dot(sl, xh) + dot(sh, xl))
        qe = q.astype(f32) - o[:, :F]
        qh, ql = split(qe)
        qh_ref[i] = qh
        ql_ref[i] = ql
        y_ref[i] = o[:, F:]


def local_reads(q, k, xh, xl, r):
    steps = HEADS // HB
    per = pl.BlockSpec((HB, TOK, F), lambda g: (g, 0, 0))
    return pl.pallas_call(
        reads_kernel,
        grid=(steps,),
        in_specs=[
            pl.BlockSpec((TOK, HB * F), lambda g: (0, g)),
            pl.BlockSpec((TOK, HB * F), lambda g: (0, g)),
            pl.BlockSpec((HB, TOK, 2 * F), lambda g: (g, 0, 0)),
            pl.BlockSpec((HB, TOK, 2 * F), lambda g: (g, 0, 0)),
            pl.BlockSpec((1, 8, TOK), lambda g: (g, 0, 0)),
        ],
        out_specs=[per, per, per],
        out_shape=[
            jax.ShapeDtypeStruct((HEADS, TOK, F), bf16),
            jax.ShapeDtypeStruct((HEADS, TOK, F), bf16),
            jax.ShapeDtypeStruct((HEADS, TOK, F), f32),
        ],
        name="local_reads",
    )(q, k, xh, xl, r)


def after(p_then, m):
    o = map_product(p_then[:, :F], m)
    return jnp.concatenate([o[:, :F], o[:, F:] + p_then[:, F:]], axis=1)


def scalar_call(kernel, scalar, out_shape, name, *args):
    whole = lambda a: pl.BlockSpec(a.shape, lambda i, s: (0,) * len(a.shape))
    return pl.pallas_call(
        kernel,
        grid_spec=pltpu.PrefetchScalarGridSpec(
            num_scalar_prefetch=1,
            grid=(1,),
            in_specs=[whole(a) for a in args],
            out_specs=jax.tree.map(whole, out_shape),
        ),
        out_shape=out_shape,
        name=name,
    )(scalar.astype(jnp.int32).reshape(1), *args)


def pair_kernel(c_ref, own_ref, got_ref, out_ref):
    c = c_ref[0]
    for j in range(4):
        own = own_ref[4 * c + j]
        got = got_ref[j]
        first = jnp.where(c == 0, own, got)
        second = jnp.where(c == 0, got, own)
        out_ref[j] = after(second, first)


def chain_kernel(z_ref, maps_ref, out_ref):
    m = maps_ref[0]
    out_ref[0] = m
    for j in range(1, 4):
        m = after(maps_ref[j], m)
        out_ref[j] = m


def apply_map(m, s):
    return mm(split(m[:, :F]), split(s)) + m[:, F:]


def plane_kernel(y_ref, m3_ref, m2_ref, m1_ref, pre_ref, out_ref):
    y = y_ref[0]
    s = jnp.where(y >= 3, m3_ref[:, F:], 0.0)
    s = jnp.where(y >= 2, apply_map(m2_ref[...], s), 0.0)
    s = jnp.where(y >= 1, apply_map(m1_ref[...], s), 0.0)
    out_ref[0] = s
    for j in range(3):
        out_ref[j + 1] = apply_map(pre_ref[j], s)


def starts_kernel(c_ref, s_ref, own_ref, got_ref, mine_ref, send_ref):
    c = c_ref[0]
    for j in range(4):
        s = s_ref[j]
        first = jnp.where(c == 0, own_ref[4 * c + j], got_ref[j])
        t = apply_map(first, s)
        mine_ref[j] = jnp.where(c == 0, s, t)
        send_ref[j] = jnp.where(c == 0, t, s)


def out_kernel(c_ref, qh_ref, ql_ref, y_ref, mine_ref, got_ref, g_ref, o_ref):
    h = pl.program_id(0)
    c = c_ref[0]
    for i in range(HB):
        hh = h * HB + i
        j = lax.rem(hh, 4)
        s = jnp.where(lax.div(hh, 4) == c, mine_ref[j], got_ref[j])
        mixed = mm((qh_ref[i], ql_ref[i]), split(s)) + y_ref[i]
        ms = jnp.mean(mixed * mixed, axis=-1, keepdims=True)
        o_ref[:, i * F:(i + 1) * F] = (mixed * lax.rsqrt(ms + EPS) * g_ref[...]).astype(bf16)


def outputs(c, qh, ql, y, mine, got, gain):
    per = pl.BlockSpec((HB, TOK, F), lambda g, s: (g, 0, 0))
    st = pl.BlockSpec((4, F, F), lambda g, s: (0, 0, 0))
    return pl.pallas_call(
        out_kernel,
        grid_spec=pltpu.PrefetchScalarGridSpec(
            num_scalar_prefetch=1,
            grid=(HEADS // HB,),
            in_specs=[per, per, per, st, st, pl.BlockSpec((1, F), lambda g, s: (0, 0))],
            out_specs=pl.BlockSpec((TOK, HB * F), lambda g, s: (0, g)),
        ),
        out_shape=jax.ShapeDtypeStruct((TOK, HEADS * F), bf16),
        name="outputs",
    )(c.astype(jnp.int32).reshape(1), qh, ql, y, mine, got, gain.reshape(1, F))


def shift(x, axis, k):
    return lax.ppermute(x, axis, [(i, (i + k) % 4) for i in range(4)])


def swap(x, axis, k):
    n = 2 if axis == "core" else 4
    return lax.ppermute(x, axis, [(i, i ^ k) for i in range(n)])


def pick(x, i):
    return lax.dynamic_index_in_dim(x, i, 0, False)


def put(x, b, i):
    return lax.dynamic_update_index_in_dim(x, b, i, 0)


def on_device(query_rows, key_rows, value_rows, beta, norm_gain, out_cotangent):
    yi, zi, ci, hi = (lax.axis_index(a) for a in ("y", "z", "core", "head"))

    cot = out_cotangent.reshape(TOK, 4, 2, F)
    cot = jnp.stack([
        lax.dynamic_index_in_dim(cot, 1 - ci, 2, False).reshape(TOK, 4 * F),
        lax.dynamic_index_in_dim(cot, ci, 2, False).reshape(TOK, 4 * F),
    ])
    cot = lax.ppermute(cot, ("y", "head"), [(a * 4 + b, b * 4 + a) for a in range(4) for b in range(4)])
    cots = put(jnp.zeros((4,) + cot.shape, bf16), cot, (yi - hi) % 4)
    for k in (1, 2, 3):
        cots = put(cots, shift(cot, "head", k), (yi - hi + k) % 4)

    maps, xh, xl, r = local_maps(key_rows, value_rows, beta)
    got = swap(lax.dynamic_slice_in_dim(maps, 4 * (1 - ci), 4, 0), "core", 1)
    comb = scalar_call(pair_kernel, ci, jax.ShapeDtypeStruct((4, F, 2 * F), f32), "pair", maps, got)
    chain = put(jnp.zeros_like(comb), pick(comb, zi), zi)
    for k in (1, 2, 3):
        chain = put(chain, shift(pick(comb, (zi + k) % 4), "z", k), (zi - k) % 4)
    qh, ql, yl = local_reads(query_rows, key_rows, xh, xl, r)
    pre = scalar_call(chain_kernel, zi, jax.ShapeDtypeStruct((4, F, 2 * F), f32), "chain", chain)
    m1, m2, m3 = (shift(pre[3], "y", k) for k in (1, 2, 3))
    sc = scalar_call(plane_kernel, yi, jax.ShapeDtypeStruct((4, F, F), f32), "plane", m3, m2, m1, pre)
    sx = put(jnp.zeros_like(sc), pick(sc, zi), zi)
    for k in (1, 2, 3):
        sx = put(sx, shift(pick(sc, (zi + k) % 4), "z", k), (zi - k) % 4)
    half = jax.ShapeDtypeStruct((4, F, F), f32)
    mine, send = scalar_call(starts_kernel, ci, (half, half), "starts", sx, maps, got)
    theirs = swap(send, "core", 1)
    attended = outputs(ci, qh, ql, yl, mine, theirs, norm_gain)

    a_up = shift(attended, "y", 1)
    a_dn = shift(attended, "y", -1)
    h = HEADS * F // 2
    far = jnp.concatenate([shift(a_up[:, :h], "y", 1), shift(a_dn[:, h:], "y", -1)], axis=1)
    att = jnp.concatenate([attended, a_up, far, a_dn], axis=0)
    cs = cots[:, 0].reshape(4 * TOK, 4 * F)
    ck = cots[:, 1].reshape(4 * TOK, 4 * F)
    w_send = dot_tn(cs, att).astype(bf16)
    w_got = swap(w_send, "core", 1)
    w = (dot_tn(ck, att) + w_got.astype(f32)).reshape(4, F, HEADS * F)

    def halving(w, first, second):
        z1, z2, z3 = zi ^ first, zi ^ first ^ second, zi ^ second
        s = swap(jnp.stack([pick(w, z1), pick(w, z2)]).astype(bf16), "z", first).astype(f32)
        keep, on = pick(w, zi) + s[0], pick(w, z3) + s[1]
        return keep + swap(on.astype(bf16), "z", second).astype(f32)

    grad = jnp.concatenate([halving(w[:, :, :h], 1, 3), halving(w[:, :, h:], 3, 1)], axis=1)
    return attended, grad


def solution(mesh):
    fine = Mesh(mesh.devices.reshape(4, 4, 2, 4), ("y", "z", "core", "head"))
    spec = P(("y", "z", "core"), "head")
    return jax.shard_map(
        on_device,
        mesh=fine,
        in_specs=(spec, spec, spec, spec, P(), spec),
        out_specs=(spec, spec),
        check_vma=False,
    )
```

profile of v0, /device:TPU:0, one launch (start us, length us, event | category | flops | bytes accessed | tf_op | source)
XLA Modules:
  0.0 148.7 jit_solution(2108765664633204515)
XLA Ops:
  0.6 1.5 %copy.10.b_ref = f32[256,8]{1,0:T(8,128)} copy(f32[256,8]{0,1:T(8,128)} %param.9) | data formatting | bytes 16384 | tf_op args[3]
  2.2 13.9 %local_maps.1 = (f32[8,128,256]{2,1,0:T(8,128)}, bf16[8,256,256]{2,1,0:T(8,128)(2,1)}, bf16[8,256,256]{2,1,0:T(8,128)(2,1)}, f32[4,8,256]{2,1,0:T(8,128)}) custom-call(bf16[256,1024]{1,0:T(8,128)(2,1)} %k_ref.3, bf16[256,1024]{1,0:T(8,128)(2,1)} %v_ref.1, f32[256,8]{1,0:T(8,128)} %copy.10.b_ref), custom_call_target="tpu_custom_call" | custom-call | tf_op jit(solution)/shard_map/local_maps/pallas_call | solution.py:154
  17.5 1.6 %collective-permute-done.got_ref = f32[4,128,256]{2,1,0:T(8,128)S(1)} collective-permute-done((f32[4,128,256]{2,1,0:T(8,128)S(1)}, f32[4,128,256]{2,1,0:T(8,128)S(1)}, u32[]{:S(2)}, u32[]{:S(2)}) %collective-permute-start) | collective-permute-done | bytes 524320 | tf_op jit(solution)/shard_map/ppermute | solution.py:317
  19.9 2.5 %pair.1 = f32[4,128,256]{2,1,0:T(8,128)} custom-call(s32[1]{0:T(128)} %bitcast.c_ref, f32[8,128,256]{2,1,0:T(8,128)} %get-tuple-element.17.own_ref, f32[4,128,256]{2,1,0:T(8,128)} %copy-done), custom_call_target="tpu_custom_call" | custom-call | tf_op jit(solution)/shard_map/pair/pallas_call | solution.py:228
  23.6 2.1 %collective-permute-start.1 = (f32[128,256]{1,0:T(8,128)S(1)}, f32[128,256]{1,0:T(8,128)S(1)}, u32[]{:S(2)}, u32[]{:S(2)}) collective-permute-start(f32[128,256]{1,0:T(8,128)S(1)} %get-tuple-element.32), channel_id=1, source_target_pairs={{0,8},{8,16},{16,24},{24,0},{1,9},{9,17},{17,25},{25,1},{2,10},{10... | collective-permute-start | bytes 393224 | tf_op jit(solution)/shard_map/ppermute | solution.py:312
  27.2 3.6 %collective-permute-start.2 = (f32[128,256]{1,0:T(8,128)S(1)}, f32[128,256]{1,0:T(8,128)S(1)}, u32[]{:S(2)}, u32[]{:S(2)}) collective-permute-start(f32[128,256]{1,0:T(8,128)S(1)} %get-tuple-element.31), channel_id=1, source_target_pairs={{0,16},{8,24},{16,0},{24,8},{1,17},{9,25},{17,1},{25,9},{2,18},{10... | collective-permute-start | bytes 393224 | tf_op jit(solution)/shard_map/ppermute | solution.py:312
  31.8 3.7 %collective-permute-done.2 = f32[128,256]{1,0:T(8,128)S(1)} collective-permute-done((f32[128,256]{1,0:T(8,128)S(1)}, f32[128,256]{1,0:T(8,128)S(1)}, u32[]{:S(2)}, u32[]{:S(2)}) %collective-permute-start.2) | collective-permute-done | bytes 131104 | tf_op jit(solution)/shard_map/ppermute | solution.py:312
  37.4 2.4 %chain.1.pre_ref = f32[4,128,256]{2,1,0:T(8,128)} custom-call(s32[1]{0:T(128)} %bitcast.2.z_ref, f32[4,128,256]{2,1,0:T(8,128)} %copy-done.2), custom_call_target="tpu_custom_call" | custom-call | tf_op jit(solution)/shard_map/chain/pallas_call | solution.py:228
  40.7 5.8 %collective-permute-start.4 = (f32[128,256]{1,0:T(8,128)S(1)}, f32[128,256]{1,0:T(8,128)S(1)}, u32[]{:S(2)}, u32[]{:S(2)}) collective-permute-start(f32[128,256]{1,0:T(8,128)S(1)} %slice_bitcast_fusion), channel_id=1, source_target_pairs={{0,96},{32,0},{64,32},{96,64},{1,97},{33,1},{65,33},{97,65},{2,98}... | collective-permute-start | bytes 393224 | tf_op jit(solution)/shard_map/ppermute | solution.py:312
  48.5 9.7 %collective-permute-done.4.m3_ref = f32[128,256]{1,0:T(8,128)S(1)} collective-permute-done((f32[128,256]{1,0:T(8,128)S(1)}, f32[128,256]{1,0:T(8,128)S(1)}, u32[]{:S(2)}, u32[]{:S(2)}) %collective-permute-start.4) | collective-permute-done | bytes 131104 | tf_op jit(solution)/shard_map/ppermute | solution.py:312
  58.9 2.5 %plane.1 = f32[4,128,128]{2,1,0:T(8,128)} custom-call(s32[1]{0:T(128)} %bitcast.1.y_ref, f32[128,256]{1,0:T(8,128)} %copy-done.9, f32[128,256]{1,0:T(8,128)} %copy-done.10, f32[128,256]{1,0:T(8,128)} %copy-done.11, f32[4,128,256]{2,1,0:T(8,128)} %chain.1.pre_ref), custom_call_target="tpu_custom_call" | custom-call | tf_op jit(solution)/shard_map/plane/pallas_call | solution.py:228
  62.4 2.1 %collective-permute-start.7 = (f32[128,128]{1,0:T(8,128)S(1)}, f32[128,128]{1,0:T(8,128)S(1)}, u32[]{:S(2)}, u32[]{:S(2)}) collective-permute-start(f32[128,128]{1,0:T(8,128)S(1)} %get-tuple-element.36), channel_id=1, source_target_pairs={{0,8},{8,16},{16,24},{24,0},{1,9},{9,17},{17,25},{25,1},{2,10},{10... | collective-permute-start | bytes 196616 | tf_op jit(solution)/shard_map/ppermute | solution.py:312
  64.6 5.0 %collective-permute-start.13 = (bf16[2,256,512]{1,2,0:T(8,128)(2,1)}, bf16[2,256,512]{1,2,0:T(8,128)(2,1)S(1)}, u32[]{:S(2)}, u32[]{:S(2)}) collective-permute-start(bf16[2,256,512]{1,2,0:T(8,128)(2,1)} %collective-permute-done.11), channel_id=1, source_target_pairs={{0,2},{1,3},{2,0},{3,1},{4,6},{5,7},{6,4},{7,5},{8,10},{9,11},{10,... | collective-permute-start | bytes 1572872 | tf_op jit(solution)/shard_map/ppermute | solution.py:312
  70.7 2.0 %collective-permute-start.8 = (f32[128,128]{1,0:T(8,128)S(1)}, f32[128,128]{1,0:T(8,128)S(1)}, u32[]{:S(2)}, u32[]{:S(2)}) collective-permute-start(f32[128,128]{1,0:T(8,128)S(1)} %get-tuple-element.35), channel_id=1, source_target_pairs={{0,16},{8,24},{16,0},{24,8},{1,17},{9,25},{17,1},{25,9},{2,18},{10... | collective-permute-start | bytes 196616 | tf_op jit(solution)/shard_map/ppermute | solution.py:312
  72.7 2.3 %collective-permute-start.9 = (f32[128,128]{1,0:T(8,128)S(1)}, f32[128,128]{1,0:T(8,128)S(1)}, u32[]{:S(2)}, u32[]{:S(2)}) collective-permute-start(f32[128,128]{1,0:T(8,128)S(1)} %get-tuple-element.34), channel_id=1, source_target_pairs={{0,24},{8,0},{16,8},{24,16},{1,25},{9,1},{17,9},{25,17},{2,26},{10... | collective-permute-start | bytes 196616 | tf_op jit(solution)/shard_map/ppermute | solution.py:312
  77.7 2.5 %starts.1 = (f32[4,128,128]{2,1,0:T(8,128)}, f32[4,128,128]{2,1,0:T(8,128)}) custom-call(s32[1]{0:T(128)} %bitcast.c_ref, f32[4,128,128]{2,1,0:T(8,128)} %copy-done.3, f32[8,128,256]{2,1,0:T(8,128)} %get-tuple-element.17.own_ref, f32[4,128,256]{2,1,0:T(8,128)} %copy-done), custom_call_target="tpu_custom_call" | custom-call | tf_op jit(solution)/shard_map/starts/pallas_call | solution.py:228
  80.2 5.0 %local_reads.1 = (bf16[8,256,128]{2,1,0:T(8,128)(2,1)}, bf16[8,256,128]{2,1,0:T(8,128)(2,1)}, f32[8,256,128]{2,1,0:T(8,128)}) custom-call(bf16[256,1024]{1,0:T(8,128)(2,1)} %q_ref.1, bf16[256,1024]{1,0:T(8,128)(2,1)} %k_ref.3, bf16[8,256,256]{2,1,0:T(8,128)(2,1)} %get-tuple-element.11.xh_ref, bf16[8,256,256]{2,1,0:T(8,128)(2,1)} %get-tuple-element.12.xl_ref, ...), custom_call_target="tpu_custom_call" | custom-call | tf_op jit(solution)/shard_map/local_reads/pallas_call | solution.py:201
  85.8 4.3 %outputs.1 = bf16[256,1024]{1,0:T(8,128)(2,1)} custom-call(s32[1]{0:T(128)} %bitcast.c_ref, bf16[8,256,128]{2,1,0:T(8,128)(2,1)} %get-tuple-element.14.qh_ref, bf16[8,256,128]{2,1,0:T(8,128)(2,1)} %get-tuple-element.15.ql_ref, f32[8,256,128]{2,1,0:T(8,128)} %get-tuple-element.16.y_ref, f32[4,128,128]{2,1,0:T(8,128)} %get-tuple-element.18.mine_ref, ...), custom_call_target="tpu_custom_call" | custom-call | tf_op jit(solution)/shard_map/outputs/pallas_call | solution.py:298
  90.2 3.2 %collective-permute-start.17 = (bf16[256,1024]{1,0:T(8,128)(2,1)}, bf16[256,1024]{1,0:T(8,128)(2,1)}, u32[]{:S(2)}, u32[]{:S(2)}) collective-permute-start(bf16[256,1024]{1,0:T(8,128)(2,1)} %outputs.1), channel_id=1, source_target_pairs={{0,96},{32,0},{64,32},{96,64},{1,97},{33,1},{65,33},{97,65},{2,98}... | collective-permute-start | bytes 1572872 | tf_op jit(solution)/shard_map/ppermute | solution.py:312
  98.2 2.0 %copy.15 = bf16[1,2,256,512]{3,2,0,1:T(8,128)(2,1)} copy(bf16[1,2,256,512]{2,3,1,0:T(8,128)(2,1)} %bitcast.23) | data formatting | bytes 1048576 | tf_op jit(solution)/shard_map/jit(dynamic_update_index_in_dim)/broadcast_in_dim | solution.py:325
  101.4 4.2 %collective-permute-done.17 = bf16[256,1024]{1,0:T(8,128)(2,1)} collective-permute-done((bf16[256,1024]{1,0:T(8,128)(2,1)}, bf16[256,1024]{1,0:T(8,128)(2,1)}, u32[]{:S(2)}, u32[]{:S(2)}) %collective-permute-start.17) | collective-permute-done | bytes 524320 | tf_op jit(solution)/shard_map/ppermute | solution.py:312
  106.5 3.9 %collective-permute-start.18 = (bf16[256,512]{1,0:T(8,128)(2,1)S(1)}, bf16[256,512]{1,0:T(8,128)(2,1)S(1)}, u32[]{:S(2)}, u32[]{:S(2)}) collective-permute-start(bf16[256,512]{1,0:T(8,128)(2,1)S(1)} %slice.49), channel_id=1, source_target_pairs={{0,96},{32,0},{64,32},{96,64},{1,97},{33,1},{65,33},{97,65},{2,98}... | collective-permute-start | bytes 786440 | tf_op jit(solution)/shard_map/ppermute | solution.py:312
  111.7 4.1 %collective-permute-done.18 = bf16[256,512]{1,0:T(8,128)(2,1)S(1)} collective-permute-done((bf16[256,512]{1,0:T(8,128)(2,1)S(1)}, bf16[256,512]{1,0:T(8,128)(2,1)S(1)}, u32[]{:S(2)}, u32[]{:S(2)}) %collective-permute-start.18) | collective-permute-done | bytes 262176 | tf_op jit(solution)/shard_map/ppermute | solution.py:312
  115.8 4.5 %collective-permute-done.16 = bf16[256,512]{1,0:T(8,128)(2,1)S(1)} collective-permute-done((bf16[256,512]{1,0:T(8,128)(2,1)S(1)}, bf16[256,512]{1,0:T(8,128)(2,1)S(1)}, u32[]{:S(2)}, u32[]{:S(2)}) %collective-permute-start.16) | collective-permute-done | bytes 262176 | tf_op jit(solution)/shard_map/ppermute | solution.py:312
  120.3 3.6 %convolution_convert_fusion = bf16[512,1024]{1,0:T(8,128)(2,1)} fusion(bf16[1024,512]{1,0:T(8,128)(2,1)S(1)} %bitcast.59, bf16[256,1024]{1,0:T(8,128)(2,1)} %collective-permute-done.17, bf16[256,512]{1,0:T(8,128)(2,1)S(1)} %collective-permute-done.18, bf16[256,512]{1,0:T(8,128)(2,1)S(1)} %collective-permute-done.16, ...), kind=kOutput, calls=%fused_computation.2 | convolution fusion | flops 1084751872 | bytes 4194304 | tf_op jit(solution)/shard_map/dot_general | solution.py:30
  123.9 2.9 %collective-permute-done.19 = bf16[512,1024]{1,0:T(8,128)(2,1)S(1)} collective-permute-done((bf16[512,1024]{1,0:T(8,128)(2,1)}, bf16[512,1024]{1,0:T(8,128)(2,1)S(1)}, u32[]{:S(2)}, u32[]{:S(2)}) %collective-permute-start.19) | collective-permute-done | bytes 1048608 | tf_op jit(solution)/shard_map/ppermute | solution.py:317
  126.8 2.5 %convert_add_fusion = f32[512,1024]{1,0:T(8,128)S(1)} fusion(bf16[512,1024]{1,0:T(8,128)(2,1)S(1)} %collective-permute-done.19, bf16[1024,512]{1,0:T(8,128)(2,1)S(1)} %bitcast.58, bf16[256,1024]{1,0:T(8,128)(2,1)} %collective-permute-done.17, bf16[256,512]{1,0:T(8,128)(2,1)S(1)} %collective-permute-done.18, bf16[256,512]{1,0:T(8,128)(2,1)} %copy-done.12, ...), kind=kOutput, calls=%fused_computation.1 | convolution fusion | flops 1085276160 | bytes 6291456 | tf_op jit(solution)/shard_map/dot_general | solution.py:30
  129.6 3.6 %collective-permute-start.22 = (bf16[2,128,512]{2,1,0:T(8,128)(2,1)S(1)}, bf16[2,128,512]{2,1,0:T(8,128)(2,1)S(1)}, u32[]{:S(2)}, u32[]{:S(2)}) collective-permute-start(bf16[2,128,512]{2,1,0:T(8,128)(2,1)S(1)} %pad_maximum_fusion.4), channel_id=1, source_target_pairs={{0,24},{8,16},{16,8},{24,0},{1,25},{9,17},{17,9},{25,1},{2,26},{10... | collective-permute-start | bytes 786440 | tf_op jit(solution)/shard_map/ppermute | solution.py:317
  133.4 6.4 %collective-permute-done.22 = bf16[2,128,512]{2,1,0:T(8,128)(2,1)S(1)} collective-permute-done((bf16[2,128,512]{2,1,0:T(8,128)(2,1)S(1)}, bf16[2,128,512]{2,1,0:T(8,128)(2,1)S(1)}, u32[]{:S(2)}, u32[]{:S(2)}) %collective-permute-start.22) | collective-permute-done | bytes 262176 | tf_op jit(solution)/shard_map/ppermute | solution.py:317
  141.6 1.6 %collective-permute-start.21 = (bf16[128,512]{1,0:T(8,128)(2,1)S(1)}, bf16[128,512]{1,0:T(8,128)(2,1)S(1)}, u32[]{:S(2)}, u32[]{:S(2)}) collective-permute-start(bf16[128,512]{1,0:T(8,128)(2,1)S(1)} %fusion.6), channel_id=1, source_target_pairs={{0,24},{8,16},{16,8},{24,0},{1,25},{9,17},{17,9},{25,1},{2,26},{10... | collective-permute-start | bytes 393224 | tf_op jit(solution)/shard_map/ppermute | solution.py:317
  143.2 1.8 %collective-permute-done.23 = bf16[128,512]{1,0:T(8,128)(2,1)S(1)} collective-permute-done((bf16[128,512]{1,0:T(8,128)(2,1)S(1)}, bf16[128,512]{1,0:T(8,128)(2,1)S(1)}, u32[]{:S(2)}, u32[]{:S(2)}) %collective-permute-start.23) | collective-permute-done | bytes 131104 | tf_op jit(solution)/shard_map/ppermute | solution.py:317
  145.1 2.8 %collective-permute-done.21 = bf16[128,512]{1,0:T(8,128)(2,1)S(1)} collective-permute-done((bf16[128,512]{1,0:T(8,128)(2,1)S(1)}, bf16[128,512]{1,0:T(8,128)(2,1)S(1)}, u32[]{:S(2)}, u32[]{:S(2)}) %collective-permute-start.21) | collective-permute-done | bytes 131104 | tf_op jit(solution)/shard_map/ppermute | solution.py:317
  (91 shorter events, 27.9 us)
Async XLA Ops:
  0.6 16.6 %copy-start.4 = (bf16[256,1024]{1,0:T(8,128)(2,1)S(1)}, bf16[256,1024]{1,0:T(8,128)(2,1)}, u32[]{:S(2)}) copy-start(bf16[256,1024]{1,0:T(8,128)(2,1)} %param.11) | copy-start | bytes 1572868
  17.1 2.0 %collective-permute-start = (f32[4,128,256]{2,1,0:T(8,128)S(1)}, f32[4,128,256]{2,1,0:T(8,128)S(1)}, u32[]{:S(2)}, u32[]{:S(2)}) collective-permute-start(f32[4,128,256]{2,1,0:T(8,128)S(1)} %constant_dynamic-slice_fusion.2), channel_id=1, source_target_pairs={{0,4},{4,0},{1,5},{5,1},{2,6},{6,2},{3,7},{7,3},{8,12},{12,8},{9,1... | collective-permute-start | bytes 1572872 | tf_op jit(solution)/shard_map/ppermute | solution.py:317
  19.1 0.8 copy-start
  23.6 8.2 %collective-permute-start.1 = (f32[128,256]{1,0:T(8,128)S(1)}, f32[128,256]{1,0:T(8,128)S(1)}, u32[]{:S(2)}, u32[]{:S(2)}) collective-permute-start(f32[128,256]{1,0:T(8,128)S(1)} %get-tuple-element.32), channel_id=1, source_target_pairs={{0,8},{8,16},{16,24},{24,0},{1,9},{9,17},{17,25},{25,1},{2,10},{10... | collective-permute-start | bytes 393224 | tf_op jit(solution)/shard_map/ppermute | solution.py:312
  25.8 38.8 %collective-permute-start.11 = (bf16[2,256,512]{1,2,0:T(8,128)(2,1)S(1)}, bf16[2,256,512]{1,2,0:T(8,128)(2,1)}, u32[]{:S(2)}, u32[]{:S(2)}) collective-permute-start(bf16[2,256,512]{1,2,0:T(8,128)(2,1)S(1)} %pad_maximum_fusion.1), channel_id=1, source_target_pairs={{0,0},{1,32},{2,64},{3,96},{32,1},{33,33},{34,65},{35,97},{64,2},{... | collective-permute-start | bytes 1572872 | tf_op jit(solution)/shard_map/ppermute | solution.py:336
  27.2 8.3 %collective-permute-start.2 = (f32[128,256]{1,0:T(8,128)S(1)}, f32[128,256]{1,0:T(8,128)S(1)}, u32[]{:S(2)}, u32[]{:S(2)}) collective-permute-start(f32[128,256]{1,0:T(8,128)S(1)} %get-tuple-element.31), channel_id=1, source_target_pairs={{0,16},{8,24},{16,0},{24,8},{1,17},{9,25},{17,1},{25,9},{2,18},{10... | collective-permute-start | bytes 393224 | tf_op jit(solution)/shard_map/ppermute | solution.py:312
  30.8 5.7 %collective-permute-start.3 = (f32[128,256]{1,0:T(8,128)S(1)}, f32[128,256]{1,0:T(8,128)S(1)}, u32[]{:S(2)}, u32[]{:S(2)}) collective-permute-start(f32[128,256]{1,0:T(8,128)S(1)} %get-tuple-element.30), channel_id=1, source_target_pairs={{0,24},{8,0},{16,8},{24,16},{1,25},{9,1},{17,9},{25,17},{2,26},{10... | collective-permute-start | bytes 393224 | tf_op jit(solution)/shard_map/ppermute | solution.py:312
  36.6 0.8 copy-start.2
  40.7 17.5 %collective-permute-start.4 = (f32[128,256]{1,0:T(8,128)S(1)}, f32[128,256]{1,0:T(8,128)S(1)}, u32[]{:S(2)}, u32[]{:S(2)}) collective-permute-start(f32[128,256]{1,0:T(8,128)S(1)} %slice_bitcast_fusion), channel_id=1, source_target_pairs={{0,96},{32,0},{64,32},{96,64},{1,97},{33,1},{65,33},{97,65},{2,98}... | collective-permute-start | bytes 393224 | tf_op jit(solution)/shard_map/ppermute | solution.py:312
  46.5 11.7 %collective-permute-start.5 = (f32[128,256]{1,0:T(8,128)S(1)}, f32[128,256]{1,0:T(8,128)S(1)}, u32[]{:S(2)}, u32[]{:S(2)}) collective-permute-start(f32[128,256]{1,0:T(8,128)S(1)} %slice_bitcast_fusion), channel_id=1, source_target_pairs={{0,64},{32,96},{64,0},{96,32},{1,65},{33,97},{65,1},{97,33},{2,66}... | collective-permute-start | bytes 393224 | tf_op jit(solution)/shard_map/ppermute | solution.py:312
  47.2 11.1 %collective-permute-start.6 = (f32[128,256]{1,0:T(8,128)S(1)}, f32[128,256]{1,0:T(8,128)S(1)}, u32[]{:S(2)}, u32[]{:S(2)}) collective-permute-start(f32[128,256]{1,0:T(8,128)S(1)} %slice_bitcast_fusion), channel_id=1, source_target_pairs={{0,32},{32,64},{64,96},{96,0},{1,33},{33,65},{65,97},{97,1},{2,34}... | collective-permute-start | bytes 393224 | tf_op jit(solution)/shard_map/ppermute | solution.py:312
  62.4 10.3 %collective-permute-start.7 = (f32[128,128]{1,0:T(8,128)S(1)}, f32[128,128]{1,0:T(8,128)S(1)}, u32[]{:S(2)}, u32[]{:S(2)}) collective-permute-start(f32[128,128]{1,0:T(8,128)S(1)} %get-tuple-element.36), channel_id=1, source_target_pairs={{0,8},{8,16},{16,24},{24,0},{1,9},{9,17},{17,25},{25,1},{2,10},{10... | collective-permute-start | bytes 196616 | tf_op jit(solution)/shard_map/ppermute | solution.py:312
  64.6 30.3 %collective-permute-start.12 = (bf16[2,256,512]{1,2,0:T(8,128)(2,1)}, bf16[2,256,512]{1,2,0:T(8,128)(2,1)}, u32[]{:S(2)}, u32[]{:S(2)}) collective-permute-start(bf16[2,256,512]{1,2,0:T(8,128)(2,1)} %collective-permute-done.11), channel_id=1, source_target_pairs={{0,1},{1,2},{2,3},{3,0},{4,5},{5,6},{6,7},{7,4},{8,9},{9,10},{10,1... | collective-permute-start | bytes 1572872 | tf_op jit(solution)/shard_map/ppermute | solution.py:312
  64.6 31.6 %collective-permute-start.13 = (bf16[2,256,512]{1,2,0:T(8,128)(2,1)}, bf16[2,256,512]{1,2,0:T(8,128)(2,1)S(1)}, u32[]{:S(2)}, u32[]{:S(2)}) collective-permute-start(bf16[2,256,512]{1,2,0:T(8,128)(2,1)} %collective-permute-done.11), channel_id=1, source_target_pairs={{0,2},{1,3},{2,0},{3,1},{4,6},{5,7},{6,4},{7,5},{8,10},{9,11},{10,... | collective-permute-start | bytes 1572872 | tf_op jit(solution)/shard_map/ppermute | solution.py:312
  69.6 28.7 %collective-permute-start.14 = (bf16[2,256,512]{1,2,0:T(8,128)(2,1)}, bf16[2,256,512]{1,2,0:T(8,128)(2,1)}, u32[]{:S(2)}, u32[]{:S(2)}) collective-permute-start(bf16[2,256,512]{1,2,0:T(8,128)(2,1)} %collective-permute-done.11), channel_id=1, source_target_pairs={{0,3},{1,0},{2,1},{3,2},{4,7},{5,4},{6,5},{7,6},{8,11},{9,8},{10,9... | collective-permute-start | bytes 1572872 | tf_op jit(solution)/shard_map/ppermute | solution.py:312
  70.7 5.8 %collective-permute-start.8 = (f32[128,128]{1,0:T(8,128)S(1)}, f32[128,128]{1,0:T(8,128)S(1)}, u32[]{:S(2)}, u32[]{:S(2)}) collective-permute-start(f32[128,128]{1,0:T(8,128)S(1)} %get-tuple-element.35), channel_id=1, source_target_pairs={{0,16},{8,24},{16,0},{24,8},{1,17},{9,25},{17,1},{25,9},{2,18},{10... | collective-permute-start | bytes 196616 | tf_op jit(solution)/shard_map/ppermute | solution.py:312
  72.7 4.3 %collective-permute-start.9 = (f32[128,128]{1,0:T(8,128)S(1)}, f32[128,128]{1,0:T(8,128)S(1)}, u32[]{:S(2)}, u32[]{:S(2)}) collective-permute-start(f32[128,128]{1,0:T(8,128)S(1)} %get-tuple-element.34), channel_id=1, source_target_pairs={{0,24},{8,0},{16,8},{24,16},{1,25},{9,1},{17,9},{25,17},{2,26},{10... | collective-permute-start | bytes 196616 | tf_op jit(solution)/shard_map/ppermute | solution.py:312
  80.2 5.0 %collective-permute-start.10 = (f32[4,128,128]{2,1,0:T(8,128)}, f32[4,128,128]{2,1,0:T(8,128)S(1)}, u32[]{:S(2)}, u32[]{:S(2)}) collective-permute-start(f32[4,128,128]{2,1,0:T(8,128)} %get-tuple-element.19), channel_id=1, source_target_pairs={{0,4},{4,0},{1,5},{5,1},{2,6},{6,2},{3,7},{7,3},{8,12},{12,8},{9,1... | collective-permute-start | bytes 786440 | tf_op jit(solution)/shard_map/ppermute | solution.py:317
  90.2 15.4 %collective-permute-start.17 = (bf16[256,1024]{1,0:T(8,128)(2,1)}, bf16[256,1024]{1,0:T(8,128)(2,1)}, u32[]{:S(2)}, u32[]{:S(2)}) collective-permute-start(bf16[256,1024]{1,0:T(8,128)(2,1)} %outputs.1), channel_id=1, source_target_pairs={{0,96},{32,0},{64,32},{96,64},{1,97},{33,1},{65,33},{97,65},{2,98}... | collective-permute-start | bytes 1572872 | tf_op jit(solution)/shard_map/ppermute | solution.py:312
  93.4 17.1 %collective-permute-start.15 = (bf16[256,1024]{1,0:T(8,128)(2,1)}, bf16[256,1024]{1,0:T(8,128)(2,1)}, u32[]{:S(2)}, u32[]{:S(2)}) collective-permute-start(bf16[256,1024]{1,0:T(8,128)(2,1)} %outputs.1), channel_id=1, source_target_pairs={{0,32},{32,64},{64,96},{96,0},{1,33},{33,65},{65,97},{97,1},{2,34}... | collective-permute-start | bytes 1572872 | tf_op jit(solution)/shard_map/ppermute | solution.py:312
  96.2 0.8 copy-start.5
  100.3 1.0 copy-start.1
  106.5 9.3 %collective-permute-start.18 = (bf16[256,512]{1,0:T(8,128)(2,1)S(1)}, bf16[256,512]{1,0:T(8,128)(2,1)S(1)}, u32[]{:S(2)}, u32[]{:S(2)}) collective-permute-start(bf16[256,512]{1,0:T(8,128)(2,1)S(1)} %slice.49), channel_id=1, source_target_pairs={{0,96},{32,0},{64,32},{96,64},{1,97},{33,1},{65,33},{97,65},{2,98}... | collective-permute-start | bytes 786440 | tf_op jit(solution)/shard_map/ppermute | solution.py:312
  111.4 8.9 %copy-start.6 = (bf16[256,1024]{1,0:T(8,128)(2,1)S(1)}, bf16[256,1024]{1,0:T(8,128)(2,1)}, u32[]{:S(2)}) copy-start(bf16[256,1024]{1,0:T(8,128)(2,1)} %outputs.1) | copy-start | bytes 1572868
  111.5 8.8 %collective-permute-start.16 = (bf16[256,512]{1,0:T(8,128)(2,1)S(1)}, bf16[256,512]{1,0:T(8,128)(2,1)S(1)}, u32[]{:S(2)}, u32[]{:S(2)}) collective-permute-start(bf16[256,512]{1,0:T(8,128)(2,1)S(1)} %slice.48), channel_id=1, source_target_pairs={{0,32},{32,64},{64,96},{96,0},{1,33},{33,65},{65,97},{97,1},{2,34}... | collective-permute-start | bytes 786440 | tf_op jit(solution)/shard_map/ppermute | solution.py:312
  120.3 3.6 %copy-start.12 = (bf16[256,512]{1,0:T(8,128)(2,1)}, bf16[256,512]{1,0:T(8,128)(2,1)S(1)}, u32[]{:S(2)}) copy-start(bf16[256,512]{1,0:T(8,128)(2,1)S(1)} %collective-permute-done.16) | copy-start | bytes 786436
  120.3 6.5 %copy-start.7 = (bf16[256,1024]{1,0:T(8,128)(2,1)S(1)}, bf16[256,1024]{1,0:T(8,128)(2,1)}, u32[]{:S(2)}) copy-start(bf16[256,1024]{1,0:T(8,128)(2,1)} %outputs.1) | copy-start | bytes 1572868
  123.9 2.9 %collective-permute-start.19 = (bf16[512,1024]{1,0:T(8,128)(2,1)}, bf16[512,1024]{1,0:T(8,128)(2,1)S(1)}, u32[]{:S(2)}, u32[]{:S(2)}) collective-permute-start(bf16[512,1024]{1,0:T(8,128)(2,1)} %convolution_convert_fusion), channel_id=1, source_target_pairs={{0,4},{4,0},{1,5},{5,1},{2,6},{6,2},{3,7},{7,3},{8,12},{12,8},{9,1... | collective-permute-start | bytes 3145736 | tf_op jit(solution)/shard_map/ppermute | solution.py:317
  129.6 10.2 %collective-permute-start.22 = (bf16[2,128,512]{2,1,0:T(8,128)(2,1)S(1)}, bf16[2,128,512]{2,1,0:T(8,128)(2,1)S(1)}, u32[]{:S(2)}, u32[]{:S(2)}) collective-permute-start(bf16[2,128,512]{2,1,0:T(8,128)(2,1)S(1)} %pad_maximum_fusion.4), channel_id=1, source_target_pairs={{0,24},{8,16},{16,8},{24,0},{1,25},{9,17},{17,9},{25,1},{2,26},{10... | collective-permute-start | bytes 786440 | tf_op jit(solution)/shard_map/ppermute | solution.py:317
  133.3 8.1 %collective-permute-start.20 = (bf16[2,128,512]{2,1,0:T(8,128)(2,1)S(1)}, bf16[2,128,512]{2,1,0:T(8,128)(2,1)S(1)}, u32[]{:S(2)}, u32[]{:S(2)}) collective-permute-start(bf16[2,128,512]{2,1,0:T(8,128)(2,1)S(1)} %pad_maximum_fusion.3), channel_id=1, source_target_pairs={{0,8},{8,0},{16,24},{24,16},{1,9},{9,1},{17,25},{25,17},{2,10},{10... | collective-permute-start | bytes 786440 | tf_op jit(solution)/shard_map/ppermute | solution.py:317
  140.0 5.0 %collective-permute-start.23 = (bf16[128,512]{1,0:T(8,128)(2,1)S(1)}, bf16[128,512]{1,0:T(8,128)(2,1)S(1)}, u32[]{:S(2)}, u32[]{:S(2)}) collective-permute-start(bf16[128,512]{1,0:T(8,128)(2,1)S(1)} %fusion.7), channel_id=1, source_target_pairs={{0,8},{8,0},{16,24},{24,16},{1,9},{9,1},{17,25},{25,17},{2,10},{10... | collective-permute-start | bytes 393224 | tf_op jit(solution)/shard_map/ppermute | solution.py:317
  141.6 6.3 %collective-permute-start.21 = (bf16[128,512]{1,0:T(8,128)(2,1)S(1)}, bf16[128,512]{1,0:T(8,128)(2,1)S(1)}, u32[]{:S(2)}, u32[]{:S(2)}) collective-permute-start(bf16[128,512]{1,0:T(8,128)(2,1)S(1)} %fusion.6), channel_id=1, source_target_pairs={{0,24},{8,16},{16,8},{24,0},{1,25},{9,17},{17,9},{25,1},{2,26},{10... | collective-permute-start | bytes 393224 | tf_op jit(solution)/shard_map/ppermute | solution.py:317
  (5 other events, 3.5 us)
where the time goes:
time: 150 us; the launch traced here: 149 us
  waiting for transfers between devices  46 us (31%)
  starting transfers between devices  41.3 us (28%)
  Pallas kernels  33 us (22%)
  local copies, waits for them, and re-layouts  20 us (13%)
  matrix products  6.14 us (4%)
    ppermute x16, starting transfers between devices, shift(): return lax.ppermute(x, axis, [(i, (i + k) % 4) for i in range(4)])  34.3 us
    ppermute x16, waiting for transfers between devices, shift(): return lax.ppermute(x, axis, [(i, (i + k) % 4) for i in range(4)])  29.1 us
    ppermute x7, waiting for transfers between devices, swap(): return lax.ppermute(x, axis, [(i, i ^ k) for i in range(n)])  16.9 us
    pallas_call x1, Pallas kernels, local_maps(): pl.pallas_call(local_kernel, grid=(steps,), in_specs=[pl.BlockSpec((TOK,...  13.9 us
    pallas_call x4, Pallas kernels, scalar_call(): pl.pallas_call(kernel, grid_spec=pltpu.PrefetchScalarGridSpec(num_scalar_...  9.88 us
    unnamed x28, local copies, waits for them, and re-layouts  7.16 us
    dot_general x2, matrix products, dot_tn(): lax.dot_general(a, b, (((0,), (0,)), ((), ())), preferred_element_type=f32)  6.14 us
    broadcast_in_dim x4, local copies, waits for them, and re-layouts, put(): return lax.dynamic_update_index_in_dim(x, b, i, 0)  5.8 us
  transfers between devices with their start and end apart: 24, of which 15 were waited for; matrix products, arithmetic and copies ran while one was open for 7% of the time, Pallas kernels for 11%

commit v1 on v0

v1 whole, which is shorter than its diff:
```python
import functools

import jax
import jax.numpy as jnp
from jax import lax
from jax.experimental import pallas as pl
from jax.experimental.pallas import tpu as pltpu
from jax.sharding import Mesh, PartitionSpec as P


F = 128
TOK = 256
HEADS = 8
EPS = 1e-06
f32 = jnp.float32
bf16 = jnp.bfloat16


def split(x):
    h = x.astype(bf16)
    return h, (x - h.astype(f32)).astype(bf16)


def dot(a, b):
    return jnp.dot(a, b, preferred_element_type=f32)


def dot_nt(a, b):
    return lax.dot_general(a, b, (((1,), (1,)), ((), ())), preferred_element_type=f32)


def dot_tn(a, b):
    return lax.dot_general(a, b, (((0,), (0,)), ((), ())), preferred_element_type=f32)


def lhs_of(s):
    return jnp.concatenate(s, axis=1)


def rhs_of(s):
    y = jnp.concatenate(s, axis=1)
    return jnp.concatenate([y, y], axis=0)


def mm(a, b):
    o = dot(lhs_of(a), rhs_of(b))
    return o[:, :F] + o[:, F:]


def mm_all(pairs):
    return [mm(a, b) for a, b in pairs]


def map_product(p, r):
    ph, pl_ = split(p)
    rh, rl = split(r)
    return dot(jnp.concatenate([ph, pl_], axis=1), jnp.concatenate([rh, rh], axis=0)) + dot(ph, rl)


HB = 2


def half_of(mine, w):
    return w[2] if mine else 1 - w[2]


def local_kernel(mine, w_ref, k_ref, v_ref, b_ref, map_ref, xh_ref, xl_ref, r_ref):
    g = pl.program_id(0)
    first_head = half_of(mine, w_ref) * 4 + g * HB
    beta_rows = b_ref[...]
    beta_cols = jnp.transpose(jnp.concatenate([beta_rows, jnp.zeros((F - HEADS, TOK), f32)], axis=0))
    lane = lax.broadcasted_iota(jnp.int32, (TOK, F), 1)
    row = lax.broadcasted_iota(jnp.int32, (F, F), 0)
    col = lax.broadcasted_iota(jnp.int32, (F, F), 1)
    eye = (row == col).astype(f32)
    strict = row > col
    in16 = jnp.logical_and(strict, (row // 16) == (col // 16))
    in64 = jnp.logical_and((row // 64) == (col // 64), (row // 16) > (col // 16))
    in128 = (row // 64) > (col // 64)

    stat = jnp.zeros((TOK, F), f32)
    ks, rs, bs, kraw = [], [], [], []
    for i in range(HB):
        k = k_ref[:, i * F:(i + 1) * F]
        kf = k.astype(f32)
        r = lax.rsqrt(jnp.sum(kf * kf, axis=-1, keepdims=True) + EPS)
        kf = jnp.where(r > 0.0, kf, 0.0)
        b = jnp.sum(jnp.where(lane == first_head + i, beta_cols, 0.0), axis=-1, keepdims=True)
        ks.append(kf)
        kraw.append(kf.astype(bf16))
        rs.append(r)
        bs.append(b)
        stat = jnp.where(lane == 2 * i, r, stat)
        stat = jnp.where(lane == 2 * i + 1, b, stat)
    stat_t = jnp.transpose(stat)
    r_ref[g] = stat_t[0:8, :]

    tiles = []
    cross = []
    for i in range(HB):
        r_row = stat_t[2 * i:2 * i + 1, :]
        br = bs[i] * rs[i]
        k1, k2 = kraw[i][:F], kraw[i][F:]
        g11 = dot_nt(k1, k1)
        g2 = dot_nt(k2, kraw[i])
        a11 = g11 * br[:F] * r_row[:, :F]
        a2 = g2 * br[F:] * r_row
        tiles += [a11, a2[:, F:]]
        cross.append(a2[:, :F])
    n = [jnp.where(in16, a, 0.0) for a in tiles]
    ns = [split(a) for a in n]
    n2 = mm_all(zip(ns, ns))
    n2s = [split(a) for a in n2]
    n4 = mm_all(zip(n2s, n2s))
    q1 = mm_all(zip(ns, n2s))
    n4s = [split(a) for a in n4]
    r1 = [eye - a + b - c for a, b, c in zip(n, n2, q1)]
    n8 = mm_all(zip(n4s, n4s))
    q2 = mm_all(zip([split(a) for a in r1], n4s))
    r2 = [a + b for a, b in zip(r1, q2)]
    q3 = mm_all(zip([split(a) for a in r2], [split(a) for a in n8]))
    d = [a + b for a, b in zip(r2, q3)]
    ds = [split(a) for a in d]
    m = mm_all(zip(ds, [split(jnp.where(in64, a, 0.0)) for a in tiles]))
    ms = [split(a) for a in m]
    m2 = mm_all(zip(ms, ms))
    e = [a + b for a, b in zip(d, mm_all(zip([split(a) for a in m2], ds)))]
    t = [a - b for a, b in zip(e, mm_all(zip(ms, [split(a) for a in e])))]
    ts = [split(a) for a in t]
    u = mm_all(zip([split(jnp.where(in128, a, 0.0)) for a in tiles], ts))
    t = [a - b for a, b in zip(t, mm_all(zip(ts, [split(a) for a in u])))]
    ts = [split(a) for a in t]
    c1 = mm_all(zip([split(a) for a in cross], ts[0::2]))
    t21 = [-a for a in mm_all(zip(ts[1::2], [split(a) for a in c1]))]

    for i in range(HB):
        b_row = stat_t[2 * i + 1:2 * i + 2, :]
        t11h, t11l = split(t[2 * i] * b_row[:, :F])
        t2h, t2l = split(jnp.concatenate([t21[i], t[2 * i + 1]], axis=1) * b_row)
        kn = ks[i] * rs[i]
        knh, knl = split(kn)
        v = v_ref[:, i * F:(i + 1) * F]
        bh = jnp.concatenate([knh, v], axis=1)
        bh1 = bh[:F]
        x1 = dot(jnp.concatenate([t11h, t11l], axis=1), jnp.concatenate([bh1, bh1], axis=0))
        x2 = dot(t2h, bh) + dot(t2l, bh)
        y1 = dot(t11h, knl[:F])
        y2 = dot(t2h, knl)
        x = jnp.concatenate([x1, x2], axis=0)
        y = jnp.concatenate([y1, y2], axis=0)
        x = jnp.concatenate([x[:, :F] + y, x[:, F:]], axis=1)
        xh, xl = split(x)
        xh_ref[g * HB + i] = xh
        xl_ref[g * HB + i] = xl
        zh, zl = split(x * rs[i])
        pw = dot_tn(kraw[i], zh) + dot_tn(kraw[i], zl)
        map_ref[g * HB + i] = jnp.concatenate([eye - pw[:, :F], pw[:, F:]], axis=1)


def vmem(shape, dtype=f32):
    return pltpu.VMEM(shape, dtype)


PARAMS = pltpu.CompilerParams(vmem_limit_bytes=24 << 20)


def in_vmem(x):
    return pltpu.with_memory_space_constraint(x, pltpu.VMEM)


ANYV = pl.BlockSpec(memory_space=pltpu.VMEM)


def local_maps(mine, where, k, v, beta_rows):
    steps = 4 // HB
    cols = pl.BlockSpec((TOK, HB * F), lambda g, w: (0, half_of(mine, w) * steps + g))
    return pl.pallas_call(
        functools.partial(local_kernel, mine),
        grid_spec=pltpu.PrefetchScalarGridSpec(
            num_scalar_prefetch=1,
            grid=(steps,),
            in_specs=[cols, cols, pl.BlockSpec((HEADS, TOK), lambda g, w: (0, 0))],
            out_specs=[ANYV] * 4,
        ),
        out_shape=[
            vmem((4, F, 2 * F)),
            vmem((4, TOK, 2 * F), bf16),
            vmem((4, TOK, 2 * F), bf16),
            vmem((steps, 8, TOK)),
        ],
        compiler_params=PARAMS,
        name="local_maps",
    )(where, k, v, beta_rows)


def reads_kernel(w_ref, q_ref, k_ref, xh_ref, xl_ref, r_ref, m_ref, qh_ref, ql_ref, y_ref):
    g = pl.program_id(0)
    row = lax.broadcasted_iota(jnp.int32, (TOK, TOK), 0)
    col = lax.broadcasted_iota(jnp.int32, (TOK, TOK), 1)
    causal = row >= col
    for i in range(HB):
        q = q_ref[:, i * F:(i + 1) * F]
        k = k_ref[:, i * F:(i + 1) * F]
        r_row = r_ref[g, 2 * i:2 * i + 1, :]
        s = dot_nt(q, k) * r_row
        s = jnp.where(jnp.logical_and(causal, r_row > 0.0), s, 0.0)
        sh, sl = split(s)
        n = g * HB + i
        xh, xl = xh_ref[n], xl_ref[n]
        o = dot(sh, xh) + (dot(sl, xh) + dot(sh, xl))
        qe = q.astype(f32) - o[:, :F]
        qh, ql = split(qe)
        qh_ref[n] = qh
        ql_ref[n] = ql
        y_ref[n] = o[:, F:]

        @pl.when(w_ref[2] == 1)
        def _():
            z = map_product(qe, m_ref[n])
            zh, zl = split(z[:, :F])
            qh_ref[n] = zh
            ql_ref[n] = zl
            y_ref[n] = o[:, F:] + z[:, F:]


def local_reads(mine, where, q, k, xh, xl, r, first):
    steps = 4 // HB
    cols = pl.BlockSpec((TOK, HB * F), lambda g, w: (0, half_of(mine, w) * steps + g))
    return pl.pallas_call(
        reads_kernel,
        grid_spec=pltpu.PrefetchScalarGridSpec(
            num_scalar_prefetch=1,
            grid=(steps,),
            in_specs=[cols, cols] + [ANYV] * 4,
            out_specs=[ANYV] * 3,
        ),
        out_shape=[vmem((4, TOK, F), bf16), vmem((4, TOK, F), bf16), vmem((4, TOK, F))],
        compiler_params=PARAMS,
        name="local_reads",
    )(where, q, k, *[in_vmem(a) for a in (xh, xl, r, first)])


def after(p_then, m):
    o = map_product(p_then[:, :F], m)
    return jnp.concatenate([o[:, :F], o[:, F:] + p_then[:, F:]], axis=1)


def stage(kernel, where, outs, *args, scratch=()):
    return pl.pallas_call(
        kernel,
        in_specs=[pl.BlockSpec(memory_space=pltpu.SMEM)] + [ANYV] * len(args),
        out_specs=[ANYV] * len(outs),
        out_shape=list(outs),
        scratch_shapes=list(scratch),
        compiler_params=PARAMS,
    )(where, *[in_vmem(a) for a in args])


def pair_kernel(w_ref, own_ref, got_ref, *out_refs):
    z, c = w_ref[1], w_ref[2]
    for k in range(4):
        j = lax.rem(z + k, 4)
        own = own_ref[j]
        got = got_ref[j]
        out_refs[k][...] = after(jnp.where(c == 0, got, own), jnp.where(c == 0, own, got))


def chain_kernel(w_ref, m0_ref, m1_ref, m2_ref, m3_ref, pre_ref, all_ref, maps_ref):
    z = w_ref[1]
    for k, ref in enumerate((m0_ref, m1_ref, m2_ref, m3_ref)):
        maps_ref[lax.rem(z - k + 4, 4)] = ref[...]
    m = maps_ref[0]
    pre_ref[0] = m
    for j in range(1, 4):
        m = after(maps_ref[j], m)
        if j < 3:
            pre_ref[j] = m
    all_ref[...] = m


def apply_map(m, s):
    return mm(split(m[:, :F]), split(s)) + m[:, F:]


def plane_kernel(w_ref, m3_ref, m2_ref, m1_ref, pre_ref, *out_refs):
    y, z = w_ref[0], w_ref[1]
    s = jnp.where(y >= 3, m3_ref[:, F:], 0.0)
    s = jnp.where(y >= 2, apply_map(m2_ref[...], s), 0.0)
    s = jnp.where(y >= 1, apply_map(m1_ref[...], s), 0.0)
    for k in range(4):
        j = lax.rem(z + k, 4)
        t = apply_map(pre_ref[jnp.maximum(j - 1, 0)], s)
        out_refs[k][...] = jnp.where(j == 0, s, t)


def order_kernel(w_ref, s0_ref, s1_ref, s2_ref, s3_ref, out_ref):
    z = w_ref[1]
    for k, ref in enumerate((s0_ref, s1_ref, s2_ref, s3_ref)):
        out_ref[lax.rem(z - k + 4, 4)] = ref[...]


def out_kernel(w_ref, qh_ref, ql_ref, y_ref, s_ref, g_ref, o_ref):
    mixed = [mm((qh_ref[i], ql_ref[i]), split(s_ref[i])) + y_ref[i] for i in range(4)]
    for i, m in enumerate(mixed):
        ms = jnp.mean(m * m, axis=-1, keepdims=True)
        o_ref[:, i * F:(i + 1) * F] = (m * lax.rsqrt(ms + EPS) * g_ref[...]).astype(bf16)


def outputs(where, qh, ql, y, s, gain):
    return stage(out_kernel, where, [vmem((TOK, 4 * F), bf16)], qh, ql, y, s, gain)[0]


def shift(x, axis, k):
    return lax.ppermute(x, axis, [(i, (i + k) % 4) for i in range(4)])


def swap(x, axis, k):
    n = 2 if axis == "core" else 4
    return lax.ppermute(x, axis, [(i, i ^ k) for i in range(n)])


def pick(x, i):
    return lax.dynamic_index_in_dim(x, i, 0, False)


def body(query_rows, key_rows, value_rows, beta, norm_gain, out_cotangent):
    yi, zi, ci, hi = (lax.axis_index(a).astype(jnp.int32) for a in ("y", "z", "core", "head"))
    where = jnp.stack([yi, zi, ci, hi])

    cot = lax.ppermute(out_cotangent, ("y", "head"), [(a * 4 + b, b * 4 + a) for a in range(4) for b in range(4)])
    cots = [cot]
    for k in (1, 2, 3):
        cots.append(shift(cot, "head", k))
    gain = norm_gain.reshape(1, F)
    beta_rows = beta.T
    m_a, xh_a, xl_a, r_a = local_maps(False, where, key_rows, value_rows, beta_rows)
    got_b = swap(m_a, "core", 1)
    m_b, xh_b, xl_b, r_b = local_maps(True, where, key_rows, value_rows, beta_rows)
    got_a = swap(m_b, "core", 1)
    m4 = vmem((F, 2 * F))
    comb = stage(pair_kernel, where, [m4] * 4, m_b, got_b)
    got = [comb[0]]
    for k in (1, 2, 3):
        got.append(shift(comb[k], "z", k))
    rd_b = local_reads(True, where, query_rows, key_rows, xh_b, xl_b, r_b, got_b)
    rd_a = local_reads(False, where, query_rows, key_rows, xh_a, xl_a, r_a, got_a)
    pre, total = stage(chain_kernel, where, [vmem((3, F, 2 * F)), m4], *got, scratch=[pltpu.VMEM((4, F, 2 * F), f32)])
    planes = []
    for k in (3, 2, 1):
        planes.append(shift(total, "y", k))
    sc = stage(plane_kernel, where, [vmem((F, F))] * 4, *planes, pre)
    sx = [sc[0]]
    for k in (1, 2, 3):
        sx.append(shift(sc[k], "z", k))
    s_b, = stage(order_kernel, where, [vmem((4, F, F))], *sx)
    s_a = swap(s_b, "core", 1)
    att_b = outputs(where, *rd_b, s_b, gain)
    up_b = shift(att_b, "y", 1)
    dn_b = shift(att_b, "y", -1)
    att_a = outputs(where, *rd_a, s_a, gain)
    up_a = shift(att_a, "y", 1)
    dn_a = shift(att_a, "y", -1)
    far_b = shift(up_b, "y", 1)
    far_a = shift(dn_a, "y", -1)

    cots = jnp.stack(cots)
    parts = stage(part_kernel, where, [vmem((4 * F, 8 * F))] * 2, cots, att_b, att_a, up_b, up_a, dn_b, dn_a)
    w_send, = stage(functools.partial(last_kernel, 0), where, [vmem((4 * F, 8 * F), bf16)], cots, far_b, far_a, parts[0])
    w_got = swap(w_send, "core", 1)
    w, = stage(functools.partial(last_kernel, 1), where, [vmem((4 * F, 8 * F))], cots, far_b, far_a, parts[1])
    h = 4 * F
    w_b = (w[:, :h] + w_got[:, h:].astype(f32)).reshape(4, F, h)
    w_a = (w[:, h:] + w_got[:, :h].astype(f32)).reshape(4, F, h)

    def halving(w, first, second):
        z1, z2, z3 = zi ^ first, zi ^ first ^ second, zi ^ second
        s = swap(jnp.concatenate([pick(w, z1), pick(w, z2)]).astype(bf16), "z", first).astype(f32)
        keep, on = pick(w, zi) + s[:F], pick(w, z3) + s[F:]
        return keep + swap(on.astype(bf16), "z", second).astype(f32)

    g_b = halving(w_b, 1, 3)
    g_a = halving(w_a, 3, 1)
    grad = jnp.where(ci == 0, jnp.concatenate([g_b, g_a], axis=1), jnp.concatenate([g_a, g_b], axis=1))
    attended = jnp.where(ci == 0, jnp.concatenate([att_b, att_a], axis=1), jnp.concatenate([att_a, att_b], axis=1))
    return attended, grad


def cot_rows(w_ref, cot_ref, k, part):
    j = lax.rem(w_ref[3] - w_ref[0] + k + 4, 4)
    core = half_of(part == 1, w_ref)
    return jnp.concatenate(
        [cot_ref[j, :, pl.ds(pl.multiple_of((2 * n + core) * F, F), F)] for n in range(4)], axis=1
    )


def part_kernel(w_ref, cot_ref, *refs):
    for s in range(2):
        rows = jnp.concatenate([cot_rows(w_ref, cot_ref, k, s) for k in (0, 1, 3)], axis=0)
        for n in range(2):
            tall = jnp.concatenate([refs[n][...], refs[2 + n][...], refs[4 + n][...]], axis=0)
            refs[6 + s][:, n * 4 * F:(n + 1) * 4 * F] = dot_tn(rows, tall)


def last_kernel(s, w_ref, cot_ref, b_ref, a_ref, part_ref, out_ref):
    rows = cot_rows(w_ref, cot_ref, 2, s)
    for n, ref in enumerate((b_ref, a_ref)):
        cols = slice(n * 4 * F, (n + 1) * 4 * F)
        out_ref[:, cols] = (part_ref[:, cols] + dot_tn(rows, ref[...])).astype(out_ref.dtype)


def solution(mesh):
    fine = Mesh(mesh.devices.reshape(4, 4, 2, 4), ("y", "z", "core", "head"))
    spec = P(("y", "z", "core"), "head")
    return jax.shard_map(
        body,
        mesh=fine,
        in_specs=(spec, spec, spec, spec, P(), spec),
        out_specs=(spec, spec),
        check_vma=False,
    )
```

time: 150 us -> 121 us (0.81)
  local copies, waits for them, and re-layouts: 20 us -> 5.81 us
  waiting for transfers between devices: 46 us -> 33.9 us
  matrix products: 6.14 us -> 0 us
  starting transfers between devices: 41.3 us -> 46.3 us
  Pallas kernels: 33 us -> 29.7 us
  other arithmetic: 1.23 us -> 4.05 us
    ppermute x16 -> x18, waiting for transfers between devices: 29.1 us -> 21.4 us  [shift(): return lax.ppermute(x, axis, [(i, (i + k) % 4) for i in range(4)])]
    ppermute x16 -> x18, starting transfers between devices: 34.3 us -> 42.1 us  [shift(): return lax.ppermute(x, axis, [(i, (i + k) % 4) for i in range(4)])]
    dot_general x2 -> x0, matrix products: 6.14 us -> none  [dot_tn(): lax.dot_general(a, b, (((0,), (0,)), ((), ())), preferred_element_type=f32)]
    broadcast_in_dim x7 -> x0, local copies, waits for them, and re-layouts: 6.03 us -> none  [the longest x4 5.8 us: put(): return lax.dynamic_update_index_in_dim(x, b, i, 0)]
    ppermute x7 -> x8, waiting for transfers between devices: 16.9 us -> 12.6 us  [swap(): return lax.ppermute(x, axis, [(i, i ^ k) for i in range(n)])]
    pallas_call x7 -> x13, Pallas kernels: 33 us -> 29.7 us  [the longest x2 13.8 us: local_maps(): pl.pallas_call(functools.partial(local_kernel, mine), grid_spec=pltpu.Pre...]
    ppermute x7 -> x8, starting transfers between devices: 5.51 us -> 2.43 us  [swap(): return lax.ppermute(x, axis, [(i, i ^ k) for i in range(n)])]
    slice x4 -> x0, local copies, waits for them, and re-layouts: 2.33 us -> none  [the longest x1 0.97 us: on_device(): a_up[:, :h]]
  transfers between devices with their start and end apart: 24 -> 27, of which waited for: 15 -> 13; matrix products, arithmetic and copies ran while one was open for 7% -> 1% of each run, Pallas kernels for 11% -> 17%
where the time goes in v1:
time: 121 us
  starting transfers between devices  46.3 us (38%)
  waiting for transfers between devices  33.9 us (28%)
  Pallas kernels  29.7 us (25%)
  local copies, waits for them, and re-layouts  5.81 us (5%)
  other arithmetic  4.05 us (3%)
    ppermute x18, starting transfers between devices, shift(): return lax.ppermute(x, axis, [(i, (i + k) % 4) for i in range(4)])  42.1 us
    ppermute x18, waiting for transfers between devices, shift(): return lax.ppermute(x, axis, [(i, (i + k) % 4) for i in range(4)])  21.4 us
    pallas_call x2, Pallas kernels, local_maps(): pl.pallas_call(functools.partial(local_kernel, mine), grid_spec=pltpu.Pre...  13.8 us
    ppermute x8, waiting for transfers between devices, swap(): return lax.ppermute(x, axis, [(i, i ^ k) for i in range(n)])  12.6 us
    pallas_call x9, Pallas kernels, stage(): pl.pallas_call(kernel, in_specs=[pl.BlockSpec(memory_space=pltpu.SMEM)] +...  11 us
    unnamed x16, local copies, waits for them, and re-layouts  5.73 us
    pallas_call x2, Pallas kernels, local_reads(): pl.pallas_call(reads_kernel, grid_spec=pltpu.PrefetchScalarGridSpec(num_s...  4.89 us
    ppermute x8, starting transfers between devices, swap(): return lax.ppermute(x, axis, [(i, i ^ k) for i in range(n)])  2.43 us
  transfers between devices with their start and end apart: 27, of which 13 were waited for; matrix products, arithmetic and copies ran while one was open for 1% of the time, Pallas kernels for 17%

profile of v1, /device:TPU:0, one launch (start us, length us, event | category | flops | bytes accessed | tf_op | source)
XLA Modules:
  0.0 120.7 jit_solution(12022603513362585048)
XLA Ops:
  3.5 6.9 %local_maps.3 = (f32[4,128,256]{2,1,0:T(8,128)S(1)}, bf16[4,256,256]{2,1,0:T(8,128)(2,1)S(1)}, bf16[4,256,256]{2,1,0:T(8,128)(2,1)S(1)}, f32[2,8,256]{2,1,0:T(8,128)S(1)}) custom-call(s32[4]{0:T(128)S(1)} %pad_add_fusion.w_ref, bf16[256,1024]{1,0:T(8,128)(2,1)S(1)} %copy-done, bf16[256,1024]{1,0:T(8,128)(2,1)S(1)} %copy-done.4, f32[8,256]{1,0:T(8,128)S(1)} %bitcast.28), custom_call_target="tpu_custom_call" | custom-call | tf_op jit(solution)/shard_map/local_maps/pallas_call | solution.py:177
  10.5 1.8 %collective-permute-start.12 = (bf16[256,1024]{1,0:T(8,128)(2,1)}, bf16[256,1024]{1,0:T(8,128)(2,1)S(1)}, u32[]{:S(2)}, u32[]{:S(2)}) collective-permute-start(bf16[256,1024]{1,0:T(8,128)(2,1)} %param.11), channel_id=1, source_target_pairs={{0,0},{1,32},{2,64},{3,96},{32,1},{33,33},{34,65},{35,97},{64,2},{... | collective-permute-start | bytes 1572872 | tf_op jit(solution)/shard_map/ppermute | solution.py:330
  12.4 6.9 %local_maps.2 = (f32[4,128,256]{2,1,0:T(8,128)S(1)}, bf16[4,256,256]{2,1,0:T(8,128)(2,1)S(1)}, bf16[4,256,256]{2,1,0:T(8,128)(2,1)S(1)}, f32[2,8,256]{2,1,0:T(8,128)S(1)}) custom-call(s32[4]{0:T(128)S(1)} %pad_add_fusion.w_ref, bf16[256,1024]{1,0:T(8,128)(2,1)S(1)} %copy-done, bf16[256,1024]{1,0:T(8,128)(2,1)S(1)} %copy-done.4, f32[8,256]{1,0:T(8,128)S(1)} %bitcast.29), custom_call_target="tpu_custom_call" | custom-call | tf_op jit(solution)/shard_map/local_maps/pallas_call | solution.py:177
  20.1 2.1 %collective-permute-start.1 = (f32[128,256]{1,0:T(8,128)S(1)}, f32[128,256]{1,0:T(8,128)S(1)}, u32[]{:S(2)}, u32[]{:S(2)}) collective-permute-start(f32[128,256]{1,0:T(8,128)S(1)} %get-tuple-element.37), channel_id=1, source_target_pairs={{0,8},{8,16},{16,24},{24,0},{1,9},{9,17},{17,25},{25,1},{2,10},{10... | collective-permute-start | bytes 393224 | tf_op jit(solution)/shard_map/ppermute | solution.py:314
  22.2 3.6 %collective-permute-start.2 = (f32[128,256]{1,0:T(8,128)S(1)}, f32[128,256]{1,0:T(8,128)S(1)}, u32[]{:S(2)}, u32[]{:S(2)}) collective-permute-start(f32[128,256]{1,0:T(8,128)S(1)} %get-tuple-element.38), channel_id=1, source_target_pairs={{0,16},{8,24},{16,0},{24,8},{1,17},{9,25},{17,1},{25,9},{2,18},{10... | collective-permute-start | bytes 393224 | tf_op jit(solution)/shard_map/ppermute | solution.py:314
  26.8 1.5 %collective-permute-done.1.m1_ref = f32[128,256]{1,0:T(8,128)S(1)} collective-permute-done((f32[128,256]{1,0:T(8,128)S(1)}, f32[128,256]{1,0:T(8,128)S(1)}, u32[]{:S(2)}, u32[]{:S(2)}) %collective-permute-start.1) | collective-permute-done | bytes 131104 | tf_op jit(solution)/shard_map/ppermute | solution.py:314
  28.4 4.0 %collective-permute-done.2.m2_ref = f32[128,256]{1,0:T(8,128)S(1)} collective-permute-done((f32[128,256]{1,0:T(8,128)S(1)}, f32[128,256]{1,0:T(8,128)S(1)}, u32[]{:S(2)}, u32[]{:S(2)}) %collective-permute-start.2) | collective-permute-done | bytes 131104 | tf_op jit(solution)/shard_map/ppermute | solution.py:314
  32.3 1.2 shard_map.78
  33.5 5.4 %collective-permute-start.4 = (f32[128,256]{1,0:T(8,128)S(1)}, f32[128,256]{1,0:T(8,128)S(1)}, u32[]{:S(2)}, u32[]{:S(2)}) collective-permute-start(f32[128,256]{1,0:T(8,128)S(1)} %get-tuple-element.40), channel_id=1, source_target_pairs={{0,96},{32,0},{64,32},{96,64},{1,97},{33,1},{65,33},{97,65},{2,98}... | collective-permute-start | bytes 393224 | tf_op jit(solution)/shard_map/ppermute | solution.py:314
  39.6 1.3 %collective-permute-start.6 = (f32[128,256]{1,0:T(8,128)S(1)}, f32[128,256]{1,0:T(8,128)S(1)}, u32[]{:S(2)}, u32[]{:S(2)}) collective-permute-start(f32[128,256]{1,0:T(8,128)S(1)} %get-tuple-element.40), channel_id=1, source_target_pairs={{0,32},{32,64},{64,96},{96,0},{1,33},{33,65},{65,97},{97,1},{2,34}... | collective-permute-start | bytes 393224 | tf_op jit(solution)/shard_map/ppermute | solution.py:314
  41.0 5.6 %collective-permute-done.4.m3_ref = f32[128,256]{1,0:T(8,128)S(1)} collective-permute-done((f32[128,256]{1,0:T(8,128)S(1)}, f32[128,256]{1,0:T(8,128)S(1)}, u32[]{:S(2)}, u32[]{:S(2)}) %collective-permute-start.4) | collective-permute-done | bytes 131104 | tf_op jit(solution)/shard_map/ppermute | solution.py:314
  47.6 1.1 shard_map.79
  48.7 1.7 %collective-permute-start.7 = (f32[128,128]{1,0:T(8,128)S(1)}, f32[128,128]{1,0:T(8,128)S(1)}, u32[]{:S(2)}, u32[]{:S(2)}) collective-permute-start(f32[128,128]{1,0:T(8,128)S(1)} %get-tuple-element.43), channel_id=1, source_target_pairs={{0,8},{8,16},{16,24},{24,0},{1,9},{9,17},{17,25},{25,1},{2,10},{10... | collective-permute-start | bytes 196616 | tf_op jit(solution)/shard_map/ppermute | solution.py:314
  50.5 2.8 %collective-permute-start.8 = (f32[128,128]{1,0:T(8,128)S(1)}, f32[128,128]{1,0:T(8,128)S(1)}, u32[]{:S(2)}, u32[]{:S(2)}) collective-permute-start(f32[128,128]{1,0:T(8,128)S(1)} %get-tuple-element.44), channel_id=1, source_target_pairs={{0,16},{8,24},{16,0},{24,8},{1,17},{9,25},{17,1},{25,9},{2,18},{10... | collective-permute-start | bytes 196616 | tf_op jit(solution)/shard_map/ppermute | solution.py:314
  55.0 1.6 %collective-permute-done.8.s2_ref = f32[128,128]{1,0:T(8,128)S(1)} collective-permute-done((f32[128,128]{1,0:T(8,128)S(1)}, f32[128,128]{1,0:T(8,128)S(1)}, u32[]{:S(2)}, u32[]{:S(2)}) %collective-permute-start.8) | collective-permute-done | bytes 65568 | tf_op jit(solution)/shard_map/ppermute | solution.py:314
  58.2 2.3 %collective-permute-start.14 = (bf16[256,1024]{1,0:T(8,128)(2,1)S(1)}, bf16[256,1024]{1,0:T(8,128)(2,1)S(1)}, u32[]{:S(2)}, u32[]{:S(2)}) collective-permute-start(bf16[256,1024]{1,0:T(8,128)(2,1)S(1)} %collective-permute-done.12), channel_id=1, source_target_pairs={{0,2},{1,3},{2,0},{3,1},{4,6},{5,7},{6,4},{7,5},{8,10},{9,11},{10,... | collective-permute-start | bytes 1572872 | tf_op jit(solution)/shard_map/ppermute | solution.py:314
  60.5 1.6 %collective-permute-start.15 = (bf16[256,1024]{1,0:T(8,128)(2,1)S(1)}, bf16[256,1024]{1,0:T(8,128)(2,1)S(1)}, u32[]{:S(2)}, u32[]{:S(2)}) collective-permute-start(bf16[256,1024]{1,0:T(8,128)(2,1)S(1)} %collective-permute-done.12), channel_id=1, source_target_pairs={{0,3},{1,0},{2,1},{3,2},{4,7},{5,4},{6,5},{7,6},{8,11},{9,8},{10,9... | collective-permute-start | bytes 1572872 | tf_op jit(solution)/shard_map/ppermute | solution.py:314
  62.1 2.4 %local_reads.2 = (bf16[4,256,128]{2,1,0:T(8,128)(2,1)S(1)}, bf16[4,256,128]{2,1,0:T(8,128)(2,1)S(1)}, f32[4,256,128]{2,1,0:T(8,128)S(1)}) custom-call(s32[4]{0:T(128)S(1)} %pad_add_fusion.w_ref, bf16[256,1024]{1,0:T(8,128)(2,1)S(1)} %copy-done.5, bf16[256,1024]{1,0:T(8,128)(2,1)S(1)} %copy-done.1, bf16[4,256,256]{2,1,0:T(8,128)(2,1)S(1)} %get-tuple-element.28.xh_ref, ...), custom_call_target="tpu_custom_call" | custom-call | tf_op jit(solution)/shard_map/local_reads/pallas_call | solution.py:229
  64.6 2.4 %local_reads.3 = (bf16[4,256,128]{2,1,0:T(8,128)(2,1)S(1)}, bf16[4,256,128]{2,1,0:T(8,128)(2,1)S(1)}, f32[4,256,128]{2,1,0:T(8,128)S(1)}) custom-call(s32[4]{0:T(128)S(1)} %pad_add_fusion.w_ref, bf16[256,1024]{1,0:T(8,128)(2,1)S(1)} %copy-done.5, bf16[256,1024]{1,0:T(8,128)(2,1)S(1)} %copy-done.1, bf16[4,256,256]{2,1,0:T(8,128)(2,1)S(1)} %get-tuple-element.46.xh_ref, ...), custom_call_target="tpu_custom_call" | custom-call | tf_op jit(solution)/shard_map/local_reads/pallas_call | solution.py:229
  69.0 3.3 %collective-permute-start.18 = (bf16[256,512]{1,0:T(8,128)(2,1)S(1)}, bf16[256,512]{1,0:T(8,128)(2,1)S(1)}, u32[]{:S(2)}, u32[]{:S(2)}) collective-permute-start(bf16[256,512]{1,0:T(8,128)(2,1)S(1)} %shard_map.82.refs_1_), channel_id=1, source_target_pairs={{0,96},{32,0},{64,32},{96,64},{1,97},{33,1},{65,33},{97,65},{2,98}... | collective-permute-start | bytes 786440 | tf_op jit(solution)/shard_map/ppermute | solution.py:314
  72.3 11.1 %collective-permute-start.21 = (bf16[256,512]{1,0:T(8,128)(2,1)S(1)}, bf16[256,512]{1,0:T(8,128)(2,1)S(1)}, u32[]{:S(2)}, u32[]{:S(2)}) collective-permute-start(bf16[256,512]{1,0:T(8,128)(2,1)S(1)} %shard_map.81.refs_0_), channel_id=1, source_target_pairs={{0,96},{32,0},{64,32},{96,64},{1,97},{33,1},{65,33},{97,65},{2,98}... | collective-permute-start | bytes 786440 | tf_op jit(solution)/shard_map/ppermute | solution.py:314
  83.5 3.2 %collective-permute-start.19 = (bf16[256,512]{1,0:T(8,128)(2,1)S(1)}, bf16[256,512]{1,0:T(8,128)(2,1)S(1)}, u32[]{:S(2)}, u32[]{:S(2)}) collective-permute-start(bf16[256,512]{1,0:T(8,128)(2,1)S(1)} %collective-permute-done.18.refs_5_), channel_id=1, source_target_pairs={{0,96},{32,0},{64,32},{96,64},{1,97},{33,1},{65,33},{97,65},{2,98}... | collective-permute-start | bytes 786440 | tf_op jit(solution)/shard_map/ppermute | solution.py:314
  87.0 3.1 %collective-permute-done.21.refs_4_ = bf16[256,512]{1,0:T(8,128)(2,1)S(1)} collective-permute-done((bf16[256,512]{1,0:T(8,128)(2,1)S(1)}, bf16[256,512]{1,0:T(8,128)(2,1)S(1)}, u32[]{:S(2)}, u32[]{:S(2)}) %collective-permute-start.21) | collective-permute-done | bytes 262176 | tf_op jit(solution)/shard_map/ppermute | solution.py:314
  90.1 3.6 %collective-permute-done.20.refs_3_ = bf16[256,512]{1,0:T(8,128)(2,1)S(1)} collective-permute-done((bf16[256,512]{1,0:T(8,128)(2,1)S(1)}, bf16[256,512]{1,0:T(8,128)(2,1)S(1)}, u32[]{:S(2)}, u32[]{:S(2)}) %collective-permute-start.20) | collective-permute-done | bytes 262176 | tf_op jit(solution)/shard_map/ppermute | solution.py:314
  93.7 2.4 %shard_map.83 = (f32[512,1024]{1,0:T(8,128)S(1)}, f32[512,1024]{1,0:T(8,128)S(1)}) custom-call(s32[4]{0:T(128)S(1)} %pad_add_fusion.w_ref, bf16[4,256,1024]{2,1,0:T(8,128)(2,1)S(1)} %pad_maximum_fusion.cot_ref, bf16[256,512]{1,0:T(8,128)(2,1)S(1)} %shard_map.81.refs_0_, bf16[256,512]{1,0:T(8,128)(2,1)S(1)} %shard_map.82.refs_1_, ...), custom_call_target="tpu_custom_call" | custom-call | tf_op jit(solution)/shard_map/pallas_call | solution.py:249
  96.1 1.3 %copy-done.2 = f32[512,1024]{1,0:T(8,128)} copy-done((f32[512,1024]{1,0:T(8,128)}, f32[512,1024]{1,0:T(8,128)S(1)}, u32[]{:S(2)}) %copy-start.2) | copy-done | bytes 2097176
  97.4 2.0 %shard_map.85 = bf16[512,1024]{1,0:T(8,128)(2,1)} custom-call(s32[4]{0:T(128)S(1)} %pad_add_fusion.w_ref, bf16[4,256,1024]{2,1,0:T(8,128)(2,1)S(1)} %pad_maximum_fusion.cot_ref, bf16[256,512]{1,0:T(8,128)(2,1)S(1)} %collective-permute-done.17.b_ref, bf16[256,512]{1,0:T(8,128)(2,1)S(1)} %collective-permute-done.19.a_ref, ...), custom_call_target="tpu_custom_call" | custom-call | tf_op jit(solution)/shard_map/pallas_call | solution.py:249
  99.4 1.6 %copy-done.3 = f32[512,1024]{1,0:T(8,128)S(1)} copy-done((f32[512,1024]{1,0:T(8,128)S(1)}, f32[512,1024]{1,0:T(8,128)}, u32[]{:S(2)}) %copy-start.3) | copy-done | bytes 2097176
  102.4 1.6 %slice_add_fusion.1 = (f32[512,512]{1,0:T(8,128)S(1)}, f32[512,512]{1,0:T(8,128)S(1)}) fusion(f32[512,1024]{1,0:T(8,128)S(1)} %shard_map.84, bf16[512,1024]{1,0:T(8,128)(2,1)} %collective-permute-done.22), kind=kLoop, calls=%fused_computation.2 | loop fusion | flops 1048576 | bytes 5242880 | tf_op jit(solution)/shard_map/add | solution.py:372
  106.8 5.8 %collective-permute-done.23 = bf16[256,512]{1,0:T(8,128)(2,1)S(1)} collective-permute-done((bf16[256,512]{1,0:T(8,128)(2,1)S(1)}, bf16[256,512]{1,0:T(8,128)(2,1)S(1)}, u32[]{:S(2)}, u32[]{:S(2)}) %collective-permute-start.23) | collective-permute-done | bytes 262176 | tf_op jit(solution)/shard_map/ppermute | solution.py:319
  113.1 1.5 %collective-permute-done.25 = bf16[256,512]{1,0:T(8,128)(2,1)S(1)} collective-permute-done((bf16[256,512]{1,0:T(8,128)(2,1)S(1)}, bf16[256,512]{1,0:T(8,128)(2,1)S(1)}, u32[]{:S(2)}, u32[]{:S(2)}) %collective-permute-start.25) | collective-permute-done | bytes 262176 | tf_op jit(solution)/shard_map/ppermute | solution.py:319
  114.8 4.1 %collective-permute-done.24 = bf16[128,512]{1,0:T(8,128)(2,1)S(1)} collective-permute-done((bf16[128,512]{1,0:T(8,128)(2,1)S(1)}, bf16[128,512]{1,0:T(8,128)(2,1)S(1)}, u32[]{:S(2)}, u32[]{:S(2)}) %collective-permute-start.24) | collective-permute-done | bytes 131104 | tf_op jit(solution)/shard_map/ppermute | solution.py:319
  (66 shorter events, 18.9 us)
Async XLA Ops:
  10.4 51.7 %copy-start.1 = (bf16[256,1024]{1,0:T(8,128)(2,1)S(1)}, bf16[256,1024]{1,0:T(8,128)(2,1)}, u32[]{:S(2)}) copy-start(bf16[256,1024]{1,0:T(8,128)(2,1)} %k_ref.7) | copy-start | bytes 1572868
  10.4 51.7 %copy-start.5 = (bf16[256,1024]{1,0:T(8,128)(2,1)S(1)}, bf16[256,1024]{1,0:T(8,128)(2,1)}, u32[]{:S(2)}) copy-start(bf16[256,1024]{1,0:T(8,128)(2,1)} %q_ref.3) | copy-start | bytes 1572868
  10.4 8.8 %collective-permute-start = (f32[4,128,256]{2,1,0:T(8,128)S(1)}, f32[4,128,256]{2,1,0:T(8,128)S(1)}, u32[]{:S(2)}, u32[]{:S(2)}) collective-permute-start(f32[4,128,256]{2,1,0:T(8,128)S(1)} %get-tuple-element.31), channel_id=1, source_target_pairs={{0,4},{4,0},{1,5},{5,1},{2,6},{6,2},{3,7},{7,3},{8,12},{12,8},{9,1... | collective-permute-start | bytes 1572872 | tf_op jit(solution)/shard_map/ppermute | solution.py:319
  10.5 43.7 %collective-permute-start.12 = (bf16[256,1024]{1,0:T(8,128)(2,1)}, bf16[256,1024]{1,0:T(8,128)(2,1)S(1)}, u32[]{:S(2)}, u32[]{:S(2)}) collective-permute-start(bf16[256,1024]{1,0:T(8,128)(2,1)} %param.11), channel_id=1, source_target_pairs={{0,0},{1,32},{2,64},{3,96},{32,1},{33,33},{34,65},{35,97},{64,2},{... | collective-permute-start | bytes 1572872 | tf_op jit(solution)/shard_map/ppermute | solution.py:330
  20.1 8.2 %collective-permute-start.1 = (f32[128,256]{1,0:T(8,128)S(1)}, f32[128,256]{1,0:T(8,128)S(1)}, u32[]{:S(2)}, u32[]{:S(2)}) collective-permute-start(f32[128,256]{1,0:T(8,128)S(1)} %get-tuple-element.37), channel_id=1, source_target_pairs={{0,8},{8,16},{16,24},{24,0},{1,9},{9,17},{17,25},{25,1},{2,10},{10... | collective-permute-start | bytes 393224 | tf_op jit(solution)/shard_map/ppermute | solution.py:314
  22.2 10.1 %collective-permute-start.2 = (f32[128,256]{1,0:T(8,128)S(1)}, f32[128,256]{1,0:T(8,128)S(1)}, u32[]{:S(2)}, u32[]{:S(2)}) collective-permute-start(f32[128,256]{1,0:T(8,128)S(1)} %get-tuple-element.38), channel_id=1, source_target_pairs={{0,16},{8,24},{16,0},{24,8},{1,17},{9,25},{17,1},{25,9},{2,18},{10... | collective-permute-start | bytes 393224 | tf_op jit(solution)/shard_map/ppermute | solution.py:314
  25.8 6.5 %collective-permute-start.3 = (f32[128,256]{1,0:T(8,128)S(1)}, f32[128,256]{1,0:T(8,128)S(1)}, u32[]{:S(2)}, u32[]{:S(2)}) collective-permute-start(f32[128,256]{1,0:T(8,128)S(1)} %get-tuple-element.39), channel_id=1, source_target_pairs={{0,24},{8,0},{16,8},{24,16},{1,25},{9,1},{17,9},{25,17},{2,26},{10... | collective-permute-start | bytes 393224 | tf_op jit(solution)/shard_map/ppermute | solution.py:314
  26.8 37.7 %collective-permute-start.10 = (f32[4,128,256]{2,1,0:T(8,128)S(1)}, f32[4,128,256]{2,1,0:T(8,128)S(1)}, u32[]{:S(2)}, u32[]{:S(2)}) collective-permute-start(f32[4,128,256]{2,1,0:T(8,128)S(1)} %get-tuple-element.35.own_ref), channel_id=1, source_target_pairs={{0,4},{4,0},{1,5},{5,1},{2,6},{6,2},{3,7},{7,3},{8,12},{12,8},{9,1... | collective-permute-start | bytes 1572872 | tf_op jit(solution)/shard_map/ppermute | solution.py:319
  33.5 13.0 %collective-permute-start.4 = (f32[128,256]{1,0:T(8,128)S(1)}, f32[128,256]{1,0:T(8,128)S(1)}, u32[]{:S(2)}, u32[]{:S(2)}) collective-permute-start(f32[128,256]{1,0:T(8,128)S(1)} %get-tuple-element.40), channel_id=1, source_target_pairs={{0,96},{32,0},{64,32},{96,64},{1,97},{33,1},{65,33},{97,65},{2,98}... | collective-permute-start | bytes 393224 | tf_op jit(solution)/shard_map/ppermute | solution.py:314
  38.9 7.6 %collective-permute-start.5 = (f32[128,256]{1,0:T(8,128)S(1)}, f32[128,256]{1,0:T(8,128)S(1)}, u32[]{:S(2)}, u32[]{:S(2)}) collective-permute-start(f32[128,256]{1,0:T(8,128)S(1)} %get-tuple-element.40), channel_id=1, source_target_pairs={{0,64},{32,96},{64,0},{96,32},{1,65},{33,97},{65,1},{97,33},{2,66}... | collective-permute-start | bytes 393224 | tf_op jit(solution)/shard_map/ppermute | solution.py:314
  39.6 8.0 %collective-permute-start.6 = (f32[128,256]{1,0:T(8,128)S(1)}, f32[128,256]{1,0:T(8,128)S(1)}, u32[]{:S(2)}, u32[]{:S(2)}) collective-permute-start(f32[128,256]{1,0:T(8,128)S(1)} %get-tuple-element.40), channel_id=1, source_target_pairs={{0,32},{32,64},{64,96},{96,0},{1,33},{33,65},{65,97},{97,1},{2,34}... | collective-permute-start | bytes 393224 | tf_op jit(solution)/shard_map/ppermute | solution.py:314
  48.7 6.3 %collective-permute-start.7 = (f32[128,128]{1,0:T(8,128)S(1)}, f32[128,128]{1,0:T(8,128)S(1)}, u32[]{:S(2)}, u32[]{:S(2)}) collective-permute-start(f32[128,128]{1,0:T(8,128)S(1)} %get-tuple-element.43), channel_id=1, source_target_pairs={{0,8},{8,16},{16,24},{24,0},{1,9},{9,17},{17,25},{25,1},{2,10},{10... | collective-permute-start | bytes 196616 | tf_op jit(solution)/shard_map/ppermute | solution.py:314
  50.5 6.2 %collective-permute-start.8 = (f32[128,128]{1,0:T(8,128)S(1)}, f32[128,128]{1,0:T(8,128)S(1)}, u32[]{:S(2)}, u32[]{:S(2)}) collective-permute-start(f32[128,128]{1,0:T(8,128)S(1)} %get-tuple-element.44), channel_id=1, source_target_pairs={{0,16},{8,24},{16,0},{24,8},{1,17},{9,25},{17,1},{25,9},{2,18},{10... | collective-permute-start | bytes 196616 | tf_op jit(solution)/shard_map/ppermute | solution.py:314
  53.2 4.3 %collective-permute-start.9 = (f32[128,128]{1,0:T(8,128)S(1)}, f32[128,128]{1,0:T(8,128)S(1)}, u32[]{:S(2)}, u32[]{:S(2)}) collective-permute-start(f32[128,128]{1,0:T(8,128)S(1)} %get-tuple-element.45), channel_id=1, source_target_pairs={{0,24},{8,0},{16,8},{24,16},{1,25},{9,1},{17,9},{25,17},{2,26},{10... | collective-permute-start | bytes 196616 | tf_op jit(solution)/shard_map/ppermute | solution.py:314
  54.2 18.1 %collective-permute-start.13 = (bf16[256,1024]{1,0:T(8,128)(2,1)S(1)}, bf16[256,1024]{1,0:T(8,128)(2,1)S(1)}, u32[]{:S(2)}, u32[]{:S(2)}) collective-permute-start(bf16[256,1024]{1,0:T(8,128)(2,1)S(1)} %collective-permute-done.12), channel_id=1, source_target_pairs={{0,1},{1,2},{2,3},{3,0},{4,5},{5,6},{6,7},{7,4},{8,9},{9,10},{10,1... | collective-permute-start | bytes 1572872 | tf_op jit(solution)/shard_map/ppermute | solution.py:314
  58.1 10.0 %collective-permute-start.11 = (f32[4,128,128]{2,1,0:T(8,128)S(1)}, f32[4,128,128]{2,1,0:T(8,128)S(1)}, u32[]{:S(2)}, u32[]{:S(2)}) collective-permute-start(f32[4,128,128]{2,1,0:T(8,128)S(1)} %shard_map.80.s_ref), channel_id=1, source_target_pairs={{0,4},{4,0},{1,5},{5,1},{2,6},{6,2},{3,7},{7,3},{8,12},{12,8},{9,1... | collective-permute-start | bytes 786440 | tf_op jit(solution)/shard_map/ppermute | solution.py:319
  58.2 25.2 %collective-permute-start.14 = (bf16[256,1024]{1,0:T(8,128)(2,1)S(1)}, bf16[256,1024]{1,0:T(8,128)(2,1)S(1)}, u32[]{:S(2)}, u32[]{:S(2)}) collective-permute-start(bf16[256,1024]{1,0:T(8,128)(2,1)S(1)} %collective-permute-done.12), channel_id=1, source_target_pairs={{0,2},{1,3},{2,0},{3,1},{4,6},{5,7},{6,4},{7,5},{8,10},{9,11},{10,... | collective-permute-start | bytes 1572872 | tf_op jit(solution)/shard_map/ppermute | solution.py:314
  60.5 26.2 %collective-permute-start.15 = (bf16[256,1024]{1,0:T(8,128)(2,1)S(1)}, bf16[256,1024]{1,0:T(8,128)(2,1)S(1)}, u32[]{:S(2)}, u32[]{:S(2)}) collective-permute-start(bf16[256,1024]{1,0:T(8,128)(2,1)S(1)} %collective-permute-done.12), channel_id=1, source_target_pairs={{0,3},{1,0},{2,1},{3,2},{4,7},{5,4},{6,5},{7,6},{8,11},{9,8},{10,9... | collective-permute-start | bytes 1572872 | tf_op jit(solution)/shard_map/ppermute | solution.py:314
  62.1 4.9 %copy-start.7 = (f32[128]{0:T(128)S(1)}, f32[128]{0:T(128)}, u32[]{:S(2)}) copy-start(f32[128]{0:T(128)} %param.10) | copy-start | bytes 1540
  68.0 15.4 %collective-permute-start.16 = (bf16[256,512]{1,0:T(8,128)(2,1)S(1)}, bf16[256,512]{1,0:T(8,128)(2,1)S(1)}, u32[]{:S(2)}, u32[]{:S(2)}) collective-permute-start(bf16[256,512]{1,0:T(8,128)(2,1)S(1)} %shard_map.81.refs_0_), channel_id=1, source_target_pairs={{0,32},{32,64},{64,96},{96,0},{1,33},{33,65},{65,97},{97,1},{2,34}... | collective-permute-start | bytes 786440 | tf_op jit(solution)/shard_map/ppermute | solution.py:314
  69.0 14.5 %collective-permute-start.18 = (bf16[256,512]{1,0:T(8,128)(2,1)S(1)}, bf16[256,512]{1,0:T(8,128)(2,1)S(1)}, u32[]{:S(2)}, u32[]{:S(2)}) collective-permute-start(bf16[256,512]{1,0:T(8,128)(2,1)S(1)} %shard_map.82.refs_1_), channel_id=1, source_target_pairs={{0,96},{32,0},{64,32},{96,64},{1,97},{33,1},{65,33},{97,65},{2,98}... | collective-permute-start | bytes 786440 | tf_op jit(solution)/shard_map/ppermute | solution.py:314
  72.3 17.8 %collective-permute-start.21 = (bf16[256,512]{1,0:T(8,128)(2,1)S(1)}, bf16[256,512]{1,0:T(8,128)(2,1)S(1)}, u32[]{:S(2)}, u32[]{:S(2)}) collective-permute-start(bf16[256,512]{1,0:T(8,128)(2,1)S(1)} %shard_map.81.refs_0_), channel_id=1, source_target_pairs={{0,96},{32,0},{64,32},{96,64},{1,97},{33,1},{65,33},{97,65},{2,98}... | collective-permute-start | bytes 786440 | tf_op jit(solution)/shard_map/ppermute | solution.py:314
  83.4 10.3 %collective-permute-start.20 = (bf16[256,512]{1,0:T(8,128)(2,1)S(1)}, bf16[256,512]{1,0:T(8,128)(2,1)S(1)}, u32[]{:S(2)}, u32[]{:S(2)}) collective-permute-start(bf16[256,512]{1,0:T(8,128)(2,1)S(1)} %shard_map.82.refs_1_), channel_id=1, source_target_pairs={{0,32},{32,64},{64,96},{96,0},{1,33},{33,65},{65,97},{97,1},{2,34}... | collective-permute-start | bytes 786440 | tf_op jit(solution)/shard_map/ppermute | solution.py:314
  83.4 14.0 %collective-permute-start.17 = (bf16[256,512]{1,0:T(8,128)(2,1)S(1)}, bf16[256,512]{1,0:T(8,128)(2,1)S(1)}, u32[]{:S(2)}, u32[]{:S(2)}) collective-permute-start(bf16[256,512]{1,0:T(8,128)(2,1)S(1)} %collective-permute-done.16.refs_2_), channel_id=1, source_target_pairs={{0,32},{32,64},{64,96},{96,0},{1,33},{33,65},{65,97},{97,1},{2,34}... | collective-permute-start | bytes 786440 | tf_op jit(solution)/shard_map/ppermute | solution.py:314
  83.5 13.9 %collective-permute-start.19 = (bf16[256,512]{1,0:T(8,128)(2,1)S(1)}, bf16[256,512]{1,0:T(8,128)(2,1)S(1)}, u32[]{:S(2)}, u32[]{:S(2)}) collective-permute-start(bf16[256,512]{1,0:T(8,128)(2,1)S(1)} %collective-permute-done.18.refs_5_), channel_id=1, source_target_pairs={{0,96},{32,0},{64,32},{96,64},{1,97},{33,1},{65,33},{97,65},{2,98}... | collective-permute-start | bytes 786440 | tf_op jit(solution)/shard_map/ppermute | solution.py:314
  96.1 1.4 %copy-start.2 = (f32[512,1024]{1,0:T(8,128)}, f32[512,1024]{1,0:T(8,128)S(1)}, u32[]{:S(2)}) copy-start(f32[512,1024]{1,0:T(8,128)S(1)} %get-tuple-element.52.part_ref) | copy-start | bytes 6291460
  99.4 3.0 %collective-permute-start.22 = (bf16[512,1024]{1,0:T(8,128)(2,1)}, bf16[512,1024]{1,0:T(8,128)(2,1)}, u32[]{:S(2)}, u32[]{:S(2)}) collective-permute-start(bf16[512,1024]{1,0:T(8,128)(2,1)} %shard_map.85), channel_id=1, source_target_pairs={{0,4},{4,0},{1,5},{5,1},{2,6},{6,2},{3,7},{7,3},{8,12},{12,8},{9,1... | collective-permute-start | bytes 3145736 | tf_op jit(solution)/shard_map/ppermute | solution.py:319
  99.4 1.6 %copy-start.3 = (f32[512,1024]{1,0:T(8,128)S(1)}, f32[512,1024]{1,0:T(8,128)}, u32[]{:S(2)}) copy-start(f32[512,1024]{1,0:T(8,128)} %copy-done.2) | copy-start | bytes 6291460
  104.1 8.4 %collective-permute-start.23 = (bf16[256,512]{1,0:T(8,128)(2,1)S(1)}, bf16[256,512]{1,0:T(8,128)(2,1)S(1)}, u32[]{:S(2)}, u32[]{:S(2)}) collective-permute-start(bf16[256,512]{1,0:T(8,128)(2,1)S(1)} %pad_maximum_fusion.1), channel_id=1, source_target_pairs={{0,8},{8,0},{16,24},{24,16},{1,9},{9,1},{17,25},{25,17},{2,10},{10... | collective-permute-start | bytes 786440 | tf_op jit(solution)/shard_map/ppermute | solution.py:319
  105.3 9.4 %collective-permute-start.25 = (bf16[256,512]{1,0:T(8,128)(2,1)S(1)}, bf16[256,512]{1,0:T(8,128)(2,1)S(1)}, u32[]{:S(2)}, u32[]{:S(2)}) collective-permute-start(bf16[256,512]{1,0:T(8,128)(2,1)S(1)} %pad_maximum_fusion.2), channel_id=1, source_target_pairs={{0,24},{8,16},{16,8},{24,0},{1,25},{9,17},{17,9},{25,1},{2,26},{10... | collective-permute-start | bytes 786440 | tf_op jit(solution)/shard_map/ppermute | solution.py:319
  112.6 6.3 %collective-permute-start.24 = (bf16[128,512]{1,0:T(8,128)(2,1)S(1)}, bf16[128,512]{1,0:T(8,128)(2,1)S(1)}, u32[]{:S(2)}, u32[]{:S(2)}) collective-permute-start(bf16[128,512]{1,0:T(8,128)(2,1)S(1)} %fusion.2), channel_id=1, source_target_pairs={{0,24},{8,16},{16,8},{24,0},{1,25},{9,17},{17,9},{25,1},{2,26},{10... | collective-permute-start | bytes 393224 | tf_op jit(solution)/shard_map/ppermute | solution.py:319
  114.7 5.0 %collective-permute-start.26 = (bf16[128,512]{1,0:T(8,128)(2,1)S(1)}, bf16[128,512]{1,0:T(8,128)(2,1)S(1)}, u32[]{:S(2)}, u32[]{:S(2)}) collective-permute-start(bf16[128,512]{1,0:T(8,128)(2,1)S(1)} %fusion), channel_id=1, source_target_pairs={{0,8},{8,0},{16,24},{24,16},{1,9},{9,1},{17,25},{25,17},{2,10},{10... | collective-permute-start | bytes 393224 | tf_op jit(solution)/shard_map/ppermute | solution.py:319
  (3 other events, 2.8 us)

commit v2 on v1

--- a/solution.py
+++ b/solution.py
@@ -57,7 +57,7 @@
     return dot(jnp.concatenate([ph, pl_], axis=1), jnp.concatenate([rh, rh], axis=0)) + dot(ph, rl)
 
 
-HB = 2
+HB = 4
 
 
 def half_of(mine, w):
@@ -164,6 +164,10 @@
 PARAMS = pltpu.CompilerParams(vmem_limit_bytes=24 << 20)
 
 
+def in_hbm(x):
+    return pltpu.with_memory_space_constraint(x, pltpu.HBM)
+
+
 def in_vmem(x):
     return pltpu.with_memory_space_constraint(x, pltpu.VMEM)
 
@@ -190,7 +194,7 @@
         ],
         compiler_params=PARAMS,
         name="local_maps",
-    )(where, k, v, beta_rows)
+    )(where, in_hbm(k), in_hbm(v), in_hbm(beta_rows))
 
 
 def reads_kernel(w_ref, q_ref, k_ref, xh_ref, xl_ref, r_ref, m_ref, qh_ref, ql_ref, y_ref):
@@ -237,7 +241,7 @@
         out_shape=[vmem((4, TOK, F), bf16), vmem((4, TOK, F), bf16), vmem((4, TOK, F))],
         compiler_params=PARAMS,
         name="local_reads",
-    )(where, q, k, *[in_vmem(a) for a in (xh, xl, r, first)])
+    )(where, in_hbm(q), in_hbm(k), *[in_vmem(a) for a in (xh, xl, r, first)])
 
 
 def after(p_then, m):
@@ -319,18 +323,13 @@
     return lax.ppermute(x, axis, [(i, i ^ k) for i in range(n)])
 
 
-def pick(x, i):
-    return lax.dynamic_index_in_dim(x, i, 0, False)
-
-
 def body(query_rows, key_rows, value_rows, beta, norm_gain, out_cotangent):
     yi, zi, ci, hi = (lax.axis_index(a).astype(jnp.int32) for a in ("y", "z", "core", "head"))
     where = jnp.stack([yi, zi, ci, hi])
 
     cot = lax.ppermute(out_cotangent, ("y", "head"), [(a * 4 + b, b * 4 + a) for a in range(4) for b in range(4)])
-    cots = [cot]
-    for k in (1, 2, 3):
-        cots.append(shift(cot, "head", k))
+    cot2 = jnp.stack([cot, swap(cot, "head", 1)])
+    cots = jnp.concatenate([cot2, swap(cot2, "head", 3)])
     gain = norm_gain.reshape(1, F)
     beta_rows = beta.T
     m_a, xh_a, xl_a, r_a = local_maps(False, where, key_rows, value_rows, beta_rows)
@@ -363,30 +362,27 @@
     far_b = shift(up_b, "y", 1)
     far_a = shift(dn_a, "y", -1)
 
-    cots = jnp.stack(cots)
     parts = stage(part_kernel, where, [vmem((4 * F, 8 * F))] * 2, cots, att_b, att_a, up_b, up_a, dn_b, dn_a)
     w_send, = stage(functools.partial(last_kernel, 0), where, [vmem((4 * F, 8 * F), bf16)], cots, far_b, far_a, parts[0])
     w_got = swap(w_send, "core", 1)
     w, = stage(functools.partial(last_kernel, 1), where, [vmem((4 * F, 8 * F))], cots, far_b, far_a, parts[1])
-    h = 4 * F
-    w_b = (w[:, :h] + w_got[:, h:].astype(f32)).reshape(4, F, h)
-    w_a = (w[:, h:] + w_got[:, :h].astype(f32)).reshape(4, F, h)
-
-    def halving(w, first, second):
-        z1, z2, z3 = zi ^ first, zi ^ first ^ second, zi ^ second
-        s = swap(jnp.concatenate([pick(w, z1), pick(w, z2)]).astype(bf16), "z", first).astype(f32)
-        keep, on = pick(w, zi) + s[:F], pick(w, z3) + s[F:]
-        return keep + swap(on.astype(bf16), "z", second).astype(f32)
-
-    g_b = halving(w_b, 1, 3)
-    g_a = halving(w_a, 3, 1)
-    grad = jnp.where(ci == 0, jnp.concatenate([g_b, g_a], axis=1), jnp.concatenate([g_a, g_b], axis=1))
+    quarter = vmem((2 * F, 4 * F), bf16)
+    kept = vmem((2 * F, 4 * F))
+    on_b, on_a, k_b, k_a = stage(sum_kernel, where, [quarter, quarter, kept, kept], w, w_got)
+    r_b = swap(on_b, "z", 1)
+    r_a = swap(on_a, "z", 3)
+    h_b = (k_b[F:] + r_b[F:].astype(f32)).astype(bf16)
+    e_b = swap(h_b, "z", 3)
+    h_a = (k_a[F:] + r_a[F:].astype(f32)).astype(bf16)
+    e_a = swap(h_a, "z", 1)
+    grad, = stage(final_kernel, where, [jax.ShapeDtypeStruct((F, 8 * F), f32)], k_b, r_b, e_b, k_a, r_a, e_a)
     attended = jnp.where(ci == 0, jnp.concatenate([att_b, att_a], axis=1), jnp.concatenate([att_a, att_b], axis=1))
     return attended, grad
 
 
 def cot_rows(w_ref, cot_ref, k, part):
-    j = lax.rem(w_ref[3] - w_ref[0] + k + 4, 4)
+    d = lax.rem(w_ref[0] - k + 4, 4) ^ w_ref[3]
+    j = d ^ (d >> 1)
     core = half_of(part == 1, w_ref)
     return jnp.concatenate(
         [cot_ref[j, :, pl.ds(pl.multiple_of((2 * n + core) * F, F), F)] for n in range(4)], axis=1
@@ -406,6 +402,27 @@
     for n, ref in enumerate((b_ref, a_ref)):
         cols = slice(n * 4 * F, (n + 1) * 4 * F)
         out_ref[:, cols] = (part_ref[:, cols] + dot_tn(rows, ref[...])).astype(out_ref.dtype)
+
+
+def sum_kernel(w_ref, keep_ref, got_ref, on_b_ref, on_a_ref, k_b_ref, k_a_ref):
+    z = w_ref[1]
+    h = 4 * F
+    for n, (on_ref, k_ref, first, second) in enumerate(((on_b_ref, k_b_ref, 1, 3), (on_a_ref, k_a_ref, 3, 1))):
+        mine = slice(n * h, (n + 1) * h)
+        theirs = slice((1 - n) * h, (2 - n) * h)
+        for i, (ref, blk) in enumerate(((on_ref, z ^ first), (on_ref, z ^ 2), (k_ref, z), (k_ref, z ^ second))):
+            rows = pl.ds(pl.multiple_of(blk * F, F), F)
+            total = keep_ref[rows, mine] + got_ref[rows, theirs].astype(f32)
+            ref[(i % 2) * F:(i % 2 + 1) * F, :] = total.astype(ref.dtype)
+
+
+def final_kernel(w_ref, k_b_ref, r_b_ref, e_b_ref, k_a_ref, r_a_ref, e_a_ref, out_ref):
+    c = w_ref[2]
+    g_b = k_b_ref[:F] + r_b_ref[:F].astype(f32) + e_b_ref[...].astype(f32)
+    g_a = k_a_ref[:F] + r_a_ref[:F].astype(f32) + e_a_ref[...].astype(f32)
+    h = 4 * F
+    out_ref[:, :h] = jnp.where(c == 0, g_b, g_a)
+    out_ref[:, h:] = jnp.where(c == 0, g_a, g_b)
 
 
 def solution(mesh):

time: 121 us -> 137 us (1.13)
  starting transfers between devices: 46.3 us -> 63.5 us
  waiting for transfers between devices: 33.9 us -> 40.8 us
  local copies, waits for them, and re-layouts: 5.81 us -> 0.01 us
  other arithmetic: 4.05 us -> 1.37 us
    ppermute x8 -> x10, starting transfers between devices: 2.43 us -> 38.9 us  [swap(): return lax.ppermute(x, axis, [(i, i ^ k) for i in range(n)])]
    ppermute x18 -> x15, starting transfers between devices: 42.1 us -> 22.9 us  [shift(): return lax.ppermute(x, axis, [(i, (i + k) % 4) for i in range(4)])]
    unnamed x16 -> x2, local copies, waits for them, and re-layouts: 5.73 us -> 0.01 us
    ppermute x8 -> x10, waiting for transfers between devices: 12.6 us -> 18.2 us  [swap(): return lax.ppermute(x, axis, [(i, i ^ k) for i in range(n)])]
    pallas_call x2, Pallas kernels: 13.8 us -> 10.9 us  [local_maps(): pl.pallas_call(functools.partial(local_kernel, mine), grid_spec=pltpu.Pre...]
    pallas_call x2, Pallas kernels: 4.89 us -> 6.63 us  [local_reads(): pl.pallas_call(reads_kernel, grid_spec=pltpu.PrefetchScalarGridSpec(num_s...]
    add x3 -> x0, other arithmetic: 1.7 us -> none  [the longest x1 1.57 us: body(): w_b = (w[:, :h] + w_got[:, h:].astype(f32)).reshape(4, F, h)]
    ppermute x18 -> x15, waiting for transfers between devices: 21.4 us -> 22.6 us  [shift(): return lax.ppermute(x, axis, [(i, (i + k) % 4) for i in range(4)])]
  transfers between devices with their start and end apart: 27 -> 26, of which waited for: 13 -> 20; matrix products, arithmetic and copies ran while one was open for 1% -> 1% of each run, Pallas kernels for 17% -> 19%
where the time goes in v2:
time: 137 us; the launch traced here: 136 us
  starting transfers between devices  63.5 us (46%)
  waiting for transfers between devices  40.8 us (30%)
  Pallas kernels  29.7 us (22%)
  other arithmetic  1.37 us (1%)
    ppermute x10, starting transfers between devices, swap(): return lax.ppermute(x, axis, [(i, i ^ k) for i in range(n)])  38.9 us
    ppermute x15, starting transfers between devices, shift(): return lax.ppermute(x, axis, [(i, (i + k) % 4) for i in range(4)])  22.9 us
    ppermute x15, waiting for transfers between devices, shift(): return lax.ppermute(x, axis, [(i, (i + k) % 4) for i in range(4)])  22.6 us
    ppermute x10, waiting for transfers between devices, swap(): return lax.ppermute(x, axis, [(i, i ^ k) for i in range(n)])  18.2 us
    pallas_call x11, Pallas kernels, stage(): pl.pallas_call(kernel, in_specs=[pl.BlockSpec(memory_space=pltpu.SMEM)] +...  12.2 us
    pallas_call x2, Pallas kernels, local_maps(): pl.pallas_call(functools.partial(local_kernel, mine), grid_spec=pltpu.Pre...  10.9 us
    pallas_call x2, Pallas kernels, local_reads(): pl.pallas_call(reads_kernel, grid_spec=pltpu.PrefetchScalarGridSpec(num_s...  6.63 us
  transfers between devices with their start and end apart: 26, of which 20 were waited for; matrix products, arithmetic and copies ran while one was open for 1% of the time, Pallas kernels for 19%

profile of v2, /device:TPU:0, one launch (start us, length us, event | category | flops | bytes accessed | tf_op | source)
XLA Modules:
  0.0 136.2 jit_solution(7593950713261218590)
XLA Ops:
  0.6 1.7 %collective-permute-start.12 = (bf16[256,1024]{1,0:T(8,128)(2,1)}, bf16[256,1024]{1,0:T(8,128)(2,1)S(1)}, u32[]{:S(2)}, u32[]{:S(2)}) collective-permute-start(bf16[256,1024]{1,0:T(8,128)(2,1)} %param.11), channel_id=1, source_target_pairs={{0,0},{1,32},{2,64},{3,96},{32,1},{33,33},{34,65},{35,97},{64,2},{... | collective-permute-start | bytes 1572872 | tf_op jit(solution)/shard_map/ppermute | solution.py:330
  2.3 26.1 %collective-permute-start.13 = (bf16[256,1024]{1,0:T(8,128)(2,1)S(1)}, bf16[256,1024]{1,0:T(8,128)(2,1)S(1)}, u32[]{:S(2)}, u32[]{:S(2)}) collective-permute-start(bf16[256,1024]{1,0:T(8,128)(2,1)S(1)} %collective-permute-done.12), channel_id=1, source_target_pairs={{0,1},{1,0},{2,3},{3,2},{4,5},{5,4},{6,7},{7,6},{8,9},{9,8},{10,11... | collective-permute-start | bytes 1572872 | tf_op jit(solution)/shard_map/ppermute | solution.py:323
  28.5 5.4 %local_maps.3 = (f32[4,128,256]{2,1,0:T(8,128)S(1)}, bf16[4,256,256]{2,1,0:T(8,128)(2,1)S(1)}, bf16[4,256,256]{2,1,0:T(8,128)(2,1)S(1)}, f32[1,8,256]{2,1,0:T(8,128)S(1)}) custom-call(s32[4]{0:T(128)S(1)} %pad_add_fusion.w_ref, bf16[256,1024]{1,0:T(8,128)(2,1)} %k_ref.7, bf16[256,1024]{1,0:T(8,128)(2,1)} %v_ref.3, f32[8,256]{1,0:T(8,128)} %bitcast.14), custom_call_target="tpu_custom_call" | custom-call | tf_op jit(solution)/shard_map/local_maps/pallas_call | solution.py:181
  34.0 5.1 %collective-permute-done.13 = bf16[256,1024]{1,0:T(8,128)(2,1)S(1)} collective-permute-done((bf16[256,1024]{1,0:T(8,128)(2,1)S(1)}, bf16[256,1024]{1,0:T(8,128)(2,1)S(1)}, u32[]{:S(2)}, u32[]{:S(2)}) %collective-permute-start.13) | collective-permute-done | bytes 524320 | tf_op jit(solution)/shard_map/ppermute | solution.py:323
  39.2 7.6 %collective-permute-start.14 = (bf16[2,256,1024]{2,1,0:T(8,128)(2,1)S(1)}, bf16[2,256,1024]{2,1,0:T(8,128)(2,1)S(1)}, u32[]{:S(2)}, u32[]{:S(2)}) collective-permute-start(bf16[2,256,1024]{2,1,0:T(8,128)(2,1)S(1)} %pad_maximum_fusion.1), channel_id=1, source_target_pairs={{0,3},{1,2},{2,1},{3,0},{4,7},{5,6},{6,5},{7,4},{8,11},{9,10},{10,... | collective-permute-start | bytes 3145736 | tf_op jit(solution)/shard_map/ppermute | solution.py:323
  46.8 5.4 %local_maps.2 = (f32[4,128,256]{2,1,0:T(8,128)S(1)}, bf16[4,256,256]{2,1,0:T(8,128)(2,1)S(1)}, bf16[4,256,256]{2,1,0:T(8,128)(2,1)S(1)}, f32[1,8,256]{2,1,0:T(8,128)S(1)}) custom-call(s32[4]{0:T(128)S(1)} %pad_add_fusion.w_ref, bf16[256,1024]{1,0:T(8,128)(2,1)} %k_ref.7, bf16[256,1024]{1,0:T(8,128)(2,1)} %v_ref.3, f32[8,256]{1,0:T(8,128)} %bitcast.15), custom_call_target="tpu_custom_call" | custom-call | tf_op jit(solution)/shard_map/local_maps/pallas_call | solution.py:181
  53.1 2.0 %collective-permute-start.1 = (f32[128,256]{1,0:T(8,128)S(1)}, f32[128,256]{1,0:T(8,128)S(1)}, u32[]{:S(2)}, u32[]{:S(2)}) collective-permute-start(f32[128,256]{1,0:T(8,128)S(1)} %get-tuple-element.41), channel_id=1, source_target_pairs={{0,8},{8,16},{16,24},{24,0},{1,9},{9,17},{17,25},{25,1},{2,10},{10... | collective-permute-start | bytes 393224 | tf_op jit(solution)/shard_map/ppermute | solution.py:318
  55.1 3.6 %collective-permute-start.2 = (f32[128,256]{1,0:T(8,128)S(1)}, f32[128,256]{1,0:T(8,128)S(1)}, u32[]{:S(2)}, u32[]{:S(2)}) collective-permute-start(f32[128,256]{1,0:T(8,128)S(1)} %get-tuple-element.42), channel_id=1, source_target_pairs={{0,16},{8,24},{16,0},{24,8},{1,17},{9,25},{17,1},{25,9},{2,18},{10... | collective-permute-start | bytes 393224 | tf_op jit(solution)/shard_map/ppermute | solution.py:318
  59.7 1.6 %collective-permute-done.1.m1_ref = f32[128,256]{1,0:T(8,128)S(1)} collective-permute-done((f32[128,256]{1,0:T(8,128)S(1)}, f32[128,256]{1,0:T(8,128)S(1)}, u32[]{:S(2)}, u32[]{:S(2)}) %collective-permute-start.1) | collective-permute-done | bytes 131104 | tf_op jit(solution)/shard_map/ppermute | solution.py:318
  61.3 1.7 %collective-permute-done.2.m2_ref = f32[128,256]{1,0:T(8,128)S(1)} collective-permute-done((f32[128,256]{1,0:T(8,128)S(1)}, f32[128,256]{1,0:T(8,128)S(1)}, u32[]{:S(2)}, u32[]{:S(2)}) %collective-permute-start.2) | collective-permute-done | bytes 131104 | tf_op jit(solution)/shard_map/ppermute | solution.py:318
  67.1 2.8 %collective-permute-done.4.m3_ref = f32[128,256]{1,0:T(8,128)S(1)} collective-permute-done((f32[128,256]{1,0:T(8,128)S(1)}, f32[128,256]{1,0:T(8,128)S(1)}, u32[]{:S(2)}, u32[]{:S(2)}) %collective-permute-start.4) | collective-permute-done | bytes 131104 | tf_op jit(solution)/shard_map/ppermute | solution.py:318
  69.9 2.4 %collective-permute-done.5.m2_ref = f32[128,256]{1,0:T(8,128)S(1)} collective-permute-done((f32[128,256]{1,0:T(8,128)S(1)}, f32[128,256]{1,0:T(8,128)S(1)}, u32[]{:S(2)}, u32[]{:S(2)}) %collective-permute-start.5) | collective-permute-done | bytes 131104 | tf_op jit(solution)/shard_map/ppermute | solution.py:318
  72.3 1.3 collective-permute-done.6.m1_ref
  74.8 1.4 %collective-permute-start.7 = (f32[128,128]{1,0:T(8,128)S(1)}, f32[128,128]{1,0:T(8,128)S(1)}, u32[]{:S(2)}, u32[]{:S(2)}) collective-permute-start(f32[128,128]{1,0:T(8,128)S(1)} %get-tuple-element.47), channel_id=1, source_target_pairs={{0,8},{8,16},{16,24},{24,0},{1,9},{9,17},{17,25},{25,1},{2,10},{10... | collective-permute-start | bytes 196616 | tf_op jit(solution)/shard_map/ppermute | solution.py:318
  76.1 2.9 %collective-permute-start.8 = (f32[128,128]{1,0:T(8,128)S(1)}, f32[128,128]{1,0:T(8,128)S(1)}, u32[]{:S(2)}, u32[]{:S(2)}) collective-permute-start(f32[128,128]{1,0:T(8,128)S(1)} %get-tuple-element.48), channel_id=1, source_target_pairs={{0,16},{8,24},{16,0},{24,8},{1,17},{9,25},{17,1},{25,9},{2,18},{10... | collective-permute-start | bytes 196616 | tf_op jit(solution)/shard_map/ppermute | solution.py:318
  80.5 1.5 %collective-permute-done.8.s2_ref = f32[128,128]{1,0:T(8,128)S(1)} collective-permute-done((f32[128,128]{1,0:T(8,128)S(1)}, f32[128,128]{1,0:T(8,128)S(1)}, u32[]{:S(2)}, u32[]{:S(2)}) %collective-permute-start.8) | collective-permute-done | bytes 65568 | tf_op jit(solution)/shard_map/ppermute | solution.py:318
  82.0 1.3 collective-permute-done.9.s3_ref
  84.0 3.3 %local_reads.2 = (bf16[4,256,128]{2,1,0:T(8,128)(2,1)S(1)}, bf16[4,256,128]{2,1,0:T(8,128)(2,1)S(1)}, f32[4,256,128]{2,1,0:T(8,128)S(1)}) custom-call(s32[4]{0:T(128)S(1)} %pad_add_fusion.w_ref, bf16[256,1024]{1,0:T(8,128)(2,1)} %q_ref.3, bf16[256,1024]{1,0:T(8,128)(2,1)} %k_ref.7, bf16[4,256,256]{2,1,0:T(8,128)(2,1)S(1)} %get-tuple-element.32.xh_ref, ...), custom_call_target="tpu_custom_call" | custom-call | tf_op jit(solution)/shard_map/local_reads/pallas_call | solution.py:233
  87.3 3.3 %local_reads.3 = (bf16[4,256,128]{2,1,0:T(8,128)(2,1)S(1)}, bf16[4,256,128]{2,1,0:T(8,128)(2,1)S(1)}, f32[4,256,128]{2,1,0:T(8,128)S(1)}) custom-call(s32[4]{0:T(128)S(1)} %pad_add_fusion.w_ref, bf16[256,1024]{1,0:T(8,128)(2,1)} %q_ref.3, bf16[256,1024]{1,0:T(8,128)(2,1)} %k_ref.7, bf16[4,256,256]{2,1,0:T(8,128)(2,1)S(1)} %get-tuple-element.50.xh_ref, ...), custom_call_target="tpu_custom_call" | custom-call | tf_op jit(solution)/shard_map/local_reads/pallas_call | solution.py:233
  92.7 3.3 %collective-permute-start.17 = (bf16[256,512]{1,0:T(8,128)(2,1)S(1)}, bf16[256,512]{1,0:T(8,128)(2,1)S(1)}, u32[]{:S(2)}, u32[]{:S(2)}) collective-permute-start(bf16[256,512]{1,0:T(8,128)(2,1)S(1)} %shard_map.82.refs_1_), channel_id=1, source_target_pairs={{0,96},{32,0},{64,32},{96,64},{1,97},{33,1},{65,33},{97,65},{2,98}... | collective-permute-start | bytes 786440 | tf_op jit(solution)/shard_map/ppermute | solution.py:318
  96.0 1.9 %collective-permute-start.19 = (bf16[256,512]{1,0:T(8,128)(2,1)S(1)}, bf16[256,512]{1,0:T(8,128)(2,1)S(1)}, u32[]{:S(2)}, u32[]{:S(2)}) collective-permute-start(bf16[256,512]{1,0:T(8,128)(2,1)S(1)} %shard_map.82.refs_1_), channel_id=1, source_target_pairs={{0,32},{32,64},{64,96},{96,0},{1,33},{33,65},{65,97},{97,1},{2,34}... | collective-permute-start | bytes 786440 | tf_op jit(solution)/shard_map/ppermute | solution.py:318
  98.0 2.8 %collective-permute-done.15.refs_2_ = bf16[256,512]{1,0:T(8,128)(2,1)S(1)} collective-permute-done((bf16[256,512]{1,0:T(8,128)(2,1)S(1)}, bf16[256,512]{1,0:T(8,128)(2,1)S(1)}, u32[]{:S(2)}, u32[]{:S(2)}) %collective-permute-start.15) | collective-permute-done | bytes 262176 | tf_op jit(solution)/shard_map/ppermute | solution.py:318
  101.6 3.7 %collective-permute-start.18 = (bf16[256,512]{1,0:T(8,128)(2,1)S(1)}, bf16[256,512]{1,0:T(8,128)(2,1)S(1)}, u32[]{:S(2)}, u32[]{:S(2)}) collective-permute-start(bf16[256,512]{1,0:T(8,128)(2,1)S(1)} %collective-permute-done.17.refs_5_), channel_id=1, source_target_pairs={{0,96},{32,0},{64,32},{96,64},{1,97},{33,1},{65,33},{97,65},{2,98}... | collective-permute-start | bytes 786440 | tf_op jit(solution)/shard_map/ppermute | solution.py:318
  105.5 1.7 %collective-permute-done.20.refs_4_ = bf16[256,512]{1,0:T(8,128)(2,1)S(1)} collective-permute-done((bf16[256,512]{1,0:T(8,128)(2,1)S(1)}, bf16[256,512]{1,0:T(8,128)(2,1)S(1)}, u32[]{:S(2)}, u32[]{:S(2)}) %collective-permute-start.20) | collective-permute-done | bytes 262176 | tf_op jit(solution)/shard_map/ppermute | solution.py:318
  107.2 2.4 %shard_map.83 = (f32[512,1024]{1,0:T(8,128)S(1)}, f32[512,1024]{1,0:T(8,128)S(1)}) custom-call(s32[4]{0:T(128)S(1)} %pad_add_fusion.w_ref, bf16[4,256,1024]{2,1,0:T(8,128)(2,1)S(1)} %pad_maximum_fusion.cot_ref, bf16[256,512]{1,0:T(8,128)(2,1)S(1)} %shard_map.81.refs_0_, bf16[256,512]{1,0:T(8,128)(2,1)S(1)} %shard_map.82.refs_1_, ...), custom_call_target="tpu_custom_call" | custom-call | tf_op jit(solution)/shard_map/pallas_call | solution.py:253
  109.6 2.4 %collective-permute-done.16.b_ref = bf16[256,512]{1,0:T(8,128)(2,1)S(1)} collective-permute-done((bf16[256,512]{1,0:T(8,128)(2,1)S(1)}, bf16[256,512]{1,0:T(8,128)(2,1)S(1)}, u32[]{:S(2)}, u32[]{:S(2)}) %collective-permute-start.16) | collective-permute-done | bytes 262176 | tf_op jit(solution)/shard_map/ppermute | solution.py:318
  118.1 2.1 %collective-permute-start.24 = (bf16[256,512]{1,0:T(8,128)(2,1)S(1)}, bf16[256,512]{1,0:T(8,128)(2,1)S(1)}, u32[]{:S(2)}, u32[]{:S(2)}) collective-permute-start(bf16[256,512]{1,0:T(8,128)(2,1)S(1)} %get-tuple-element.61), channel_id=1, source_target_pairs={{0,24},{8,16},{16,8},{24,0},{1,25},{9,17},{17,9},{25,1},{2,26},{10... | collective-permute-start | bytes 786440 | tf_op jit(solution)/shard_map/ppermute | solution.py:323
  120.2 7.8 %collective-permute-done.24.r_a_ref = bf16[256,512]{1,0:T(8,128)(2,1)S(1)} collective-permute-done((bf16[256,512]{1,0:T(8,128)(2,1)S(1)}, bf16[256,512]{1,0:T(8,128)(2,1)S(1)}, u32[]{:S(2)}, u32[]{:S(2)}) %collective-permute-start.24) | collective-permute-done | bytes 262176 | tf_op jit(solution)/shard_map/ppermute | solution.py:323
  128.5 1.7 %collective-permute-start.23 = (bf16[128,512]{1,0:T(8,128)(2,1)S(1)}, bf16[128,512]{1,0:T(8,128)(2,1)S(1)}, u32[]{:S(2)}, u32[]{:S(2)}) collective-permute-start(bf16[128,512]{1,0:T(8,128)(2,1)S(1)} %add_convert_fusion.1), channel_id=1, source_target_pairs={{0,24},{8,16},{16,8},{24,0},{1,25},{9,17},{17,9},{25,1},{2,26},{10... | collective-permute-start | bytes 393224 | tf_op jit(solution)/shard_map/ppermute | solution.py:323
  131.2 1.9 %collective-permute-done.25.e_a_ref = bf16[128,512]{1,0:T(8,128)(2,1)S(1)} collective-permute-done((bf16[128,512]{1,0:T(8,128)(2,1)S(1)}, bf16[128,512]{1,0:T(8,128)(2,1)S(1)}, u32[]{:S(2)}, u32[]{:S(2)}) %collective-permute-start.25) | collective-permute-done | bytes 131104 | tf_op jit(solution)/shard_map/ppermute | solution.py:323
  133.0 1.7 %collective-permute-done.23.e_b_ref = bf16[128,512]{1,0:T(8,128)(2,1)S(1)} collective-permute-done((bf16[128,512]{1,0:T(8,128)(2,1)S(1)}, bf16[128,512]{1,0:T(8,128)(2,1)S(1)}, u32[]{:S(2)}, u32[]{:S(2)}) %collective-permute-start.23) | collective-permute-done | bytes 131104 | tf_op jit(solution)/shard_map/ppermute | solution.py:323
  134.8 1.4 %shard_map.87 = f32[128,1024]{1,0:T(8,128)} custom-call(s32[4]{0:T(128)S(1)} %pad_add_fusion.w_ref, f32[256,512]{1,0:T(8,128)S(1)} %get-tuple-element.58.k_b_ref, bf16[256,512]{1,0:T(8,128)(2,1)S(1)} %collective-permute-done.22.r_b_ref, bf16[128,512]{1,0:T(8,128)(2,1)S(1)} %collective-permute-done.23.e_b_ref, f32[256,512]{1,0:T(8,128)S(1)} %get-tuple-element.60.k_a_ref, ...), custom_call_target="tpu_custom_call" | custom-call | tf_op jit(solution)/shard_map/pallas_call | solution.py:253
  (43 shorter events, 20.0 us)
Async XLA Ops:
  0.6 1.7 %collective-permute-start.12 = (bf16[256,1024]{1,0:T(8,128)(2,1)}, bf16[256,1024]{1,0:T(8,128)(2,1)S(1)}, u32[]{:S(2)}, u32[]{:S(2)}) collective-permute-start(bf16[256,1024]{1,0:T(8,128)(2,1)} %param.11), channel_id=1, source_target_pairs={{0,0},{1,32},{2,64},{3,96},{32,1},{33,33},{34,65},{35,97},{64,2},{... | collective-permute-start | bytes 1572872 | tf_op jit(solution)/shard_map/ppermute | solution.py:330
  2.3 36.8 %collective-permute-start.13 = (bf16[256,1024]{1,0:T(8,128)(2,1)S(1)}, bf16[256,1024]{1,0:T(8,128)(2,1)S(1)}, u32[]{:S(2)}, u32[]{:S(2)}) collective-permute-start(bf16[256,1024]{1,0:T(8,128)(2,1)S(1)} %collective-permute-done.12), channel_id=1, source_target_pairs={{0,1},{1,0},{2,3},{3,2},{4,5},{5,4},{6,7},{7,6},{8,9},{9,8},{10,11... | collective-permute-start | bytes 1572872 | tf_op jit(solution)/shard_map/ppermute | solution.py:323
  33.9 18.3 %collective-permute-start = (f32[4,128,256]{2,1,0:T(8,128)S(1)}, f32[4,128,256]{2,1,0:T(8,128)S(1)}, u32[]{:S(2)}, u32[]{:S(2)}) collective-permute-start(f32[4,128,256]{2,1,0:T(8,128)S(1)} %get-tuple-element.35), channel_id=1, source_target_pairs={{0,4},{4,0},{1,5},{5,1},{2,6},{6,2},{3,7},{7,3},{8,12},{12,8},{9,1... | collective-permute-start | bytes 1572872 | tf_op jit(solution)/shard_map/ppermute | solution.py:323
  39.2 66.1 %collective-permute-start.14 = (bf16[2,256,1024]{2,1,0:T(8,128)(2,1)S(1)}, bf16[2,256,1024]{2,1,0:T(8,128)(2,1)S(1)}, u32[]{:S(2)}, u32[]{:S(2)}) collective-permute-start(bf16[2,256,1024]{2,1,0:T(8,128)(2,1)S(1)} %pad_maximum_fusion.1), channel_id=1, source_target_pairs={{0,3},{1,2},{2,1},{3,0},{4,7},{5,6},{6,5},{7,4},{8,11},{9,10},{10,... | collective-permute-start | bytes 3145736 | tf_op jit(solution)/shard_map/ppermute | solution.py:323
  53.1 8.2 %collective-permute-start.1 = (f32[128,256]{1,0:T(8,128)S(1)}, f32[128,256]{1,0:T(8,128)S(1)}, u32[]{:S(2)}, u32[]{:S(2)}) collective-permute-start(f32[128,256]{1,0:T(8,128)S(1)} %get-tuple-element.41), channel_id=1, source_target_pairs={{0,8},{8,16},{16,24},{24,0},{1,9},{9,17},{17,25},{25,1},{2,10},{10... | collective-permute-start | bytes 393224 | tf_op jit(solution)/shard_map/ppermute | solution.py:318
  55.1 7.9 %collective-permute-start.2 = (f32[128,256]{1,0:T(8,128)S(1)}, f32[128,256]{1,0:T(8,128)S(1)}, u32[]{:S(2)}, u32[]{:S(2)}) collective-permute-start(f32[128,256]{1,0:T(8,128)S(1)} %get-tuple-element.42), channel_id=1, source_target_pairs={{0,16},{8,24},{16,0},{24,8},{1,17},{9,25},{17,1},{25,9},{2,18},{10... | collective-permute-start | bytes 393224 | tf_op jit(solution)/shard_map/ppermute | solution.py:318
  58.7 5.0 %collective-permute-start.3 = (f32[128,256]{1,0:T(8,128)S(1)}, f32[128,256]{1,0:T(8,128)S(1)}, u32[]{:S(2)}, u32[]{:S(2)}) collective-permute-start(f32[128,256]{1,0:T(8,128)S(1)} %get-tuple-element.43), channel_id=1, source_target_pairs={{0,24},{8,0},{16,8},{24,16},{1,25},{9,1},{17,9},{25,17},{2,26},{10... | collective-permute-start | bytes 393224 | tf_op jit(solution)/shard_map/ppermute | solution.py:318
  59.7 27.6 %collective-permute-start.10 = (f32[4,128,256]{2,1,0:T(8,128)S(1)}, f32[4,128,256]{2,1,0:T(8,128)S(1)}, u32[]{:S(2)}, u32[]{:S(2)}) collective-permute-start(f32[4,128,256]{2,1,0:T(8,128)S(1)} %get-tuple-element.39.own_ref), channel_id=1, source_target_pairs={{0,4},{4,0},{1,5},{5,1},{2,6},{6,2},{3,7},{7,3},{8,12},{12,8},{9,1... | collective-permute-start | bytes 1572872 | tf_op jit(solution)/shard_map/ppermute | solution.py:323
  64.8 5.0 %collective-permute-start.4 = (f32[128,256]{1,0:T(8,128)S(1)}, f32[128,256]{1,0:T(8,128)S(1)}, u32[]{:S(2)}, u32[]{:S(2)}) collective-permute-start(f32[128,256]{1,0:T(8,128)S(1)} %get-tuple-element.44), channel_id=1, source_target_pairs={{0,96},{32,0},{64,32},{96,64},{1,97},{33,1},{65,33},{97,65},{2,98}... | collective-permute-start | bytes 393224 | tf_op jit(solution)/shard_map/ppermute | solution.py:318
  65.7 6.6 %collective-permute-start.5 = (f32[128,256]{1,0:T(8,128)S(1)}, f32[128,256]{1,0:T(8,128)S(1)}, u32[]{:S(2)}, u32[]{:S(2)}) collective-permute-start(f32[128,256]{1,0:T(8,128)S(1)} %get-tuple-element.44), channel_id=1, source_target_pairs={{0,64},{32,96},{64,0},{96,32},{1,65},{33,97},{65,1},{97,33},{2,66}... | collective-permute-start | bytes 393224 | tf_op jit(solution)/shard_map/ppermute | solution.py:318
  65.8 7.9 %collective-permute-start.6 = (f32[128,256]{1,0:T(8,128)S(1)}, f32[128,256]{1,0:T(8,128)S(1)}, u32[]{:S(2)}, u32[]{:S(2)}) collective-permute-start(f32[128,256]{1,0:T(8,128)S(1)} %get-tuple-element.44), channel_id=1, source_target_pairs={{0,32},{32,64},{64,96},{96,0},{1,33},{33,65},{65,97},{97,1},{2,34}... | collective-permute-start | bytes 393224 | tf_op jit(solution)/shard_map/ppermute | solution.py:318
  74.8 5.7 %collective-permute-start.7 = (f32[128,128]{1,0:T(8,128)S(1)}, f32[128,128]{1,0:T(8,128)S(1)}, u32[]{:S(2)}, u32[]{:S(2)}) collective-permute-start(f32[128,128]{1,0:T(8,128)S(1)} %get-tuple-element.47), channel_id=1, source_target_pairs={{0,8},{8,16},{16,24},{24,0},{1,9},{9,17},{17,25},{25,1},{2,10},{10... | collective-permute-start | bytes 196616 | tf_op jit(solution)/shard_map/ppermute | solution.py:318
  76.1 5.8 %collective-permute-start.8 = (f32[128,128]{1,0:T(8,128)S(1)}, f32[128,128]{1,0:T(8,128)S(1)}, u32[]{:S(2)}, u32[]{:S(2)}) collective-permute-start(f32[128,128]{1,0:T(8,128)S(1)} %get-tuple-element.48), channel_id=1, source_target_pairs={{0,16},{8,24},{16,0},{24,8},{1,17},{9,25},{17,1},{25,9},{2,18},{10... | collective-permute-start | bytes 196616 | tf_op jit(solution)/shard_map/ppermute | solution.py:318
  79.0 4.3 %collective-permute-start.9 = (f32[128,128]{1,0:T(8,128)S(1)}, f32[128,128]{1,0:T(8,128)S(1)}, u32[]{:S(2)}, u32[]{:S(2)}) collective-permute-start(f32[128,128]{1,0:T(8,128)S(1)} %get-tuple-element.49), channel_id=1, source_target_pairs={{0,24},{8,0},{16,8},{24,16},{1,25},{9,1},{17,9},{25,17},{2,26},{10... | collective-permute-start | bytes 196616 | tf_op jit(solution)/shard_map/ppermute | solution.py:318
  83.9 7.8 %collective-permute-start.11 = (f32[4,128,128]{2,1,0:T(8,128)S(1)}, f32[4,128,128]{2,1,0:T(8,128)S(1)}, u32[]{:S(2)}, u32[]{:S(2)}) collective-permute-start(f32[4,128,128]{2,1,0:T(8,128)S(1)} %shard_map.80.s_ref), channel_id=1, source_target_pairs={{0,4},{4,0},{1,5},{5,1},{2,6},{6,2},{3,7},{7,3},{8,12},{12,8},{9,1... | collective-permute-start | bytes 786440 | tf_op jit(solution)/shard_map/ppermute | solution.py:323
  84.0 6.7 %copy-start = (f32[128]{0:T(128)S(1)}, f32[128]{0:T(128)}, u32[]{:S(2)}) copy-start(f32[128]{0:T(128)} %param.10) | copy-start | bytes 1540
  91.6 9.2 %collective-permute-start.15 = (bf16[256,512]{1,0:T(8,128)(2,1)S(1)}, bf16[256,512]{1,0:T(8,128)(2,1)S(1)}, u32[]{:S(2)}, u32[]{:S(2)}) collective-permute-start(bf16[256,512]{1,0:T(8,128)(2,1)S(1)} %shard_map.81.refs_0_), channel_id=1, source_target_pairs={{0,32},{32,64},{64,96},{96,0},{1,33},{33,65},{65,97},{97,1},{2,34}... | collective-permute-start | bytes 786440 | tf_op jit(solution)/shard_map/ppermute | solution.py:318
  92.7 9.0 %collective-permute-start.17 = (bf16[256,512]{1,0:T(8,128)(2,1)S(1)}, bf16[256,512]{1,0:T(8,128)(2,1)S(1)}, u32[]{:S(2)}, u32[]{:S(2)}) collective-permute-start(bf16[256,512]{1,0:T(8,128)(2,1)S(1)} %shard_map.82.refs_1_), channel_id=1, source_target_pairs={{0,96},{32,0},{64,32},{96,64},{1,97},{33,1},{65,33},{97,65},{2,98}... | collective-permute-start | bytes 786440 | tf_op jit(solution)/shard_map/ppermute | solution.py:318
  95.9 11.3 %collective-permute-start.20 = (bf16[256,512]{1,0:T(8,128)(2,1)S(1)}, bf16[256,512]{1,0:T(8,128)(2,1)S(1)}, u32[]{:S(2)}, u32[]{:S(2)}) collective-permute-start(bf16[256,512]{1,0:T(8,128)(2,1)S(1)} %shard_map.81.refs_0_), channel_id=1, source_target_pairs={{0,96},{32,0},{64,32},{96,64},{1,97},{33,1},{65,33},{97,65},{2,98}... | collective-permute-start | bytes 786440 | tf_op jit(solution)/shard_map/ppermute | solution.py:318
  96.0 11.2 %collective-permute-start.19 = (bf16[256,512]{1,0:T(8,128)(2,1)S(1)}, bf16[256,512]{1,0:T(8,128)(2,1)S(1)}, u32[]{:S(2)}, u32[]{:S(2)}) collective-permute-start(bf16[256,512]{1,0:T(8,128)(2,1)S(1)} %shard_map.82.refs_1_), channel_id=1, source_target_pairs={{0,32},{32,64},{64,96},{96,0},{1,33},{33,65},{65,97},{97,1},{2,34}... | collective-permute-start | bytes 786440 | tf_op jit(solution)/shard_map/ppermute | solution.py:318
  100.8 11.2 %collective-permute-start.16 = (bf16[256,512]{1,0:T(8,128)(2,1)S(1)}, bf16[256,512]{1,0:T(8,128)(2,1)S(1)}, u32[]{:S(2)}, u32[]{:S(2)}) collective-permute-start(bf16[256,512]{1,0:T(8,128)(2,1)S(1)} %collective-permute-done.15.refs_2_), channel_id=1, source_target_pairs={{0,32},{32,64},{64,96},{96,0},{1,33},{33,65},{65,97},{97,1},{2,34}... | collective-permute-start | bytes 786440 | tf_op jit(solution)/shard_map/ppermute | solution.py:318
  101.6 11.2 %collective-permute-start.18 = (bf16[256,512]{1,0:T(8,128)(2,1)S(1)}, bf16[256,512]{1,0:T(8,128)(2,1)S(1)}, u32[]{:S(2)}, u32[]{:S(2)}) collective-permute-start(bf16[256,512]{1,0:T(8,128)(2,1)S(1)} %collective-permute-done.17.refs_5_), channel_id=1, source_target_pairs={{0,96},{32,0},{64,32},{96,64},{1,97},{33,1},{65,33},{97,65},{2,98}... | collective-permute-start | bytes 786440 | tf_op jit(solution)/shard_map/ppermute | solution.py:318
  113.9 3.5 %collective-permute-start.21 = (bf16[512,1024]{1,0:T(8,128)(2,1)S(1)}, bf16[512,1024]{1,0:T(8,128)(2,1)S(1)}, u32[]{:S(2)}, u32[]{:S(2)}) collective-permute-start(bf16[512,1024]{1,0:T(8,128)(2,1)S(1)} %shard_map.85), channel_id=1, source_target_pairs={{0,4},{4,0},{1,5},{5,1},{2,6},{6,2},{3,7},{7,3},{8,12},{12,8},{9,1... | collective-permute-start | bytes 3145736 | tf_op jit(solution)/shard_map/ppermute | solution.py:323
  118.1 9.9 %collective-permute-start.24 = (bf16[256,512]{1,0:T(8,128)(2,1)S(1)}, bf16[256,512]{1,0:T(8,128)(2,1)S(1)}, u32[]{:S(2)}, u32[]{:S(2)}) collective-permute-start(bf16[256,512]{1,0:T(8,128)(2,1)S(1)} %get-tuple-element.61), channel_id=1, source_target_pairs={{0,24},{8,16},{16,8},{24,0},{1,25},{9,17},{17,9},{25,1},{2,26},{10... | collective-permute-start | bytes 786440 | tf_op jit(solution)/shard_map/ppermute | solution.py:323
  120.2 8.3 %collective-permute-start.22 = (bf16[256,512]{1,0:T(8,128)(2,1)S(1)}, bf16[256,512]{1,0:T(8,128)(2,1)S(1)}, u32[]{:S(2)}, u32[]{:S(2)}) collective-permute-start(bf16[256,512]{1,0:T(8,128)(2,1)S(1)} %get-tuple-element.59), channel_id=1, source_target_pairs={{0,8},{8,0},{16,24},{24,16},{1,9},{9,1},{17,25},{25,17},{2,10},{10... | collective-permute-start | bytes 786440 | tf_op jit(solution)/shard_map/ppermute | solution.py:323
  128.0 5.0 %collective-permute-start.25 = (bf16[128,512]{1,0:T(8,128)(2,1)S(1)}, bf16[128,512]{1,0:T(8,128)(2,1)S(1)}, u32[]{:S(2)}, u32[]{:S(2)}) collective-permute-start(bf16[128,512]{1,0:T(8,128)(2,1)S(1)} %add_convert_fusion), channel_id=1, source_target_pairs={{0,8},{8,0},{16,24},{24,16},{1,9},{9,1},{17,25},{25,17},{2,10},{10... | collective-permute-start | bytes 393224 | tf_op jit(solution)/shard_map/ppermute | solution.py:323
  128.5 6.3 %collective-permute-start.23 = (bf16[128,512]{1,0:T(8,128)(2,1)S(1)}, bf16[128,512]{1,0:T(8,128)(2,1)S(1)}, u32[]{:S(2)}, u32[]{:S(2)}) collective-permute-start(bf16[128,512]{1,0:T(8,128)(2,1)S(1)} %add_convert_fusion.1), channel_id=1, source_target_pairs={{0,24},{8,16},{16,8},{24,0},{1,25},{9,17},{17,9},{25,1},{2,26},{10... | collective-permute-start | bytes 393224 | tf_op jit(solution)/shard_map/ppermute | solution.py:323

commit v3 on v2

--- a/solution.py
+++ b/solution.py
@@ -375,7 +375,9 @@
     e_b = swap(h_b, "z", 3)
     h_a = (k_a[F:] + r_a[F:].astype(f32)).astype(bf16)
     e_a = swap(h_a, "z", 1)
-    grad, = stage(final_kernel, where, [jax.ShapeDtypeStruct((F, 8 * F), f32)], k_b, r_b, e_b, k_a, r_a, e_a)
+    g_b = k_b[:F] + r_b[:F].astype(f32) + e_b.astype(f32)
+    g_a = k_a[:F] + r_a[:F].astype(f32) + e_a.astype(f32)
+    grad = jnp.where(ci == 0, jnp.concatenate([g_b, g_a], axis=1), jnp.concatenate([g_a, g_b], axis=1))
     attended = jnp.where(ci == 0, jnp.concatenate([att_b, att_a], axis=1), jnp.concatenate([att_a, att_b], axis=1))
     return attended, grad
 
@@ -416,15 +418,6 @@
             ref[(i % 2) * F:(i % 2 + 1) * F, :] = total.astype(ref.dtype)
 
 
-def final_kernel(w_ref, k_b_ref, r_b_ref, e_b_ref, k_a_ref, r_a_ref, e_a_ref, out_ref):
-    c = w_ref[2]
-    g_b = k_b_ref[:F] + r_b_ref[:F].astype(f32) + e_b_ref[...].astype(f32)
-    g_a = k_a_ref[:F] + r_a_ref[:F].astype(f32) + e_a_ref[...].astype(f32)
-    h = 4 * F
-    out_ref[:, :h] = jnp.where(c == 0, g_b, g_a)
-    out_ref[:, h:] = jnp.where(c == 0, g_a, g_b)
-
-
 def solution(mesh):
     fine = Mesh(mesh.devices.reshape(4, 4, 2, 4), ("y", "z", "core", "head"))
     spec = P(("y", "z", "core"), "head")

time: 137 us -> 135 us (0.985)
  Pallas kernels: 29.7 us -> 28.3 us
  waiting for transfers between devices: 40.8 us -> 39.4 us
    pallas_call x11 -> x10, Pallas kernels: 12.2 us -> 10.8 us  [stage(): pl.pallas_call(kernel, in_specs=[pl.BlockSpec(memory_space=pltpu.SMEM)] +...]
  transfers between devices with their start and end apart: 26 -> 26, of which waited for: 20 -> 19; matrix products, arithmetic and copies ran while one was open for 1% -> 1% of each run, Pallas kernels for 19% -> 20%
where the time goes in v3:
time: 135 us
  starting transfers between devices  64 us (47%)
  waiting for transfers between devices  39.4 us (29%)
  Pallas kernels  28.3 us (21%)
  other arithmetic  2.29 us (2%)
    ppermute x10, starting transfers between devices, swap(): return lax.ppermute(x, axis, [(i, i ^ k) for i in range(n)])  39.4 us
    ppermute x15, starting transfers between devices, shift(): return lax.ppermute(x, axis, [(i, (i + k) % 4) for i in range(4)])  22.9 us
    ppermute x15, waiting for transfers between devices, shift(): return lax.ppermute(x, axis, [(i, (i + k) % 4) for i in range(4)])  22.6 us
    ppermute x10, waiting for transfers between devices, swap(): return lax.ppermute(x, axis, [(i, i ^ k) for i in range(n)])  16.8 us
    pallas_call x2, Pallas kernels, local_maps(): pl.pallas_call(functools.partial(local_kernel, mine), grid_spec=pltpu.Pre...  10.9 us
    pallas_call x10, Pallas kernels, stage(): pl.pallas_call(kernel, in_specs=[pl.BlockSpec(memory_space=pltpu.SMEM)] +...  10.8 us
    pallas_call x2, Pallas kernels, local_reads(): pl.pallas_call(reads_kernel, grid_spec=pltpu.PrefetchScalarGridSpec(num_s...  6.63 us
  transfers between devices with their start and end apart: 26, of which 19 were waited for; matrix products, arithmetic and copies ran while one was open for 1% of the time, Pallas kernels for 20%

profile of v3, /device:TPU:0, one launch (start us, length us, event | category | flops | bytes accessed | tf_op | source)
XLA Modules:
  0.0 134.8 jit_solution(3276056589259510762)
XLA Ops:
  0.6 1.7 %collective-permute-start.12 = (bf16[256,1024]{1,0:T(8,128)(2,1)}, bf16[256,1024]{1,0:T(8,128)(2,1)S(1)}, u32[]{:S(2)}, u32[]{:S(2)}) collective-permute-start(bf16[256,1024]{1,0:T(8,128)(2,1)} %param.11), channel_id=1, source_target_pairs={{0,0},{1,32},{2,64},{3,96},{32,1},{33,33},{34,65},{35,97},{64,2},{... | collective-permute-start | bytes 1572872 | tf_op jit(solution)/shard_map/ppermute | solution.py:330
  2.3 26.1 %collective-permute-start.13 = (bf16[256,1024]{1,0:T(8,128)(2,1)S(1)}, bf16[256,1024]{1,0:T(8,128)(2,1)S(1)}, u32[]{:S(2)}, u32[]{:S(2)}) collective-permute-start(bf16[256,1024]{1,0:T(8,128)(2,1)S(1)} %collective-permute-done.12), channel_id=1, source_target_pairs={{0,1},{1,0},{2,3},{3,2},{4,5},{5,4},{6,7},{7,6},{8,9},{9,8},{10,11... | collective-permute-start | bytes 1572872 | tf_op jit(solution)/shard_map/ppermute | solution.py:323
  28.5 5.4 %local_maps.3 = (f32[4,128,256]{2,1,0:T(8,128)S(1)}, bf16[4,256,256]{2,1,0:T(8,128)(2,1)S(1)}, bf16[4,256,256]{2,1,0:T(8,128)(2,1)S(1)}, f32[1,8,256]{2,1,0:T(8,128)S(1)}) custom-call(s32[4]{0:T(128)S(1)} %pad_add_fusion.w_ref, bf16[256,1024]{1,0:T(8,128)(2,1)} %k_ref.7, bf16[256,1024]{1,0:T(8,128)(2,1)} %v_ref.3, f32[8,256]{1,0:T(8,128)} %bitcast.14), custom_call_target="tpu_custom_call" | custom-call | tf_op jit(solution)/shard_map/local_maps/pallas_call | solution.py:181
  34.0 5.1 %collective-permute-done.13 = bf16[256,1024]{1,0:T(8,128)(2,1)S(1)} collective-permute-done((bf16[256,1024]{1,0:T(8,128)(2,1)S(1)}, bf16[256,1024]{1,0:T(8,128)(2,1)S(1)}, u32[]{:S(2)}, u32[]{:S(2)}) %collective-permute-start.13) | collective-permute-done | bytes 524320 | tf_op jit(solution)/shard_map/ppermute | solution.py:323
  39.2 7.6 %collective-permute-start.14 = (bf16[2,256,1024]{2,1,0:T(8,128)(2,1)S(1)}, bf16[2,256,1024]{2,1,0:T(8,128)(2,1)S(1)}, u32[]{:S(2)}, u32[]{:S(2)}) collective-permute-start(bf16[2,256,1024]{2,1,0:T(8,128)(2,1)S(1)} %pad_maximum_fusion.1), channel_id=1, source_target_pairs={{0,3},{1,2},{2,1},{3,0},{4,7},{5,6},{6,5},{7,4},{8,11},{9,10},{10,... | collective-permute-start | bytes 3145736 | tf_op jit(solution)/shard_map/ppermute | solution.py:323
  46.8 5.4 %local_maps.2 = (f32[4,128,256]{2,1,0:T(8,128)S(1)}, bf16[4,256,256]{2,1,0:T(8,128)(2,1)S(1)}, bf16[4,256,256]{2,1,0:T(8,128)(2,1)S(1)}, f32[1,8,256]{2,1,0:T(8,128)S(1)}) custom-call(s32[4]{0:T(128)S(1)} %pad_add_fusion.w_ref, bf16[256,1024]{1,0:T(8,128)(2,1)} %k_ref.7, bf16[256,1024]{1,0:T(8,128)(2,1)} %v_ref.3, f32[8,256]{1,0:T(8,128)} %bitcast.15), custom_call_target="tpu_custom_call" | custom-call | tf_op jit(solution)/shard_map/local_maps/pallas_call | solution.py:181
  53.1 2.0 %collective-permute-start.1 = (f32[128,256]{1,0:T(8,128)S(1)}, f32[128,256]{1,0:T(8,128)S(1)}, u32[]{:S(2)}, u32[]{:S(2)}) collective-permute-start(f32[128,256]{1,0:T(8,128)S(1)} %get-tuple-element.41), channel_id=1, source_target_pairs={{0,8},{8,16},{16,24},{24,0},{1,9},{9,17},{17,25},{25,1},{2,10},{10... | collective-permute-start | bytes 393224 | tf_op jit(solution)/shard_map/ppermute | solution.py:318
  55.1 3.6 %collective-permute-start.2 = (f32[128,256]{1,0:T(8,128)S(1)}, f32[128,256]{1,0:T(8,128)S(1)}, u32[]{:S(2)}, u32[]{:S(2)}) collective-permute-start(f32[128,256]{1,0:T(8,128)S(1)} %get-tuple-element.42), channel_id=1, source_target_pairs={{0,16},{8,24},{16,0},{24,8},{1,17},{9,25},{17,1},{25,9},{2,18},{10... | collective-permute-start | bytes 393224 | tf_op jit(solution)/shard_map/ppermute | solution.py:318
  59.7 1.6 %collective-permute-done.1.m1_ref = f32[128,256]{1,0:T(8,128)S(1)} collective-permute-done((f32[128,256]{1,0:T(8,128)S(1)}, f32[128,256]{1,0:T(8,128)S(1)}, u32[]{:S(2)}, u32[]{:S(2)}) %collective-permute-start.1) | collective-permute-done | bytes 131104 | tf_op jit(solution)/shard_map/ppermute | solution.py:318
  61.3 1.7 %collective-permute-done.2.m2_ref = f32[128,256]{1,0:T(8,128)S(1)} collective-permute-done((f32[128,256]{1,0:T(8,128)S(1)}, f32[128,256]{1,0:T(8,128)S(1)}, u32[]{:S(2)}, u32[]{:S(2)}) %collective-permute-start.2) | collective-permute-done | bytes 131104 | tf_op jit(solution)/shard_map/ppermute | solution.py:318
  65.8 1.3 collective-permute-start.6
  67.1 2.8 %collective-permute-done.4.m3_ref = f32[128,256]{1,0:T(8,128)S(1)} collective-permute-done((f32[128,256]{1,0:T(8,128)S(1)}, f32[128,256]{1,0:T(8,128)S(1)}, u32[]{:S(2)}, u32[]{:S(2)}) %collective-permute-start.4) | collective-permute-done | bytes 131104 | tf_op jit(solution)/shard_map/ppermute | solution.py:318
  69.9 2.4 %collective-permute-done.5.m2_ref = f32[128,256]{1,0:T(8,128)S(1)} collective-permute-done((f32[128,256]{1,0:T(8,128)S(1)}, f32[128,256]{1,0:T(8,128)S(1)}, u32[]{:S(2)}, u32[]{:S(2)}) %collective-permute-start.5) | collective-permute-done | bytes 131104 | tf_op jit(solution)/shard_map/ppermute | solution.py:318
  72.3 1.3 collective-permute-done.6.m1_ref
  74.8 1.4 %collective-permute-start.7 = (f32[128,128]{1,0:T(8,128)S(1)}, f32[128,128]{1,0:T(8,128)S(1)}, u32[]{:S(2)}, u32[]{:S(2)}) collective-permute-start(f32[128,128]{1,0:T(8,128)S(1)} %get-tuple-element.47), channel_id=1, source_target_pairs={{0,8},{8,16},{16,24},{24,0},{1,9},{9,17},{17,25},{25,1},{2,10},{10... | collective-permute-start | bytes 196616 | tf_op jit(solution)/shard_map/ppermute | solution.py:318
  76.1 2.9 %collective-permute-start.8 = (f32[128,128]{1,0:T(8,128)S(1)}, f32[128,128]{1,0:T(8,128)S(1)}, u32[]{:S(2)}, u32[]{:S(2)}) collective-permute-start(f32[128,128]{1,0:T(8,128)S(1)} %get-tuple-element.48), channel_id=1, source_target_pairs={{0,16},{8,24},{16,0},{24,8},{1,17},{9,25},{17,1},{25,9},{2,18},{10... | collective-permute-start | bytes 196616 | tf_op jit(solution)/shard_map/ppermute | solution.py:318
  80.5 1.5 %collective-permute-done.8.s2_ref = f32[128,128]{1,0:T(8,128)S(1)} collective-permute-done((f32[128,128]{1,0:T(8,128)S(1)}, f32[128,128]{1,0:T(8,128)S(1)}, u32[]{:S(2)}, u32[]{:S(2)}) %collective-permute-start.8) | collective-permute-done | bytes 65568 | tf_op jit(solution)/shard_map/ppermute | solution.py:318
  82.0 1.3 collective-permute-done.9.s3_ref
  84.0 3.3 %local_reads.2 = (bf16[4,256,128]{2,1,0:T(8,128)(2,1)S(1)}, bf16[4,256,128]{2,1,0:T(8,128)(2,1)S(1)}, f32[4,256,128]{2,1,0:T(8,128)S(1)}) custom-call(s32[4]{0:T(128)S(1)} %pad_add_fusion.w_ref, bf16[256,1024]{1,0:T(8,128)(2,1)} %q_ref.3, bf16[256,1024]{1,0:T(8,128)(2,1)} %k_ref.7, bf16[4,256,256]{2,1,0:T(8,128)(2,1)S(1)} %get-tuple-element.32.xh_ref, ...), custom_call_target="tpu_custom_call" | custom-call | tf_op jit(solution)/shard_map/local_reads/pallas_call | solution.py:233
  87.3 3.3 %local_reads.3 = (bf16[4,256,128]{2,1,0:T(8,128)(2,1)S(1)}, bf16[4,256,128]{2,1,0:T(8,128)(2,1)S(1)}, f32[4,256,128]{2,1,0:T(8,128)S(1)}) custom-call(s32[4]{0:T(128)S(1)} %pad_add_fusion.w_ref, bf16[256,1024]{1,0:T(8,128)(2,1)} %q_ref.3, bf16[256,1024]{1,0:T(8,128)(2,1)} %k_ref.7, bf16[4,256,256]{2,1,0:T(8,128)(2,1)S(1)} %get-tuple-element.50.xh_ref, ...), custom_call_target="tpu_custom_call" | custom-call | tf_op jit(solution)/shard_map/local_reads/pallas_call | solution.py:233
  92.7 3.3 %collective-permute-start.17 = (bf16[256,512]{1,0:T(8,128)(2,1)S(1)}, bf16[256,512]{1,0:T(8,128)(2,1)S(1)}, u32[]{:S(2)}, u32[]{:S(2)}) collective-permute-start(bf16[256,512]{1,0:T(8,128)(2,1)S(1)} %shard_map.82.refs_1_), channel_id=1, source_target_pairs={{0,96},{32,0},{64,32},{96,64},{1,97},{33,1},{65,33},{97,65},{2,98}... | collective-permute-start | bytes 786440 | tf_op jit(solution)/shard_map/ppermute | solution.py:318
  96.0 1.9 %collective-permute-start.19 = (bf16[256,512]{1,0:T(8,128)(2,1)S(1)}, bf16[256,512]{1,0:T(8,128)(2,1)S(1)}, u32[]{:S(2)}, u32[]{:S(2)}) collective-permute-start(bf16[256,512]{1,0:T(8,128)(2,1)S(1)} %shard_map.82.refs_1_), channel_id=1, source_target_pairs={{0,32},{32,64},{64,96},{96,0},{1,33},{33,65},{65,97},{97,1},{2,34}... | collective-permute-start | bytes 786440 | tf_op jit(solution)/shard_map/ppermute | solution.py:318
  98.0 2.8 %collective-permute-done.15.refs_2_ = bf16[256,512]{1,0:T(8,128)(2,1)S(1)} collective-permute-done((bf16[256,512]{1,0:T(8,128)(2,1)S(1)}, bf16[256,512]{1,0:T(8,128)(2,1)S(1)}, u32[]{:S(2)}, u32[]{:S(2)}) %collective-permute-start.15) | collective-permute-done | bytes 262176 | tf_op jit(solution)/shard_map/ppermute | solution.py:318
  101.6 3.7 %collective-permute-start.18 = (bf16[256,512]{1,0:T(8,128)(2,1)S(1)}, bf16[256,512]{1,0:T(8,128)(2,1)S(1)}, u32[]{:S(2)}, u32[]{:S(2)}) collective-permute-start(bf16[256,512]{1,0:T(8,128)(2,1)S(1)} %collective-permute-done.17.refs_5_), channel_id=1, source_target_pairs={{0,96},{32,0},{64,32},{96,64},{1,97},{33,1},{65,33},{97,65},{2,98}... | collective-permute-start | bytes 786440 | tf_op jit(solution)/shard_map/ppermute | solution.py:318
  105.5 1.7 %collective-permute-done.20.refs_4_ = bf16[256,512]{1,0:T(8,128)(2,1)S(1)} collective-permute-done((bf16[256,512]{1,0:T(8,128)(2,1)S(1)}, bf16[256,512]{1,0:T(8,128)(2,1)S(1)}, u32[]{:S(2)}, u32[]{:S(2)}) %collective-permute-start.20) | collective-permute-done | bytes 262176 | tf_op jit(solution)/shard_map/ppermute | solution.py:318
  107.2 2.4 %shard_map.83 = (f32[512,1024]{1,0:T(8,128)S(1)}, f32[512,1024]{1,0:T(8,128)S(1)}) custom-call(s32[4]{0:T(128)S(1)} %pad_add_fusion.w_ref, bf16[4,256,1024]{2,1,0:T(8,128)(2,1)S(1)} %pad_maximum_fusion.cot_ref, bf16[256,512]{1,0:T(8,128)(2,1)S(1)} %shard_map.81.refs_0_, bf16[256,512]{1,0:T(8,128)(2,1)S(1)} %shard_map.82.refs_1_, ...), custom_call_target="tpu_custom_call" | custom-call | tf_op jit(solution)/shard_map/pallas_call | solution.py:253
  109.6 2.4 %collective-permute-done.16.b_ref = bf16[256,512]{1,0:T(8,128)(2,1)S(1)} collective-permute-done((bf16[256,512]{1,0:T(8,128)(2,1)S(1)}, bf16[256,512]{1,0:T(8,128)(2,1)S(1)}, u32[]{:S(2)}, u32[]{:S(2)}) %collective-permute-start.16) | collective-permute-done | bytes 262176 | tf_op jit(solution)/shard_map/ppermute | solution.py:318
  116.1 1.3 collective-permute-done.21.got_ref
  118.5 1.8 %collective-permute-start.24 = (bf16[256,512]{1,0:T(8,128)(2,1)S(1)}, bf16[256,512]{1,0:T(8,128)(2,1)S(1)}, u32[]{:S(2)}, u32[]{:S(2)}) collective-permute-start(bf16[256,512]{1,0:T(8,128)(2,1)S(1)} %get-tuple-element.61), channel_id=1, source_target_pairs={{0,24},{8,16},{16,8},{24,0},{1,25},{9,17},{17,9},{25,1},{2,26},{10... | collective-permute-start | bytes 786440 | tf_op jit(solution)/shard_map/ppermute | solution.py:323
  121.2 5.6 %collective-permute-done.22 = bf16[256,512]{1,0:T(8,128)(2,1)S(1)} collective-permute-done((bf16[256,512]{1,0:T(8,128)(2,1)S(1)}, bf16[256,512]{1,0:T(8,128)(2,1)S(1)}, u32[]{:S(2)}, u32[]{:S(2)}) %collective-permute-start.22) | collective-permute-done | bytes 262176 | tf_op jit(solution)/shard_map/ppermute | solution.py:323
  126.8 2.1 %collective-permute-start.23 = (bf16[128,512]{1,0:T(8,128)(2,1)S(1)}, bf16[128,512]{1,0:T(8,128)(2,1)S(1)}, u32[]{:S(2)}, u32[]{:S(2)}) collective-permute-start(bf16[128,512]{1,0:T(8,128)(2,1)S(1)} %add_convert_fusion.1), channel_id=1, source_target_pairs={{0,24},{8,16},{16,8},{24,0},{1,25},{9,17},{17,9},{25,1},{2,26},{10... | collective-permute-start | bytes 393224 | tf_op jit(solution)/shard_map/ppermute | solution.py:323
  129.0 4.1 %collective-permute-done.23 = bf16[128,512]{1,0:T(8,128)(2,1)S(1)} collective-permute-done((bf16[128,512]{1,0:T(8,128)(2,1)S(1)}, bf16[128,512]{1,0:T(8,128)(2,1)S(1)}, u32[]{:S(2)}, u32[]{:S(2)}) %collective-permute-start.23) | collective-permute-done | bytes 131104 | tf_op jit(solution)/shard_map/ppermute | solution.py:323
  (45 shorter events, 19.2 us)
Async XLA Ops:
  0.6 1.7 %collective-permute-start.12 = (bf16[256,1024]{1,0:T(8,128)(2,1)}, bf16[256,1024]{1,0:T(8,128)(2,1)S(1)}, u32[]{:S(2)}, u32[]{:S(2)}) collective-permute-start(bf16[256,1024]{1,0:T(8,128)(2,1)} %param.11), channel_id=1, source_target_pairs={{0,0},{1,32},{2,64},{3,96},{32,1},{33,33},{34,65},{35,97},{64,2},{... | collective-permute-start | bytes 1572872 | tf_op jit(solution)/shard_map/ppermute | solution.py:330
  2.3 36.8 %collective-permute-start.13 = (bf16[256,1024]{1,0:T(8,128)(2,1)S(1)}, bf16[256,1024]{1,0:T(8,128)(2,1)S(1)}, u32[]{:S(2)}, u32[]{:S(2)}) collective-permute-start(bf16[256,1024]{1,0:T(8,128)(2,1)S(1)} %collective-permute-done.12), channel_id=1, source_target_pairs={{0,1},{1,0},{2,3},{3,2},{4,5},{5,4},{6,7},{7,6},{8,9},{9,8},{10,11... | collective-permute-start | bytes 1572872 | tf_op jit(solution)/shard_map/ppermute | solution.py:323
  33.9 18.3 %collective-permute-start = (f32[4,128,256]{2,1,0:T(8,128)S(1)}, f32[4,128,256]{2,1,0:T(8,128)S(1)}, u32[]{:S(2)}, u32[]{:S(2)}) collective-permute-start(f32[4,128,256]{2,1,0:T(8,128)S(1)} %get-tuple-element.35), channel_id=1, source_target_pairs={{0,4},{4,0},{1,5},{5,1},{2,6},{6,2},{3,7},{7,3},{8,12},{12,8},{9,1... | collective-permute-start | bytes 1572872 | tf_op jit(solution)/shard_map/ppermute | solution.py:323
  39.2 66.1 %collective-permute-start.14 = (bf16[2,256,1024]{2,1,0:T(8,128)(2,1)S(1)}, bf16[2,256,1024]{2,1,0:T(8,128)(2,1)S(1)}, u32[]{:S(2)}, u32[]{:S(2)}) collective-permute-start(bf16[2,256,1024]{2,1,0:T(8,128)(2,1)S(1)} %pad_maximum_fusion.1), channel_id=1, source_target_pairs={{0,3},{1,2},{2,1},{3,0},{4,7},{5,6},{6,5},{7,4},{8,11},{9,10},{10,... | collective-permute-start | bytes 3145736 | tf_op jit(solution)/shard_map/ppermute | solution.py:323
  53.1 8.2 %collective-permute-start.1 = (f32[128,256]{1,0:T(8,128)S(1)}, f32[128,256]{1,0:T(8,128)S(1)}, u32[]{:S(2)}, u32[]{:S(2)}) collective-permute-start(f32[128,256]{1,0:T(8,128)S(1)} %get-tuple-element.41), channel_id=1, source_target_pairs={{0,8},{8,16},{16,24},{24,0},{1,9},{9,17},{17,25},{25,1},{2,10},{10... | collective-permute-start | bytes 393224 | tf_op jit(solution)/shard_map/ppermute | solution.py:318
  55.1 7.9 %collective-permute-start.2 = (f32[128,256]{1,0:T(8,128)S(1)}, f32[128,256]{1,0:T(8,128)S(1)}, u32[]{:S(2)}, u32[]{:S(2)}) collective-permute-start(f32[128,256]{1,0:T(8,128)S(1)} %get-tuple-element.42), channel_id=1, source_target_pairs={{0,16},{8,24},{16,0},{24,8},{1,17},{9,25},{17,1},{25,9},{2,18},{10... | collective-permute-start | bytes 393224 | tf_op jit(solution)/shard_map/ppermute | solution.py:318
  58.7 5.0 %collective-permute-start.3 = (f32[128,256]{1,0:T(8,128)S(1)}, f32[128,256]{1,0:T(8,128)S(1)}, u32[]{:S(2)}, u32[]{:S(2)}) collective-permute-start(f32[128,256]{1,0:T(8,128)S(1)} %get-tuple-element.43), channel_id=1, source_target_pairs={{0,24},{8,0},{16,8},{24,16},{1,25},{9,1},{17,9},{25,17},{2,26},{10... | collective-permute-start | bytes 393224 | tf_op jit(solution)/shard_map/ppermute | solution.py:318
  59.7 27.6 %collective-permute-start.10 = (f32[4,128,256]{2,1,0:T(8,128)S(1)}, f32[4,128,256]{2,1,0:T(8,128)S(1)}, u32[]{:S(2)}, u32[]{:S(2)}) collective-permute-start(f32[4,128,256]{2,1,0:T(8,128)S(1)} %get-tuple-element.39.own_ref), channel_id=1, source_target_pairs={{0,4},{4,0},{1,5},{5,1},{2,6},{6,2},{3,7},{7,3},{8,12},{12,8},{9,1... | collective-permute-start | bytes 1572872 | tf_op jit(solution)/shard_map/ppermute | solution.py:323
  64.8 5.0 %collective-permute-start.4 = (f32[128,256]{1,0:T(8,128)S(1)}, f32[128,256]{1,0:T(8,128)S(1)}, u32[]{:S(2)}, u32[]{:S(2)}) collective-permute-start(f32[128,256]{1,0:T(8,128)S(1)} %get-tuple-element.44), channel_id=1, source_target_pairs={{0,96},{32,0},{64,32},{96,64},{1,97},{33,1},{65,33},{97,65},{2,98}... | collective-permute-start | bytes 393224 | tf_op jit(solution)/shard_map/ppermute | solution.py:318
  65.7 6.6 %collective-permute-start.5 = (f32[128,256]{1,0:T(8,128)S(1)}, f32[128,256]{1,0:T(8,128)S(1)}, u32[]{:S(2)}, u32[]{:S(2)}) collective-permute-start(f32[128,256]{1,0:T(8,128)S(1)} %get-tuple-element.44), channel_id=1, source_target_pairs={{0,64},{32,96},{64,0},{96,32},{1,65},{33,97},{65,1},{97,33},{2,66}... | collective-permute-start | bytes 393224 | tf_op jit(solution)/shard_map/ppermute | solution.py:318
  65.8 7.9 %collective-permute-start.6 = (f32[128,256]{1,0:T(8,128)S(1)}, f32[128,256]{1,0:T(8,128)S(1)}, u32[]{:S(2)}, u32[]{:S(2)}) collective-permute-start(f32[128,256]{1,0:T(8,128)S(1)} %get-tuple-element.44), channel_id=1, source_target_pairs={{0,32},{32,64},{64,96},{96,0},{1,33},{33,65},{65,97},{97,1},{2,34}... | collective-permute-start | bytes 393224 | tf_op jit(solution)/shard_map/ppermute | solution.py:318
  74.8 5.7 %collective-permute-start.7 = (f32[128,128]{1,0:T(8,128)S(1)}, f32[128,128]{1,0:T(8,128)S(1)}, u32[]{:S(2)}, u32[]{:S(2)}) collective-permute-start(f32[128,128]{1,0:T(8,128)S(1)} %get-tuple-element.47), channel_id=1, source_target_pairs={{0,8},{8,16},{16,24},{24,0},{1,9},{9,17},{17,25},{25,1},{2,10},{10... | collective-permute-start | bytes 196616 | tf_op jit(solution)/shard_map/ppermute | solution.py:318
  76.1 5.8 %collective-permute-start.8 = (f32[128,128]{1,0:T(8,128)S(1)}, f32[128,128]{1,0:T(8,128)S(1)}, u32[]{:S(2)}, u32[]{:S(2)}) collective-permute-start(f32[128,128]{1,0:T(8,128)S(1)} %get-tuple-element.48), channel_id=1, source_target_pairs={{0,16},{8,24},{16,0},{24,8},{1,17},{9,25},{17,1},{25,9},{2,18},{10... | collective-permute-start | bytes 196616 | tf_op jit(solution)/shard_map/ppermute | solution.py:318
  79.0 4.3 %collective-permute-start.9 = (f32[128,128]{1,0:T(8,128)S(1)}, f32[128,128]{1,0:T(8,128)S(1)}, u32[]{:S(2)}, u32[]{:S(2)}) collective-permute-start(f32[128,128]{1,0:T(8,128)S(1)} %get-tuple-element.49), channel_id=1, source_target_pairs={{0,24},{8,0},{16,8},{24,16},{1,25},{9,1},{17,9},{25,17},{2,26},{10... | collective-permute-start | bytes 196616 | tf_op jit(solution)/shard_map/ppermute | solution.py:318
  83.9 7.8 %collective-permute-start.11 = (f32[4,128,128]{2,1,0:T(8,128)S(1)}, f32[4,128,128]{2,1,0:T(8,128)S(1)}, u32[]{:S(2)}, u32[]{:S(2)}) collective-permute-start(f32[4,128,128]{2,1,0:T(8,128)S(1)} %shard_map.80.s_ref), channel_id=1, source_target_pairs={{0,4},{4,0},{1,5},{5,1},{2,6},{6,2},{3,7},{7,3},{8,12},{12,8},{9,1... | collective-permute-start | bytes 786440 | tf_op jit(solution)/shard_map/ppermute | solution.py:323
  84.0 6.7 %copy-start = (f32[128]{0:T(128)S(1)}, f32[128]{0:T(128)}, u32[]{:S(2)}) copy-start(f32[128]{0:T(128)} %param.10) | copy-start | bytes 1540
  91.6 9.2 %collective-permute-start.15 = (bf16[256,512]{1,0:T(8,128)(2,1)S(1)}, bf16[256,512]{1,0:T(8,128)(2,1)S(1)}, u32[]{:S(2)}, u32[]{:S(2)}) collective-permute-start(bf16[256,512]{1,0:T(8,128)(2,1)S(1)} %shard_map.81.refs_0_), channel_id=1, source_target_pairs={{0,32},{32,64},{64,96},{96,0},{1,33},{33,65},{65,97},{97,1},{2,34}... | collective-permute-start | bytes 786440 | tf_op jit(solution)/shard_map/ppermute | solution.py:318
  92.7 9.0 %collective-permute-start.17 = (bf16[256,512]{1,0:T(8,128)(2,1)S(1)}, bf16[256,512]{1,0:T(8,128)(2,1)S(1)}, u32[]{:S(2)}, u32[]{:S(2)}) collective-permute-start(bf16[256,512]{1,0:T(8,128)(2,1)S(1)} %shard_map.82.refs_1_), channel_id=1, source_target_pairs={{0,96},{32,0},{64,32},{96,64},{1,97},{33,1},{65,33},{97,65},{2,98}... | collective-permute-start | bytes 786440 | tf_op jit(solution)/shard_map/ppermute | solution.py:318
  95.9 11.3 %collective-permute-start.20 = (bf16[256,512]{1,0:T(8,128)(2,1)S(1)}, bf16[256,512]{1,0:T(8,128)(2,1)S(1)}, u32[]{:S(2)}, u32[]{:S(2)}) collective-permute-start(bf16[256,512]{1,0:T(8,128)(2,1)S(1)} %shard_map.81.refs_0_), channel_id=1, source_target_pairs={{0,96},{32,0},{64,32},{96,64},{1,97},{33,1},{65,33},{97,65},{2,98}... | collective-permute-start | bytes 786440 | tf_op jit(solution)/shard_map/ppermute | solution.py:318
  96.0 11.2 %collective-permute-start.19 = (bf16[256,512]{1,0:T(8,128)(2,1)S(1)}, bf16[256,512]{1,0:T(8,128)(2,1)S(1)}, u32[]{:S(2)}, u32[]{:S(2)}) collective-permute-start(bf16[256,512]{1,0:T(8,128)(2,1)S(1)} %shard_map.82.refs_1_), channel_id=1, source_target_pairs={{0,32},{32,64},{64,96},{96,0},{1,33},{33,65},{65,97},{97,1},{2,34}... | collective-permute-start | bytes 786440 | tf_op jit(solution)/shard_map/ppermute | solution.py:318
  100.8 11.2 %collective-permute-start.16 = (bf16[256,512]{1,0:T(8,128)(2,1)S(1)}, bf16[256,512]{1,0:T(8,128)(2,1)S(1)}, u32[]{:S(2)}, u32[]{:S(2)}) collective-permute-start(bf16[256,512]{1,0:T(8,128)(2,1)S(1)} %collective-permute-done.15.refs_2_), channel_id=1, source_target_pairs={{0,32},{32,64},{64,96},{96,0},{1,33},{33,65},{65,97},{97,1},{2,34}... | collective-permute-start | bytes 786440 | tf_op jit(solution)/shard_map/ppermute | solution.py:318
  101.6 11.2 %collective-permute-start.18 = (bf16[256,512]{1,0:T(8,128)(2,1)S(1)}, bf16[256,512]{1,0:T(8,128)(2,1)S(1)}, u32[]{:S(2)}, u32[]{:S(2)}) collective-permute-start(bf16[256,512]{1,0:T(8,128)(2,1)S(1)} %collective-permute-done.17.refs_5_), channel_id=1, source_target_pairs={{0,96},{32,0},{64,32},{96,64},{1,97},{33,1},{65,33},{97,65},{2,98}... | collective-permute-start | bytes 786440 | tf_op jit(solution)/shard_map/ppermute | solution.py:318
  113.9 3.5 %collective-permute-start.21 = (bf16[512,1024]{1,0:T(8,128)(2,1)S(1)}, bf16[512,1024]{1,0:T(8,128)(2,1)S(1)}, u32[]{:S(2)}, u32[]{:S(2)}) collective-permute-start(bf16[512,1024]{1,0:T(8,128)(2,1)S(1)} %shard_map.85), channel_id=1, source_target_pairs={{0,4},{4,0},{1,5},{5,1},{2,6},{6,2},{3,7},{7,3},{8,12},{12,8},{9,1... | collective-permute-start | bytes 3145736 | tf_op jit(solution)/shard_map/ppermute | solution.py:323
  118.1 8.7 %collective-permute-start.22 = (bf16[256,512]{1,0:T(8,128)(2,1)S(1)}, bf16[256,512]{1,0:T(8,128)(2,1)S(1)}, u32[]{:S(2)}, u32[]{:S(2)}) collective-permute-start(bf16[256,512]{1,0:T(8,128)(2,1)S(1)} %get-tuple-element.59), channel_id=1, source_target_pairs={{0,8},{8,0},{16,24},{24,16},{1,9},{9,1},{17,25},{25,17},{2,10},{10... | collective-permute-start | bytes 786440 | tf_op jit(solution)/shard_map/ppermute | solution.py:323
  118.5 10.4 %collective-permute-start.24 = (bf16[256,512]{1,0:T(8,128)(2,1)S(1)}, bf16[256,512]{1,0:T(8,128)(2,1)S(1)}, u32[]{:S(2)}, u32[]{:S(2)}) collective-permute-start(bf16[256,512]{1,0:T(8,128)(2,1)S(1)} %get-tuple-element.61), channel_id=1, source_target_pairs={{0,24},{8,16},{16,8},{24,0},{1,25},{9,17},{17,9},{25,1},{2,26},{10... | collective-permute-start | bytes 786440 | tf_op jit(solution)/shard_map/ppermute | solution.py:323
  126.8 6.3 %collective-permute-start.23 = (bf16[128,512]{1,0:T(8,128)(2,1)S(1)}, bf16[128,512]{1,0:T(8,128)(2,1)S(1)}, u32[]{:S(2)}, u32[]{:S(2)}) collective-permute-start(bf16[128,512]{1,0:T(8,128)(2,1)S(1)} %add_convert_fusion.1), channel_id=1, source_target_pairs={{0,24},{8,16},{16,8},{24,0},{1,25},{9,17},{17,9},{25,1},{2,26},{10... | collective-permute-start | bytes 393224 | tf_op jit(solution)/shard_map/ppermute | solution.py:323
  128.9 5.0 %collective-permute-start.25 = (bf16[128,512]{1,0:T(8,128)(2,1)S(1)}, bf16[128,512]{1,0:T(8,128)(2,1)S(1)}, u32[]{:S(2)}, u32[]{:S(2)}) collective-permute-start(bf16[128,512]{1,0:T(8,128)(2,1)S(1)} %add_convert_fusion), channel_id=1, source_target_pairs={{0,8},{8,0},{16,24},{24,16},{1,9},{9,1},{17,25},{25,17},{2,10},{10... | collective-permute-start | bytes 393224 | tf_op jit(solution)/shard_map/ppermute | solution.py:323

commit v4 on v3

--- a/solution.py
+++ b/solution.py
@@ -14,6 +14,7 @@
 EPS = 1e-06
 f32 = jnp.float32
 bf16 = jnp.bfloat16
+f16 = jnp.float16
 
 
 def split(x):
@@ -249,6 +250,17 @@
     return jnp.concatenate([o[:, :F], o[:, F:] + p_then[:, F:]], axis=1)
 
 
+SHRINK = 1.0 / 32.0
+
+
+def packed(m):
+    return jnp.concatenate([m[:, :F], m[:, F:] * SHRINK], axis=1)
+
+
+def unpacked(m):
+    return jnp.concatenate([m[:, :F], m[:, F:] * (1.0 / SHRINK)], axis=1)
+
+
 def stage(kernel, where, outs, *args, scratch=()):
     return pl.pallas_call(
         kernel,
@@ -266,20 +278,21 @@
         j = lax.rem(z + k, 4)
         own = own_ref[j]
         got = got_ref[j]
-        out_refs[k][...] = after(jnp.where(c == 0, got, own), jnp.where(c == 0, own, got))
+        m = after(jnp.where(c == 0, got, own), jnp.where(c == 0, own, got))
+        out_refs[k][...] = m if k == 0 else packed(m)
 
 
 def chain_kernel(w_ref, m0_ref, m1_ref, m2_ref, m3_ref, pre_ref, all_ref, maps_ref):
     z = w_ref[1]
     for k, ref in enumerate((m0_ref, m1_ref, m2_ref, m3_ref)):
-        maps_ref[lax.rem(z - k + 4, 4)] = ref[...]
+        maps_ref[lax.rem(z - k + 4, 4)] = ref[...] if k == 0 else unpacked(ref[...])
     m = maps_ref[0]
     pre_ref[0] = m
     for j in range(1, 4):
         m = after(maps_ref[j], m)
         if j < 3:
             pre_ref[j] = m
-    all_ref[...] = m
+    all_ref[...] = packed(m)
 
 
 def apply_map(m, s):
@@ -288,9 +301,9 @@
 
 def plane_kernel(w_ref, m3_ref, m2_ref, m1_ref, pre_ref, *out_refs):
     y, z = w_ref[0], w_ref[1]
-    s = jnp.where(y >= 3, m3_ref[:, F:], 0.0)
-    s = jnp.where(y >= 2, apply_map(m2_ref[...], s), 0.0)
-    s = jnp.where(y >= 1, apply_map(m1_ref[...], s), 0.0)
+    s = jnp.where(y >= 3, unpacked(m3_ref[...])[:, F:], 0.0)
+    s = jnp.where(y >= 2, apply_map(unpacked(m2_ref[...]), s), 0.0)
+    s = jnp.where(y >= 1, apply_map(unpacked(m1_ref[...]), s), 0.0)
     for k in range(4):
         j = lax.rem(z + k, 4)
         t = apply_map(pre_ref[jnp.maximum(j - 1, 0)], s)
@@ -340,13 +353,13 @@
     comb = stage(pair_kernel, where, [m4] * 4, m_b, got_b)
     got = [comb[0]]
     for k in (1, 2, 3):
-        got.append(shift(comb[k], "z", k))
+        got.append(shift(comb[k].astype(f16), "z", k).astype(f32))
     rd_b = local_reads(True, where, query_rows, key_rows, xh_b, xl_b, r_b, got_b)
     rd_a = local_reads(False, where, query_rows, key_rows, xh_a, xl_a, r_a, got_a)
     pre, total = stage(chain_kernel, where, [vmem((3, F, 2 * F)), m4], *got, scratch=[pltpu.VMEM((4, F, 2 * F), f32)])
     planes = []
     for k in (3, 2, 1):
-        planes.append(shift(total, "y", k))
+        planes.append(shift(total.astype(f16), "y", k).astype(f32))
     sc = stage(plane_kernel, where, [vmem((F, F))] * 4, *planes, pre)
     sx = [sc[0]]
     for k in (1, 2, 3):

time: 135 us -> 133 us (0.985)
  waiting for transfers between devices: 39.4 us -> 37.3 us
    ppermute x15, waiting for transfers between devices: 22.6 us -> 20.5 us  [shift(): return lax.ppermute(x, axis, [(i, (i + k) % 4) for i in range(4)])]
where the time goes in v4:
time: 133 us
  starting transfers between devices  63.9 us (48%)
  waiting for transfers between devices  37.3 us (28%)
  Pallas kernels  28.3 us (21%)
  other arithmetic  2.39 us (2%)
    ppermute x10, starting transfers between devices, swap(): return lax.ppermute(x, axis, [(i, i ^ k) for i in range(n)])  39.4 us
    ppermute x15, starting transfers between devices, shift(): return lax.ppermute(x, axis, [(i, (i + k) % 4) for i in range(4)])  22.7 us
    ppermute x15, waiting for transfers between devices, shift(): return lax.ppermute(x, axis, [(i, (i + k) % 4) for i in range(4)])  20.5 us
    ppermute x10, waiting for transfers between devices, swap(): return lax.ppermute(x, axis, [(i, i ^ k) for i in range(n)])  16.8 us
    pallas_call x2, Pallas kernels, local_maps(): pl.pallas_call(functools.partial(local_kernel, mine), grid_spec=pltpu.Pre...  10.9 us
    pallas_call x10, Pallas kernels, stage(): pl.pallas_call(kernel, in_specs=[pl.BlockSpec(memory_space=pltpu.SMEM)] +...  10.8 us
    pallas_call x2, Pallas kernels, local_reads(): pl.pallas_call(reads_kernel, grid_spec=pltpu.PrefetchScalarGridSpec(num_s...  6.63 us
  transfers between devices with their start and end apart: 26, of which 19 were waited for; matrix products, arithmetic and copies ran while one was open for 1% of the time, Pallas kernels for 20%

profile of v4, /device:TPU:0, one launch (start us, length us, event | category | flops | bytes accessed | tf_op | source)
XLA Modules:
  0.0 132.8 jit_solution(13794772075538506054)
XLA Ops:
  0.6 1.7 %collective-permute-start.12 = (bf16[256,1024]{1,0:T(8,128)(2,1)}, bf16[256,1024]{1,0:T(8,128)(2,1)S(1)}, u32[]{:S(2)}, u32[]{:S(2)}) collective-permute-start(bf16[256,1024]{1,0:T(8,128)(2,1)} %param.11), channel_id=1, source_target_pairs={{0,0},{1,32},{2,64},{3,96},{32,1},{33,33},{34,65},{35,97},{64,2},{... | collective-permute-start | bytes 1572872 | tf_op jit(solution)/shard_map/ppermute | solution.py:343
  2.3 26.1 %collective-permute-start.13 = (bf16[256,1024]{1,0:T(8,128)(2,1)S(1)}, bf16[256,1024]{1,0:T(8,128)(2,1)S(1)}, u32[]{:S(2)}, u32[]{:S(2)}) collective-permute-start(bf16[256,1024]{1,0:T(8,128)(2,1)S(1)} %collective-permute-done.12), channel_id=1, source_target_pairs={{0,1},{1,0},{2,3},{3,2},{4,5},{5,4},{6,7},{7,6},{8,9},{9,8},{10,11... | collective-permute-start | bytes 1572872 | tf_op jit(solution)/shard_map/ppermute | solution.py:336
  28.5 5.4 %local_maps.3 = (f32[4,128,256]{2,1,0:T(8,128)S(1)}, bf16[4,256,256]{2,1,0:T(8,128)(2,1)S(1)}, bf16[4,256,256]{2,1,0:T(8,128)(2,1)S(1)}, f32[1,8,256]{2,1,0:T(8,128)S(1)}) custom-call(s32[4]{0:T(128)S(1)} %pad_add_fusion.w_ref, bf16[256,1024]{1,0:T(8,128)(2,1)} %k_ref.7, bf16[256,1024]{1,0:T(8,128)(2,1)} %v_ref.3, f32[8,256]{1,0:T(8,128)} %bitcast.14), custom_call_target="tpu_custom_call" | custom-call | tf_op jit(solution)/shard_map/local_maps/pallas_call | solution.py:182
  34.0 5.1 %collective-permute-done.13 = bf16[256,1024]{1,0:T(8,128)(2,1)S(1)} collective-permute-done((bf16[256,1024]{1,0:T(8,128)(2,1)S(1)}, bf16[256,1024]{1,0:T(8,128)(2,1)S(1)}, u32[]{:S(2)}, u32[]{:S(2)}) %collective-permute-start.13) | collective-permute-done | bytes 524320 | tf_op jit(solution)/shard_map/ppermute | solution.py:336
  39.2 7.6 %collective-permute-start.14 = (bf16[2,256,1024]{2,1,0:T(8,128)(2,1)S(1)}, bf16[2,256,1024]{2,1,0:T(8,128)(2,1)S(1)}, u32[]{:S(2)}, u32[]{:S(2)}) collective-permute-start(bf16[2,256,1024]{2,1,0:T(8,128)(2,1)S(1)} %pad_maximum_fusion.1), channel_id=1, source_target_pairs={{0,3},{1,2},{2,1},{3,0},{4,7},{5,6},{6,5},{7,4},{8,11},{9,10},{10,... | collective-permute-start | bytes 3145736 | tf_op jit(solution)/shard_map/ppermute | solution.py:336
  46.8 5.4 %local_maps.2 = (f32[4,128,256]{2,1,0:T(8,128)S(1)}, bf16[4,256,256]{2,1,0:T(8,128)(2,1)S(1)}, bf16[4,256,256]{2,1,0:T(8,128)(2,1)S(1)}, f32[1,8,256]{2,1,0:T(8,128)S(1)}) custom-call(s32[4]{0:T(128)S(1)} %pad_add_fusion.w_ref, bf16[256,1024]{1,0:T(8,128)(2,1)} %k_ref.7, bf16[256,1024]{1,0:T(8,128)(2,1)} %v_ref.3, f32[8,256]{1,0:T(8,128)} %bitcast.15), custom_call_target="tpu_custom_call" | custom-call | tf_op jit(solution)/shard_map/local_maps/pallas_call | solution.py:182
  53.3 2.0 %collective-permute-start.1 = (f16[128,256]{1,0:T(8,128)(2,1)S(1)}, f16[128,256]{1,0:T(8,128)(2,1)S(1)}, u32[]{:S(2)}, u32[]{:S(2)}) collective-permute-start(f16[128,256]{1,0:T(8,128)(2,1)S(1)} %convert_element_type.56), channel_id=1, source_target_pairs={{0,8},{8,16},{16,24},{24,0},{1,9},{9,17},{17,25},{25,1},{2,10},{10... | collective-permute-start | bytes 196616 | tf_op jit(solution)/shard_map/ppermute | solution.py:331
  55.3 3.7 %collective-permute-start.2 = (f16[128,256]{1,0:T(8,128)(2,1)S(1)}, f16[128,256]{1,0:T(8,128)(2,1)S(1)}, u32[]{:S(2)}, u32[]{:S(2)}) collective-permute-start(f16[128,256]{1,0:T(8,128)(2,1)S(1)} %convert_element_type.58), channel_id=1, source_target_pairs={{0,16},{8,24},{16,0},{24,8},{1,17},{9,25},{17,1},{25,9},{2,18},{10... | collective-permute-start | bytes 196616 | tf_op jit(solution)/shard_map/ppermute | solution.py:331
  60.1 2.6 %collective-permute-done.2 = f16[128,256]{1,0:T(8,128)(2,1)S(1)} collective-permute-done((f16[128,256]{1,0:T(8,128)(2,1)S(1)}, f16[128,256]{1,0:T(8,128)(2,1)S(1)}, u32[]{:S(2)}, u32[]{:S(2)}) %collective-permute-start.2) | collective-permute-done | bytes 65568 | tf_op jit(solution)/shard_map/ppermute | solution.py:331
  63.3 1.2 shard_map.78
  65.4 1.3 collective-permute-start.6
  66.7 2.1 %collective-permute-done.4 = f16[128,256]{1,0:T(8,128)(2,1)S(1)} collective-permute-done((f16[128,256]{1,0:T(8,128)(2,1)S(1)}, f16[128,256]{1,0:T(8,128)(2,1)S(1)}, u32[]{:S(2)}, u32[]{:S(2)}) %collective-permute-start.4) | collective-permute-done | bytes 65568 | tf_op jit(solution)/shard_map/ppermute | solution.py:331
  68.8 2.4 %collective-permute-done.5 = f16[128,256]{1,0:T(8,128)(2,1)S(1)} collective-permute-done((f16[128,256]{1,0:T(8,128)(2,1)S(1)}, f16[128,256]{1,0:T(8,128)(2,1)S(1)}, u32[]{:S(2)}, u32[]{:S(2)}) %collective-permute-start.5) | collective-permute-done | bytes 65568 | tf_op jit(solution)/shard_map/ppermute | solution.py:331
  71.9 1.1 shard_map.79
  74.2 2.8 %collective-permute-start.8 = (f32[128,128]{1,0:T(8,128)S(1)}, f32[128,128]{1,0:T(8,128)S(1)}, u32[]{:S(2)}, u32[]{:S(2)}) collective-permute-start(f32[128,128]{1,0:T(8,128)S(1)} %get-tuple-element.48), channel_id=1, source_target_pairs={{0,16},{8,24},{16,0},{24,8},{1,17},{9,25},{17,1},{25,9},{2,18},{10... | collective-permute-start | bytes 196616 | tf_op jit(solution)/shard_map/ppermute | solution.py:331
  78.8 1.2 collective-permute-done.8.s2_ref
  79.9 1.3 collective-permute-done.9.s3_ref
  81.9 3.3 %local_reads.2 = (bf16[4,256,128]{2,1,0:T(8,128)(2,1)S(1)}, bf16[4,256,128]{2,1,0:T(8,128)(2,1)S(1)}, f32[4,256,128]{2,1,0:T(8,128)S(1)}) custom-call(s32[4]{0:T(128)S(1)} %pad_add_fusion.w_ref, bf16[256,1024]{1,0:T(8,128)(2,1)} %q_ref.3, bf16[256,1024]{1,0:T(8,128)(2,1)} %k_ref.7, bf16[4,256,256]{2,1,0:T(8,128)(2,1)S(1)} %get-tuple-element.32.xh_ref, ...), custom_call_target="tpu_custom_call" | custom-call | tf_op jit(solution)/shard_map/local_reads/pallas_call | solution.py:234
  85.2 3.3 %local_reads.3 = (bf16[4,256,128]{2,1,0:T(8,128)(2,1)S(1)}, bf16[4,256,128]{2,1,0:T(8,128)(2,1)S(1)}, f32[4,256,128]{2,1,0:T(8,128)S(1)}) custom-call(s32[4]{0:T(128)S(1)} %pad_add_fusion.w_ref, bf16[256,1024]{1,0:T(8,128)(2,1)} %q_ref.3, bf16[256,1024]{1,0:T(8,128)(2,1)} %k_ref.7, bf16[4,256,256]{2,1,0:T(8,128)(2,1)S(1)} %get-tuple-element.50.xh_ref, ...), custom_call_target="tpu_custom_call" | custom-call | tf_op jit(solution)/shard_map/local_reads/pallas_call | solution.py:234
  91.0 2.8 %collective-permute-start.17 = (bf16[256,512]{1,0:T(8,128)(2,1)S(1)}, bf16[256,512]{1,0:T(8,128)(2,1)S(1)}, u32[]{:S(2)}, u32[]{:S(2)}) collective-permute-start(bf16[256,512]{1,0:T(8,128)(2,1)S(1)} %shard_map.82.refs_1_), channel_id=1, source_target_pairs={{0,96},{32,0},{64,32},{96,64},{1,97},{33,1},{65,33},{97,65},{2,98}... | collective-permute-start | bytes 786440 | tf_op jit(solution)/shard_map/ppermute | solution.py:331
  94.3 1.6 %collective-permute-start.19 = (bf16[256,512]{1,0:T(8,128)(2,1)S(1)}, bf16[256,512]{1,0:T(8,128)(2,1)S(1)}, u32[]{:S(2)}, u32[]{:S(2)}) collective-permute-start(bf16[256,512]{1,0:T(8,128)(2,1)S(1)} %shard_map.82.refs_1_), channel_id=1, source_target_pairs={{0,32},{32,64},{64,96},{96,0},{1,33},{33,65},{65,97},{97,1},{2,34}... | collective-permute-start | bytes 786440 | tf_op jit(solution)/shard_map/ppermute | solution.py:331
  95.9 2.8 %collective-permute-done.15.refs_2_ = bf16[256,512]{1,0:T(8,128)(2,1)S(1)} collective-permute-done((bf16[256,512]{1,0:T(8,128)(2,1)S(1)}, bf16[256,512]{1,0:T(8,128)(2,1)S(1)}, u32[]{:S(2)}, u32[]{:S(2)}) %collective-permute-start.15) | collective-permute-done | bytes 262176 | tf_op jit(solution)/shard_map/ppermute | solution.py:331
  99.6 3.7 %collective-permute-start.18 = (bf16[256,512]{1,0:T(8,128)(2,1)S(1)}, bf16[256,512]{1,0:T(8,128)(2,1)S(1)}, u32[]{:S(2)}, u32[]{:S(2)}) collective-permute-start(bf16[256,512]{1,0:T(8,128)(2,1)S(1)} %collective-permute-done.17.refs_5_), channel_id=1, source_target_pairs={{0,96},{32,0},{64,32},{96,64},{1,97},{33,1},{65,33},{97,65},{2,98}... | collective-permute-start | bytes 786440 | tf_op jit(solution)/shard_map/ppermute | solution.py:331
  103.5 1.7 %collective-permute-done.20.refs_4_ = bf16[256,512]{1,0:T(8,128)(2,1)S(1)} collective-permute-done((bf16[256,512]{1,0:T(8,128)(2,1)S(1)}, bf16[256,512]{1,0:T(8,128)(2,1)S(1)}, u32[]{:S(2)}, u32[]{:S(2)}) %collective-permute-start.20) | collective-permute-done | bytes 262176 | tf_op jit(solution)/shard_map/ppermute | solution.py:331
  105.2 2.4 %shard_map.83 = (f32[512,1024]{1,0:T(8,128)S(1)}, f32[512,1024]{1,0:T(8,128)S(1)}) custom-call(s32[4]{0:T(128)S(1)} %pad_add_fusion.w_ref, bf16[4,256,1024]{2,1,0:T(8,128)(2,1)S(1)} %pad_maximum_fusion.cot_ref, bf16[256,512]{1,0:T(8,128)(2,1)S(1)} %shard_map.81.refs_0_, bf16[256,512]{1,0:T(8,128)(2,1)S(1)} %shard_map.82.refs_1_, ...), custom_call_target="tpu_custom_call" | custom-call | tf_op jit(solution)/shard_map/pallas_call | solution.py:265
  107.6 2.7 %collective-permute-done.16.b_ref = bf16[256,512]{1,0:T(8,128)(2,1)S(1)} collective-permute-done((bf16[256,512]{1,0:T(8,128)(2,1)S(1)}, bf16[256,512]{1,0:T(8,128)(2,1)S(1)}, u32[]{:S(2)}, u32[]{:S(2)}) %collective-permute-start.16) | collective-permute-done | bytes 262176 | tf_op jit(solution)/shard_map/ppermute | solution.py:331
  111.8 1.2 collective-permute-start.21
  114.0 1.3 collective-permute-done.21.got_ref
  116.5 1.7 %collective-permute-start.24 = (bf16[256,512]{1,0:T(8,128)(2,1)S(1)}, bf16[256,512]{1,0:T(8,128)(2,1)S(1)}, u32[]{:S(2)}, u32[]{:S(2)}) collective-permute-start(bf16[256,512]{1,0:T(8,128)(2,1)S(1)} %get-tuple-element.61), channel_id=1, source_target_pairs={{0,24},{8,16},{16,8},{24,0},{1,25},{9,17},{17,9},{25,1},{2,26},{10... | collective-permute-start | bytes 786440 | tf_op jit(solution)/shard_map/ppermute | solution.py:336
  119.1 5.6 %collective-permute-done.22 = bf16[256,512]{1,0:T(8,128)(2,1)S(1)} collective-permute-done((bf16[256,512]{1,0:T(8,128)(2,1)S(1)}, bf16[256,512]{1,0:T(8,128)(2,1)S(1)}, u32[]{:S(2)}, u32[]{:S(2)}) %collective-permute-start.22) | collective-permute-done | bytes 262176 | tf_op jit(solution)/shard_map/ppermute | solution.py:336
  124.7 2.1 %collective-permute-start.23 = (bf16[128,512]{1,0:T(8,128)(2,1)S(1)}, bf16[128,512]{1,0:T(8,128)(2,1)S(1)}, u32[]{:S(2)}, u32[]{:S(2)}) collective-permute-start(bf16[128,512]{1,0:T(8,128)(2,1)S(1)} %add_convert_fusion.1), channel_id=1, source_target_pairs={{0,24},{8,16},{16,8},{24,0},{1,25},{9,17},{17,9},{25,1},{2,26},{10... | collective-permute-start | bytes 393224 | tf_op jit(solution)/shard_map/ppermute | solution.py:336
  126.9 4.1 %collective-permute-done.23 = bf16[128,512]{1,0:T(8,128)(2,1)S(1)} collective-permute-done((bf16[128,512]{1,0:T(8,128)(2,1)S(1)}, bf16[128,512]{1,0:T(8,128)(2,1)S(1)}, u32[]{:S(2)}, u32[]{:S(2)}) %collective-permute-start.23) | collective-permute-done | bytes 131104 | tf_op jit(solution)/shard_map/ppermute | solution.py:336
  (55 shorter events, 18.7 us)
Async XLA Ops:
  0.6 1.7 %collective-permute-start.12 = (bf16[256,1024]{1,0:T(8,128)(2,1)}, bf16[256,1024]{1,0:T(8,128)(2,1)S(1)}, u32[]{:S(2)}, u32[]{:S(2)}) collective-permute-start(bf16[256,1024]{1,0:T(8,128)(2,1)} %param.11), channel_id=1, source_target_pairs={{0,0},{1,32},{2,64},{3,96},{32,1},{33,33},{34,65},{35,97},{64,2},{... | collective-permute-start | bytes 1572872 | tf_op jit(solution)/shard_map/ppermute | solution.py:343
  2.3 36.8 %collective-permute-start.13 = (bf16[256,1024]{1,0:T(8,128)(2,1)S(1)}, bf16[256,1024]{1,0:T(8,128)(2,1)S(1)}, u32[]{:S(2)}, u32[]{:S(2)}) collective-permute-start(bf16[256,1024]{1,0:T(8,128)(2,1)S(1)} %collective-permute-done.12), channel_id=1, source_target_pairs={{0,1},{1,0},{2,3},{3,2},{4,5},{5,4},{6,7},{7,6},{8,9},{9,8},{10,11... | collective-permute-start | bytes 1572872 | tf_op jit(solution)/shard_map/ppermute | solution.py:336
  33.9 18.4 %collective-permute-start = (f32[4,128,256]{2,1,0:T(8,128)S(1)}, f32[4,128,256]{2,1,0:T(8,128)S(1)}, u32[]{:S(2)}, u32[]{:S(2)}) collective-permute-start(f32[4,128,256]{2,1,0:T(8,128)S(1)} %get-tuple-element.35), channel_id=1, source_target_pairs={{0,4},{4,0},{1,5},{5,1},{2,6},{6,2},{3,7},{7,3},{8,12},{12,8},{9,1... | collective-permute-start | bytes 1572872 | tf_op jit(solution)/shard_map/ppermute | solution.py:336
  39.2 64.0 %collective-permute-start.14 = (bf16[2,256,1024]{2,1,0:T(8,128)(2,1)S(1)}, bf16[2,256,1024]{2,1,0:T(8,128)(2,1)S(1)}, u32[]{:S(2)}, u32[]{:S(2)}) collective-permute-start(bf16[2,256,1024]{2,1,0:T(8,128)(2,1)S(1)} %pad_maximum_fusion.1), channel_id=1, source_target_pairs={{0,3},{1,2},{2,1},{3,0},{4,7},{5,6},{6,5},{7,4},{8,11},{9,10},{10,... | collective-permute-start | bytes 3145736 | tf_op jit(solution)/shard_map/ppermute | solution.py:336
  52.3 33.0 %collective-permute-start.10 = (f32[4,128,256]{2,1,0:T(8,128)S(1)}, f32[4,128,256]{2,1,0:T(8,128)S(1)}, u32[]{:S(2)}, u32[]{:S(2)}) collective-permute-start(f32[4,128,256]{2,1,0:T(8,128)S(1)} %get-tuple-element.39.own_ref), channel_id=1, source_target_pairs={{0,4},{4,0},{1,5},{5,1},{2,6},{6,2},{3,7},{7,3},{8,12},{12,8},{9,1... | collective-permute-start | bytes 1572872 | tf_op jit(solution)/shard_map/ppermute | solution.py:336
  53.3 6.9 %collective-permute-start.1 = (f16[128,256]{1,0:T(8,128)(2,1)S(1)}, f16[128,256]{1,0:T(8,128)(2,1)S(1)}, u32[]{:S(2)}, u32[]{:S(2)}) collective-permute-start(f16[128,256]{1,0:T(8,128)(2,1)S(1)} %convert_element_type.56), channel_id=1, source_target_pairs={{0,8},{8,16},{16,24},{24,0},{1,9},{9,17},{17,25},{25,1},{2,10},{10... | collective-permute-start | bytes 196616 | tf_op jit(solution)/shard_map/ppermute | solution.py:331
  55.3 7.4 %collective-permute-start.2 = (f16[128,256]{1,0:T(8,128)(2,1)S(1)}, f16[128,256]{1,0:T(8,128)(2,1)S(1)}, u32[]{:S(2)}, u32[]{:S(2)}) collective-permute-start(f16[128,256]{1,0:T(8,128)(2,1)S(1)} %convert_element_type.58), channel_id=1, source_target_pairs={{0,16},{8,24},{16,0},{24,8},{1,17},{9,25},{17,1},{25,9},{2,18},{10... | collective-permute-start | bytes 196616 | tf_op jit(solution)/shard_map/ppermute | solution.py:331
  58.9 4.3 %collective-permute-start.3 = (f16[128,256]{1,0:T(8,128)(2,1)S(1)}, f16[128,256]{1,0:T(8,128)(2,1)S(1)}, u32[]{:S(2)}, u32[]{:S(2)}) collective-permute-start(f16[128,256]{1,0:T(8,128)(2,1)S(1)} %convert_element_type.60), channel_id=1, source_target_pairs={{0,24},{8,0},{16,8},{24,16},{1,25},{9,1},{17,9},{25,17},{2,26},{10... | collective-permute-start | bytes 196616 | tf_op jit(solution)/shard_map/ppermute | solution.py:331
  64.5 4.3 %collective-permute-start.4 = (f16[128,256]{1,0:T(8,128)(2,1)S(1)}, f16[128,256]{1,0:T(8,128)(2,1)S(1)}, u32[]{:S(2)}, u32[]{:S(2)}) collective-permute-start(f16[128,256]{1,0:T(8,128)(2,1)S(1)} %convert_element_type.62), channel_id=1, source_target_pairs={{0,96},{32,0},{64,32},{96,64},{1,97},{33,1},{65,33},{97,65},{2,98}... | collective-permute-start | bytes 196616 | tf_op jit(solution)/shard_map/ppermute | solution.py:331
  65.4 5.9 %collective-permute-start.5 = (f16[128,256]{1,0:T(8,128)(2,1)S(1)}, f16[128,256]{1,0:T(8,128)(2,1)S(1)}, u32[]{:S(2)}, u32[]{:S(2)}) collective-permute-start(f16[128,256]{1,0:T(8,128)(2,1)S(1)} %convert_element_type.62), channel_id=1, source_target_pairs={{0,64},{32,96},{64,0},{96,32},{1,65},{33,97},{65,1},{97,33},{2,66}... | collective-permute-start | bytes 196616 | tf_op jit(solution)/shard_map/ppermute | solution.py:331
  65.4 6.5 %collective-permute-start.6 = (f16[128,256]{1,0:T(8,128)(2,1)S(1)}, f16[128,256]{1,0:T(8,128)(2,1)S(1)}, u32[]{:S(2)}, u32[]{:S(2)}) collective-permute-start(f16[128,256]{1,0:T(8,128)(2,1)S(1)} %convert_element_type.62), channel_id=1, source_target_pairs={{0,32},{32,64},{64,96},{96,0},{1,33},{33,65},{65,97},{97,1},{2,34}... | collective-permute-start | bytes 196616 | tf_op jit(solution)/shard_map/ppermute | solution.py:331
  73.0 5.7 %collective-permute-start.7 = (f32[128,128]{1,0:T(8,128)S(1)}, f32[128,128]{1,0:T(8,128)S(1)}, u32[]{:S(2)}, u32[]{:S(2)}) collective-permute-start(f32[128,128]{1,0:T(8,128)S(1)} %get-tuple-element.47), channel_id=1, source_target_pairs={{0,8},{8,16},{16,24},{24,0},{1,9},{9,17},{17,25},{25,1},{2,10},{10... | collective-permute-start | bytes 196616 | tf_op jit(solution)/shard_map/ppermute | solution.py:331
  74.2 5.8 %collective-permute-start.8 = (f32[128,128]{1,0:T(8,128)S(1)}, f32[128,128]{1,0:T(8,128)S(1)}, u32[]{:S(2)}, u32[]{:S(2)}) collective-permute-start(f32[128,128]{1,0:T(8,128)S(1)} %get-tuple-element.48), channel_id=1, source_target_pairs={{0,16},{8,24},{16,0},{24,8},{1,17},{9,25},{17,1},{25,9},{2,18},{10... | collective-permute-start | bytes 196616 | tf_op jit(solution)/shard_map/ppermute | solution.py:331
  77.0 4.3 %collective-permute-start.9 = (f32[128,128]{1,0:T(8,128)S(1)}, f32[128,128]{1,0:T(8,128)S(1)}, u32[]{:S(2)}, u32[]{:S(2)}) collective-permute-start(f32[128,128]{1,0:T(8,128)S(1)} %get-tuple-element.49), channel_id=1, source_target_pairs={{0,24},{8,0},{16,8},{24,16},{1,25},{9,1},{17,9},{25,17},{2,26},{10... | collective-permute-start | bytes 196616 | tf_op jit(solution)/shard_map/ppermute | solution.py:331
  81.8 8.3 %collective-permute-start.11 = (f32[4,128,128]{2,1,0:T(8,128)S(1)}, f32[4,128,128]{2,1,0:T(8,128)S(1)}, u32[]{:S(2)}, u32[]{:S(2)}) collective-permute-start(f32[4,128,128]{2,1,0:T(8,128)S(1)} %shard_map.80.s_ref), channel_id=1, source_target_pairs={{0,4},{4,0},{1,5},{5,1},{2,6},{6,2},{3,7},{7,3},{8,12},{12,8},{9,1... | collective-permute-start | bytes 786440 | tf_op jit(solution)/shard_map/ppermute | solution.py:336
  81.9 6.7 %copy-start = (f32[128]{0:T(128)S(1)}, f32[128]{0:T(128)}, u32[]{:S(2)}) copy-start(f32[128]{0:T(128)} %param.10) | copy-start | bytes 1540
  89.5 9.2 %collective-permute-start.15 = (bf16[256,512]{1,0:T(8,128)(2,1)S(1)}, bf16[256,512]{1,0:T(8,128)(2,1)S(1)}, u32[]{:S(2)}, u32[]{:S(2)}) collective-permute-start(bf16[256,512]{1,0:T(8,128)(2,1)S(1)} %shard_map.81.refs_0_), channel_id=1, source_target_pairs={{0,32},{32,64},{64,96},{96,0},{1,33},{33,65},{65,97},{97,1},{2,34}... | collective-permute-start | bytes 786440 | tf_op jit(solution)/shard_map/ppermute | solution.py:331
  91.0 8.5 %collective-permute-start.17 = (bf16[256,512]{1,0:T(8,128)(2,1)S(1)}, bf16[256,512]{1,0:T(8,128)(2,1)S(1)}, u32[]{:S(2)}, u32[]{:S(2)}) collective-permute-start(bf16[256,512]{1,0:T(8,128)(2,1)S(1)} %shard_map.82.refs_1_), channel_id=1, source_target_pairs={{0,96},{32,0},{64,32},{96,64},{1,97},{33,1},{65,33},{97,65},{2,98}... | collective-permute-start | bytes 786440 | tf_op jit(solution)/shard_map/ppermute | solution.py:331
  93.9 11.3 %collective-permute-start.20 = (bf16[256,512]{1,0:T(8,128)(2,1)S(1)}, bf16[256,512]{1,0:T(8,128)(2,1)S(1)}, u32[]{:S(2)}, u32[]{:S(2)}) collective-permute-start(bf16[256,512]{1,0:T(8,128)(2,1)S(1)} %shard_map.81.refs_0_), channel_id=1, source_target_pairs={{0,96},{32,0},{64,32},{96,64},{1,97},{33,1},{65,33},{97,65},{2,98}... | collective-permute-start | bytes 786440 | tf_op jit(solution)/shard_map/ppermute | solution.py:331
  94.3 10.9 %collective-permute-start.19 = (bf16[256,512]{1,0:T(8,128)(2,1)S(1)}, bf16[256,512]{1,0:T(8,128)(2,1)S(1)}, u32[]{:S(2)}, u32[]{:S(2)}) collective-permute-start(bf16[256,512]{1,0:T(8,128)(2,1)S(1)} %shard_map.82.refs_1_), channel_id=1, source_target_pairs={{0,32},{32,64},{64,96},{96,0},{1,33},{33,65},{65,97},{97,1},{2,34}... | collective-permute-start | bytes 786440 | tf_op jit(solution)/shard_map/ppermute | solution.py:331
  98.7 11.6 %collective-permute-start.16 = (bf16[256,512]{1,0:T(8,128)(2,1)S(1)}, bf16[256,512]{1,0:T(8,128)(2,1)S(1)}, u32[]{:S(2)}, u32[]{:S(2)}) collective-permute-start(bf16[256,512]{1,0:T(8,128)(2,1)S(1)} %collective-permute-done.15.refs_2_), channel_id=1, source_target_pairs={{0,32},{32,64},{64,96},{96,0},{1,33},{33,65},{65,97},{97,1},{2,34}... | collective-permute-start | bytes 786440 | tf_op jit(solution)/shard_map/ppermute | solution.py:331
  99.6 11.2 %collective-permute-start.18 = (bf16[256,512]{1,0:T(8,128)(2,1)S(1)}, bf16[256,512]{1,0:T(8,128)(2,1)S(1)}, u32[]{:S(2)}, u32[]{:S(2)}) collective-permute-start(bf16[256,512]{1,0:T(8,128)(2,1)S(1)} %collective-permute-done.17.refs_5_), channel_id=1, source_target_pairs={{0,96},{32,0},{64,32},{96,64},{1,97},{33,1},{65,33},{97,65},{2,98}... | collective-permute-start | bytes 786440 | tf_op jit(solution)/shard_map/ppermute | solution.py:331
  111.8 3.5 %collective-permute-start.21 = (bf16[512,1024]{1,0:T(8,128)(2,1)S(1)}, bf16[512,1024]{1,0:T(8,128)(2,1)S(1)}, u32[]{:S(2)}, u32[]{:S(2)}) collective-permute-start(bf16[512,1024]{1,0:T(8,128)(2,1)S(1)} %shard_map.85), channel_id=1, source_target_pairs={{0,4},{4,0},{1,5},{5,1},{2,6},{6,2},{3,7},{7,3},{8,12},{12,8},{9,1... | collective-permute-start | bytes 3145736 | tf_op jit(solution)/shard_map/ppermute | solution.py:336
  116.0 8.7 %collective-permute-start.22 = (bf16[256,512]{1,0:T(8,128)(2,1)S(1)}, bf16[256,512]{1,0:T(8,128)(2,1)S(1)}, u32[]{:S(2)}, u32[]{:S(2)}) collective-permute-start(bf16[256,512]{1,0:T(8,128)(2,1)S(1)} %get-tuple-element.59), channel_id=1, source_target_pairs={{0,8},{8,0},{16,24},{24,16},{1,9},{9,1},{17,25},{25,17},{2,10},{10... | collective-permute-start | bytes 786440 | tf_op jit(solution)/shard_map/ppermute | solution.py:336
  116.5 10.3 %collective-permute-start.24 = (bf16[256,512]{1,0:T(8,128)(2,1)S(1)}, bf16[256,512]{1,0:T(8,128)(2,1)S(1)}, u32[]{:S(2)}, u32[]{:S(2)}) collective-permute-start(bf16[256,512]{1,0:T(8,128)(2,1)S(1)} %get-tuple-element.61), channel_id=1, source_target_pairs={{0,24},{8,16},{16,8},{24,0},{1,25},{9,17},{17,9},{25,1},{2,26},{10... | collective-permute-start | bytes 786440 | tf_op jit(solution)/shard_map/ppermute | solution.py:336
  124.7 6.3 %collective-permute-start.23 = (bf16[128,512]{1,0:T(8,128)(2,1)S(1)}, bf16[128,512]{1,0:T(8,128)(2,1)S(1)}, u32[]{:S(2)}, u32[]{:S(2)}) collective-permute-start(bf16[128,512]{1,0:T(8,128)(2,1)S(1)} %add_convert_fusion.1), channel_id=1, source_target_pairs={{0,24},{8,16},{16,8},{24,0},{1,25},{9,17},{17,9},{25,1},{2,26},{10... | collective-permute-start | bytes 393224 | tf_op jit(solution)/shard_map/ppermute | solution.py:336
  126.8 5.0 %collective-permute-start.25 = (bf16[128,512]{1,0:T(8,128)(2,1)S(1)}, bf16[128,512]{1,0:T(8,128)(2,1)S(1)}, u32[]{:S(2)}, u32[]{:S(2)}) collective-permute-start(bf16[128,512]{1,0:T(8,128)(2,1)S(1)} %add_convert_fusion), channel_id=1, source_target_pairs={{0,8},{8,0},{16,24},{24,16},{1,9},{9,1},{17,25},{25,17},{2,10},{10... | collective-permute-start | bytes 393224 | tf_op jit(solution)/shard_map/ppermute | solution.py:336

commit v5 on v4

--- a/solution.py
+++ b/solution.py
@@ -46,6 +46,12 @@
 def mm(a, b):
     o = dot(lhs_of(a), rhs_of(b))
     return o[:, :F] + o[:, F:]
+
+
+def mm_two(a, c, b):
+    o = dot(jnp.concatenate([lhs_of(a), lhs_of(c)], axis=0), rhs_of(b))
+    o = o[:, :F] + o[:, F:]
+    return o[:F], o[F:]
 
 
 def mm_all(pairs):
@@ -112,12 +118,10 @@
     ns = [split(a) for a in n]
     n2 = mm_all(zip(ns, ns))
     n2s = [split(a) for a in n2]
-    n4 = mm_all(zip(n2s, n2s))
-    q1 = mm_all(zip(ns, n2s))
+    n4, q1 = zip(*[mm_two(b, a, b) for a, b in zip(ns, n2s)])
     n4s = [split(a) for a in n4]
     r1 = [eye - a + b - c for a, b, c in zip(n, n2, q1)]
-    n8 = mm_all(zip(n4s, n4s))
-    q2 = mm_all(zip([split(a) for a in r1], n4s))
+    n8, q2 = zip(*[mm_two(b, split(a), b) for a, b in zip(r1, n4s)])
     r2 = [a + b for a, b in zip(r1, q2)]
     q3 = mm_all(zip([split(a) for a in r2], [split(a) for a in n8]))
     d = [a + b for a, b in zip(r2, q3)]
@@ -212,7 +216,9 @@
         sh, sl = split(s)
         n = g * HB + i
         xh, xl = xh_ref[n], xl_ref[n]
-        o = dot(sh, xh) + (dot(sl, xh) + dot(sh, xl))
+        top = dot(jnp.concatenate([sh[:F, :F], sl[:F, :F]], axis=1), jnp.concatenate([xh[:F], xh[:F]], axis=0))
+        top += dot(sh[:F, :F], xl[:F])
+        o = jnp.concatenate([top, dot(sh[F:], xh) + (dot(sl[F:], xh) + dot(sh[F:], xl))], axis=0)
         qe = q.astype(f32) - o[:, :F]
         qh, ql = split(qe)
         qh_ref[n] = qh

time: 133 us -> 133 us (level)
  no operation moved by 1% of the time
where the time goes in v5:
time: 133 us
  starting transfers between devices  63.9 us (48%)
  waiting for transfers between devices  37.4 us (28%)
  Pallas kernels  28.1 us (21%)
  other arithmetic  2.39 us (2%)
    ppermute x10, starting transfers between devices, swap(): return lax.ppermute(x, axis, [(i, i ^ k) for i in range(n)])  39.4 us
    ppermute x15, starting transfers between devices, shift(): return lax.ppermute(x, axis, [(i, (i + k) % 4) for i in range(4)])  22.7 us
    ppermute x15, waiting for transfers between devices, shift(): return lax.ppermute(x, axis, [(i, (i + k) % 4) for i in range(4)])  20.5 us
    ppermute x10, waiting for transfers between devices, swap(): return lax.ppermute(x, axis, [(i, i ^ k) for i in range(n)])  16.9 us
    pallas_call x2, Pallas kernels, local_maps(): pl.pallas_call(functools.partial(local_kernel, mine), grid_spec=pltpu.Pre...  10.8 us
    pallas_call x10, Pallas kernels, stage(): pl.pallas_call(kernel, in_specs=[pl.BlockSpec(memory_space=pltpu.SMEM)] +...  10.8 us
    pallas_call x2, Pallas kernels, local_reads(): pl.pallas_call(reads_kernel, grid_spec=pltpu.PrefetchScalarGridSpec(num_s...  6.47 us
  transfers between devices with their start and end apart: 26, of which 19 were waited for; matrix products, arithmetic and copies ran while one was open for 1% of the time, Pallas kernels for 20%

profile of v5, /device:TPU:0, one launch (start us, length us, event | category | flops | bytes accessed | tf_op | source)
XLA Modules:
  0.0 132.6 jit_solution(293070530091457216)
XLA Ops:
  0.6 1.7 %collective-permute-start.12 = (bf16[256,1024]{1,0:T(8,128)(2,1)}, bf16[256,1024]{1,0:T(8,128)(2,1)S(1)}, u32[]{:S(2)}, u32[]{:S(2)}) collective-permute-start(bf16[256,1024]{1,0:T(8,128)(2,1)} %param.11), channel_id=1, source_target_pairs={{0,0},{1,32},{2,64},{3,96},{32,1},{33,33},{34,65},{35,97},{64,2},{... | collective-permute-start | bytes 1572872 | tf_op jit(solution)/shard_map/ppermute | solution.py:349
  2.3 26.1 %collective-permute-start.13 = (bf16[256,1024]{1,0:T(8,128)(2,1)S(1)}, bf16[256,1024]{1,0:T(8,128)(2,1)S(1)}, u32[]{:S(2)}, u32[]{:S(2)}) collective-permute-start(bf16[256,1024]{1,0:T(8,128)(2,1)S(1)} %collective-permute-done.12), channel_id=1, source_target_pairs={{0,1},{1,0},{2,3},{3,2},{4,5},{5,4},{6,7},{7,6},{8,9},{9,8},{10,11... | collective-permute-start | bytes 1572872 | tf_op jit(solution)/shard_map/ppermute | solution.py:342
  28.5 5.4 %local_maps.3 = (f32[4,128,256]{2,1,0:T(8,128)S(1)}, bf16[4,256,256]{2,1,0:T(8,128)(2,1)S(1)}, bf16[4,256,256]{2,1,0:T(8,128)(2,1)S(1)}, f32[1,8,256]{2,1,0:T(8,128)S(1)}) custom-call(s32[4]{0:T(128)S(1)} %pad_add_fusion.w_ref, bf16[256,1024]{1,0:T(8,128)(2,1)} %k_ref.7, bf16[256,1024]{1,0:T(8,128)(2,1)} %v_ref.3, f32[8,256]{1,0:T(8,128)} %bitcast.14), custom_call_target="tpu_custom_call" | custom-call | tf_op jit(solution)/shard_map/local_maps/pallas_call | solution.py:186
  34.0 5.1 %collective-permute-done.13 = bf16[256,1024]{1,0:T(8,128)(2,1)S(1)} collective-permute-done((bf16[256,1024]{1,0:T(8,128)(2,1)S(1)}, bf16[256,1024]{1,0:T(8,128)(2,1)S(1)}, u32[]{:S(2)}, u32[]{:S(2)}) %collective-permute-start.13) | collective-permute-done | bytes 524320 | tf_op jit(solution)/shard_map/ppermute | solution.py:342
  39.2 7.6 %collective-permute-start.14 = (bf16[2,256,1024]{2,1,0:T(8,128)(2,1)S(1)}, bf16[2,256,1024]{2,1,0:T(8,128)(2,1)S(1)}, u32[]{:S(2)}, u32[]{:S(2)}) collective-permute-start(bf16[2,256,1024]{2,1,0:T(8,128)(2,1)S(1)} %pad_maximum_fusion.1), channel_id=1, source_target_pairs={{0,3},{1,2},{2,1},{3,0},{4,7},{5,6},{6,5},{7,4},{8,11},{9,10},{10,... | collective-permute-start | bytes 3145736 | tf_op jit(solution)/shard_map/ppermute | solution.py:342
  46.8 5.4 %local_maps.2 = (f32[4,128,256]{2,1,0:T(8,128)S(1)}, bf16[4,256,256]{2,1,0:T(8,128)(2,1)S(1)}, bf16[4,256,256]{2,1,0:T(8,128)(2,1)S(1)}, f32[1,8,256]{2,1,0:T(8,128)S(1)}) custom-call(s32[4]{0:T(128)S(1)} %pad_add_fusion.w_ref, bf16[256,1024]{1,0:T(8,128)(2,1)} %k_ref.7, bf16[256,1024]{1,0:T(8,128)(2,1)} %v_ref.3, f32[8,256]{1,0:T(8,128)} %bitcast.15), custom_call_target="tpu_custom_call" | custom-call | tf_op jit(solution)/shard_map/local_maps/pallas_call | solution.py:186
  53.2 2.0 %collective-permute-start.1 = (f16[128,256]{1,0:T(8,128)(2,1)S(1)}, f16[128,256]{1,0:T(8,128)(2,1)S(1)}, u32[]{:S(2)}, u32[]{:S(2)}) collective-permute-start(f16[128,256]{1,0:T(8,128)(2,1)S(1)} %convert_element_type.56), channel_id=1, source_target_pairs={{0,8},{8,16},{16,24},{24,0},{1,9},{9,17},{17,25},{25,1},{2,10},{10... | collective-permute-start | bytes 196616 | tf_op jit(solution)/shard_map/ppermute | solution.py:337
  55.2 3.7 %collective-permute-start.2 = (f16[128,256]{1,0:T(8,128)(2,1)S(1)}, f16[128,256]{1,0:T(8,128)(2,1)S(1)}, u32[]{:S(2)}, u32[]{:S(2)}) collective-permute-start(f16[128,256]{1,0:T(8,128)(2,1)S(1)} %convert_element_type.58), channel_id=1, source_target_pairs={{0,16},{8,24},{16,0},{24,8},{1,17},{9,25},{17,1},{25,9},{2,18},{10... | collective-permute-start | bytes 196616 | tf_op jit(solution)/shard_map/ppermute | solution.py:337
  60.1 2.6 %collective-permute-done.2 = f16[128,256]{1,0:T(8,128)(2,1)S(1)} collective-permute-done((f16[128,256]{1,0:T(8,128)(2,1)S(1)}, f16[128,256]{1,0:T(8,128)(2,1)S(1)}, u32[]{:S(2)}, u32[]{:S(2)}) %collective-permute-start.2) | collective-permute-done | bytes 65568 | tf_op jit(solution)/shard_map/ppermute | solution.py:337
  63.3 1.2 shard_map.78
  65.4 1.3 collective-permute-start.6
  66.7 2.1 %collective-permute-done.4 = f16[128,256]{1,0:T(8,128)(2,1)S(1)} collective-permute-done((f16[128,256]{1,0:T(8,128)(2,1)S(1)}, f16[128,256]{1,0:T(8,128)(2,1)S(1)}, u32[]{:S(2)}, u32[]{:S(2)}) %collective-permute-start.4) | collective-permute-done | bytes 65568 | tf_op jit(solution)/shard_map/ppermute | solution.py:337
  68.8 2.4 %collective-permute-done.5 = f16[128,256]{1,0:T(8,128)(2,1)S(1)} collective-permute-done((f16[128,256]{1,0:T(8,128)(2,1)S(1)}, f16[128,256]{1,0:T(8,128)(2,1)S(1)}, u32[]{:S(2)}, u32[]{:S(2)}) %collective-permute-start.5) | collective-permute-done | bytes 65568 | tf_op jit(solution)/shard_map/ppermute | solution.py:337
  71.9 1.1 shard_map.79
  74.1 2.8 %collective-permute-start.8 = (f32[128,128]{1,0:T(8,128)S(1)}, f32[128,128]{1,0:T(8,128)S(1)}, u32[]{:S(2)}, u32[]{:S(2)}) collective-permute-start(f32[128,128]{1,0:T(8,128)S(1)} %get-tuple-element.48), channel_id=1, source_target_pairs={{0,16},{8,24},{16,0},{24,8},{1,17},{9,25},{17,1},{25,9},{2,18},{10... | collective-permute-start | bytes 196616 | tf_op jit(solution)/shard_map/ppermute | solution.py:337
  78.8 1.2 collective-permute-done.8.s2_ref
  79.9 1.3 collective-permute-done.9.s3_ref
  81.9 3.2 %local_reads.2 = (bf16[4,256,128]{2,1,0:T(8,128)(2,1)S(1)}, bf16[4,256,128]{2,1,0:T(8,128)(2,1)S(1)}, f32[4,256,128]{2,1,0:T(8,128)S(1)}) custom-call(s32[4]{0:T(128)S(1)} %pad_add_fusion.w_ref, bf16[256,1024]{1,0:T(8,128)(2,1)} %q_ref.3, bf16[256,1024]{1,0:T(8,128)(2,1)} %k_ref.7, bf16[4,256,256]{2,1,0:T(8,128)(2,1)S(1)} %get-tuple-element.32.xh_ref, ...), custom_call_target="tpu_custom_call" | custom-call | tf_op jit(solution)/shard_map/local_reads/pallas_call | solution.py:240
  85.2 3.2 %local_reads.3 = (bf16[4,256,128]{2,1,0:T(8,128)(2,1)S(1)}, bf16[4,256,128]{2,1,0:T(8,128)(2,1)S(1)}, f32[4,256,128]{2,1,0:T(8,128)S(1)}) custom-call(s32[4]{0:T(128)S(1)} %pad_add_fusion.w_ref, bf16[256,1024]{1,0:T(8,128)(2,1)} %q_ref.3, bf16[256,1024]{1,0:T(8,128)(2,1)} %k_ref.7, bf16[4,256,256]{2,1,0:T(8,128)(2,1)S(1)} %get-tuple-element.50.xh_ref, ...), custom_call_target="tpu_custom_call" | custom-call | tf_op jit(solution)/shard_map/local_reads/pallas_call | solution.py:240
  90.9 2.8 %collective-permute-start.17 = (bf16[256,512]{1,0:T(8,128)(2,1)S(1)}, bf16[256,512]{1,0:T(8,128)(2,1)S(1)}, u32[]{:S(2)}, u32[]{:S(2)}) collective-permute-start(bf16[256,512]{1,0:T(8,128)(2,1)S(1)} %shard_map.82.refs_1_), channel_id=1, source_target_pairs={{0,96},{32,0},{64,32},{96,64},{1,97},{33,1},{65,33},{97,65},{2,98}... | collective-permute-start | bytes 786440 | tf_op jit(solution)/shard_map/ppermute | solution.py:337
  94.1 1.6 %collective-permute-start.19 = (bf16[256,512]{1,0:T(8,128)(2,1)S(1)}, bf16[256,512]{1,0:T(8,128)(2,1)S(1)}, u32[]{:S(2)}, u32[]{:S(2)}) collective-permute-start(bf16[256,512]{1,0:T(8,128)(2,1)S(1)} %shard_map.82.refs_1_), channel_id=1, source_target_pairs={{0,32},{32,64},{64,96},{96,0},{1,33},{33,65},{65,97},{97,1},{2,34}... | collective-permute-start | bytes 786440 | tf_op jit(solution)/shard_map/ppermute | solution.py:337
  95.7 2.8 %collective-permute-done.15.refs_2_ = bf16[256,512]{1,0:T(8,128)(2,1)S(1)} collective-permute-done((bf16[256,512]{1,0:T(8,128)(2,1)S(1)}, bf16[256,512]{1,0:T(8,128)(2,1)S(1)}, u32[]{:S(2)}, u32[]{:S(2)}) %collective-permute-start.15) | collective-permute-done | bytes 262176 | tf_op jit(solution)/shard_map/ppermute | solution.py:337
  99.4 3.7 %collective-permute-start.18 = (bf16[256,512]{1,0:T(8,128)(2,1)S(1)}, bf16[256,512]{1,0:T(8,128)(2,1)S(1)}, u32[]{:S(2)}, u32[]{:S(2)}) collective-permute-start(bf16[256,512]{1,0:T(8,128)(2,1)S(1)} %collective-permute-done.17.refs_5_), channel_id=1, source_target_pairs={{0,96},{32,0},{64,32},{96,64},{1,97},{33,1},{65,33},{97,65},{2,98}... | collective-permute-start | bytes 786440 | tf_op jit(solution)/shard_map/ppermute | solution.py:337
  103.3 1.7 %collective-permute-done.20.refs_4_ = bf16[256,512]{1,0:T(8,128)(2,1)S(1)} collective-permute-done((bf16[256,512]{1,0:T(8,128)(2,1)S(1)}, bf16[256,512]{1,0:T(8,128)(2,1)S(1)}, u32[]{:S(2)}, u32[]{:S(2)}) %collective-permute-start.20) | collective-permute-done | bytes 262176 | tf_op jit(solution)/shard_map/ppermute | solution.py:337
  105.0 2.4 %shard_map.83 = (f32[512,1024]{1,0:T(8,128)S(1)}, f32[512,1024]{1,0:T(8,128)S(1)}) custom-call(s32[4]{0:T(128)S(1)} %pad_add_fusion.w_ref, bf16[4,256,1024]{2,1,0:T(8,128)(2,1)S(1)} %pad_maximum_fusion.cot_ref, bf16[256,512]{1,0:T(8,128)(2,1)S(1)} %shard_map.81.refs_0_, bf16[256,512]{1,0:T(8,128)(2,1)S(1)} %shard_map.82.refs_1_, ...), custom_call_target="tpu_custom_call" | custom-call | tf_op jit(solution)/shard_map/pallas_call | solution.py:271
  107.4 2.7 %collective-permute-done.16.b_ref = bf16[256,512]{1,0:T(8,128)(2,1)S(1)} collective-permute-done((bf16[256,512]{1,0:T(8,128)(2,1)S(1)}, bf16[256,512]{1,0:T(8,128)(2,1)S(1)}, u32[]{:S(2)}, u32[]{:S(2)}) %collective-permute-start.16) | collective-permute-done | bytes 262176 | tf_op jit(solution)/shard_map/ppermute | solution.py:337
  111.7 1.2 collective-permute-start.21
  113.9 1.3 collective-permute-done.21.got_ref
  116.4 1.7 %collective-permute-start.24 = (bf16[256,512]{1,0:T(8,128)(2,1)S(1)}, bf16[256,512]{1,0:T(8,128)(2,1)S(1)}, u32[]{:S(2)}, u32[]{:S(2)}) collective-permute-start(bf16[256,512]{1,0:T(8,128)(2,1)S(1)} %get-tuple-element.61), channel_id=1, source_target_pairs={{0,24},{8,16},{16,8},{24,0},{1,25},{9,17},{17,9},{25,1},{2,26},{10... | collective-permute-start | bytes 786440 | tf_op jit(solution)/shard_map/ppermute | solution.py:342
  119.0 5.6 %collective-permute-done.22 = bf16[256,512]{1,0:T(8,128)(2,1)S(1)} collective-permute-done((bf16[256,512]{1,0:T(8,128)(2,1)S(1)}, bf16[256,512]{1,0:T(8,128)(2,1)S(1)}, u32[]{:S(2)}, u32[]{:S(2)}) %collective-permute-start.22) | collective-permute-done | bytes 262176 | tf_op jit(solution)/shard_map/ppermute | solution.py:342
  124.5 2.1 %collective-permute-start.23 = (bf16[128,512]{1,0:T(8,128)(2,1)S(1)}, bf16[128,512]{1,0:T(8,128)(2,1)S(1)}, u32[]{:S(2)}, u32[]{:S(2)}) collective-permute-start(bf16[128,512]{1,0:T(8,128)(2,1)S(1)} %add_convert_fusion.1), channel_id=1, source_target_pairs={{0,24},{8,16},{16,8},{24,0},{1,25},{9,17},{17,9},{25,1},{2,26},{10... | collective-permute-start | bytes 393224 | tf_op jit(solution)/shard_map/ppermute | solution.py:342
  126.8 4.1 %collective-permute-done.23 = bf16[128,512]{1,0:T(8,128)(2,1)S(1)} collective-permute-done((bf16[128,512]{1,0:T(8,128)(2,1)S(1)}, bf16[128,512]{1,0:T(8,128)(2,1)S(1)}, u32[]{:S(2)}, u32[]{:S(2)}) %collective-permute-start.23) | collective-permute-done | bytes 131104 | tf_op jit(solution)/shard_map/ppermute | solution.py:342
  (55 shorter events, 18.8 us)
Async XLA Ops:
  0.6 1.7 %collective-permute-start.12 = (bf16[256,1024]{1,0:T(8,128)(2,1)}, bf16[256,1024]{1,0:T(8,128)(2,1)S(1)}, u32[]{:S(2)}, u32[]{:S(2)}) collective-permute-start(bf16[256,1024]{1,0:T(8,128)(2,1)} %param.11), channel_id=1, source_target_pairs={{0,0},{1,32},{2,64},{3,96},{32,1},{33,33},{34,65},{35,97},{64,2},{... | collective-permute-start | bytes 1572872 | tf_op jit(solution)/shard_map/ppermute | solution.py:349
  2.3 36.8 %collective-permute-start.13 = (bf16[256,1024]{1,0:T(8,128)(2,1)S(1)}, bf16[256,1024]{1,0:T(8,128)(2,1)S(1)}, u32[]{:S(2)}, u32[]{:S(2)}) collective-permute-start(bf16[256,1024]{1,0:T(8,128)(2,1)S(1)} %collective-permute-done.12), channel_id=1, source_target_pairs={{0,1},{1,0},{2,3},{3,2},{4,5},{5,4},{6,7},{7,6},{8,9},{9,8},{10,11... | collective-permute-start | bytes 1572872 | tf_op jit(solution)/shard_map/ppermute | solution.py:342
  33.9 18.4 %collective-permute-start = (f32[4,128,256]{2,1,0:T(8,128)S(1)}, f32[4,128,256]{2,1,0:T(8,128)S(1)}, u32[]{:S(2)}, u32[]{:S(2)}) collective-permute-start(f32[4,128,256]{2,1,0:T(8,128)S(1)} %get-tuple-element.35), channel_id=1, source_target_pairs={{0,4},{4,0},{1,5},{5,1},{2,6},{6,2},{3,7},{7,3},{8,12},{12,8},{9,1... | collective-permute-start | bytes 1572872 | tf_op jit(solution)/shard_map/ppermute | solution.py:342
  39.2 63.9 %collective-permute-start.14 = (bf16[2,256,1024]{2,1,0:T(8,128)(2,1)S(1)}, bf16[2,256,1024]{2,1,0:T(8,128)(2,1)S(1)}, u32[]{:S(2)}, u32[]{:S(2)}) collective-permute-start(bf16[2,256,1024]{2,1,0:T(8,128)(2,1)S(1)} %pad_maximum_fusion.1), channel_id=1, source_target_pairs={{0,3},{1,2},{2,1},{3,0},{4,7},{5,6},{6,5},{7,4},{8,11},{9,10},{10,... | collective-permute-start | bytes 3145736 | tf_op jit(solution)/shard_map/ppermute | solution.py:342
  52.2 32.9 %collective-permute-start.10 = (f32[4,128,256]{2,1,0:T(8,128)S(1)}, f32[4,128,256]{2,1,0:T(8,128)S(1)}, u32[]{:S(2)}, u32[]{:S(2)}) collective-permute-start(f32[4,128,256]{2,1,0:T(8,128)S(1)} %get-tuple-element.39.own_ref), channel_id=1, source_target_pairs={{0,4},{4,0},{1,5},{5,1},{2,6},{6,2},{3,7},{7,3},{8,12},{12,8},{9,1... | collective-permute-start | bytes 1572872 | tf_op jit(solution)/shard_map/ppermute | solution.py:342
  53.2 6.9 %collective-permute-start.1 = (f16[128,256]{1,0:T(8,128)(2,1)S(1)}, f16[128,256]{1,0:T(8,128)(2,1)S(1)}, u32[]{:S(2)}, u32[]{:S(2)}) collective-permute-start(f16[128,256]{1,0:T(8,128)(2,1)S(1)} %convert_element_type.56), channel_id=1, source_target_pairs={{0,8},{8,16},{16,24},{24,0},{1,9},{9,17},{17,25},{25,1},{2,10},{10... | collective-permute-start | bytes 196616 | tf_op jit(solution)/shard_map/ppermute | solution.py:337
  55.2 7.4 %collective-permute-start.2 = (f16[128,256]{1,0:T(8,128)(2,1)S(1)}, f16[128,256]{1,0:T(8,128)(2,1)S(1)}, u32[]{:S(2)}, u32[]{:S(2)}) collective-permute-start(f16[128,256]{1,0:T(8,128)(2,1)S(1)} %convert_element_type.58), channel_id=1, source_target_pairs={{0,16},{8,24},{16,0},{24,8},{1,17},{9,25},{17,1},{25,9},{2,18},{10... | collective-permute-start | bytes 196616 | tf_op jit(solution)/shard_map/ppermute | solution.py:337
  58.9 4.3 %collective-permute-start.3 = (f16[128,256]{1,0:T(8,128)(2,1)S(1)}, f16[128,256]{1,0:T(8,128)(2,1)S(1)}, u32[]{:S(2)}, u32[]{:S(2)}) collective-permute-start(f16[128,256]{1,0:T(8,128)(2,1)S(1)} %convert_element_type.60), channel_id=1, source_target_pairs={{0,24},{8,0},{16,8},{24,16},{1,25},{9,1},{17,9},{25,17},{2,26},{10... | collective-permute-start | bytes 196616 | tf_op jit(solution)/shard_map/ppermute | solution.py:337
  64.5 4.3 %collective-permute-start.4 = (f16[128,256]{1,0:T(8,128)(2,1)S(1)}, f16[128,256]{1,0:T(8,128)(2,1)S(1)}, u32[]{:S(2)}, u32[]{:S(2)}) collective-permute-start(f16[128,256]{1,0:T(8,128)(2,1)S(1)} %convert_element_type.62), channel_id=1, source_target_pairs={{0,96},{32,0},{64,32},{96,64},{1,97},{33,1},{65,33},{97,65},{2,98}... | collective-permute-start | bytes 196616 | tf_op jit(solution)/shard_map/ppermute | solution.py:337
  65.3 5.9 %collective-permute-start.5 = (f16[128,256]{1,0:T(8,128)(2,1)S(1)}, f16[128,256]{1,0:T(8,128)(2,1)S(1)}, u32[]{:S(2)}, u32[]{:S(2)}) collective-permute-start(f16[128,256]{1,0:T(8,128)(2,1)S(1)} %convert_element_type.62), channel_id=1, source_target_pairs={{0,64},{32,96},{64,0},{96,32},{1,65},{33,97},{65,1},{97,33},{2,66}... | collective-permute-start | bytes 196616 | tf_op jit(solution)/shard_map/ppermute | solution.py:337
  65.4 6.5 %collective-permute-start.6 = (f16[128,256]{1,0:T(8,128)(2,1)S(1)}, f16[128,256]{1,0:T(8,128)(2,1)S(1)}, u32[]{:S(2)}, u32[]{:S(2)}) collective-permute-start(f16[128,256]{1,0:T(8,128)(2,1)S(1)} %convert_element_type.62), channel_id=1, source_target_pairs={{0,32},{32,64},{64,96},{96,0},{1,33},{33,65},{65,97},{97,1},{2,34}... | collective-permute-start | bytes 196616 | tf_op jit(solution)/shard_map/ppermute | solution.py:337
  73.0 5.7 %collective-permute-start.7 = (f32[128,128]{1,0:T(8,128)S(1)}, f32[128,128]{1,0:T(8,128)S(1)}, u32[]{:S(2)}, u32[]{:S(2)}) collective-permute-start(f32[128,128]{1,0:T(8,128)S(1)} %get-tuple-element.47), channel_id=1, source_target_pairs={{0,8},{8,16},{16,24},{24,0},{1,9},{9,17},{17,25},{25,1},{2,10},{10... | collective-permute-start | bytes 196616 | tf_op jit(solution)/shard_map/ppermute | solution.py:337
  74.1 5.8 %collective-permute-start.8 = (f32[128,128]{1,0:T(8,128)S(1)}, f32[128,128]{1,0:T(8,128)S(1)}, u32[]{:S(2)}, u32[]{:S(2)}) collective-permute-start(f32[128,128]{1,0:T(8,128)S(1)} %get-tuple-element.48), channel_id=1, source_target_pairs={{0,16},{8,24},{16,0},{24,8},{1,17},{9,25},{17,1},{25,9},{2,18},{10... | collective-permute-start | bytes 196616 | tf_op jit(solution)/shard_map/ppermute | solution.py:337
  77.0 4.3 %collective-permute-start.9 = (f32[128,128]{1,0:T(8,128)S(1)}, f32[128,128]{1,0:T(8,128)S(1)}, u32[]{:S(2)}, u32[]{:S(2)}) collective-permute-start(f32[128,128]{1,0:T(8,128)S(1)} %get-tuple-element.49), channel_id=1, source_target_pairs={{0,24},{8,0},{16,8},{24,16},{1,25},{9,1},{17,9},{25,17},{2,26},{10... | collective-permute-start | bytes 196616 | tf_op jit(solution)/shard_map/ppermute | solution.py:337
  81.8 8.1 %collective-permute-start.11 = (f32[4,128,128]{2,1,0:T(8,128)S(1)}, f32[4,128,128]{2,1,0:T(8,128)S(1)}, u32[]{:S(2)}, u32[]{:S(2)}) collective-permute-start(f32[4,128,128]{2,1,0:T(8,128)S(1)} %shard_map.80.s_ref), channel_id=1, source_target_pairs={{0,4},{4,0},{1,5},{5,1},{2,6},{6,2},{3,7},{7,3},{8,12},{12,8},{9,1... | collective-permute-start | bytes 786440 | tf_op jit(solution)/shard_map/ppermute | solution.py:342
  81.9 6.5 %copy-start = (f32[128]{0:T(128)S(1)}, f32[128]{0:T(128)}, u32[]{:S(2)}) copy-start(f32[128]{0:T(128)} %param.10) | copy-start | bytes 1540
  89.4 9.2 %collective-permute-start.15 = (bf16[256,512]{1,0:T(8,128)(2,1)S(1)}, bf16[256,512]{1,0:T(8,128)(2,1)S(1)}, u32[]{:S(2)}, u32[]{:S(2)}) collective-permute-start(bf16[256,512]{1,0:T(8,128)(2,1)S(1)} %shard_map.81.refs_0_), channel_id=1, source_target_pairs={{0,32},{32,64},{64,96},{96,0},{1,33},{33,65},{65,97},{97,1},{2,34}... | collective-permute-start | bytes 786440 | tf_op jit(solution)/shard_map/ppermute | solution.py:337
  90.9 8.5 %collective-permute-start.17 = (bf16[256,512]{1,0:T(8,128)(2,1)S(1)}, bf16[256,512]{1,0:T(8,128)(2,1)S(1)}, u32[]{:S(2)}, u32[]{:S(2)}) collective-permute-start(bf16[256,512]{1,0:T(8,128)(2,1)S(1)} %shard_map.82.refs_1_), channel_id=1, source_target_pairs={{0,96},{32,0},{64,32},{96,64},{1,97},{33,1},{65,33},{97,65},{2,98}... | collective-permute-start | bytes 786440 | tf_op jit(solution)/shard_map/ppermute | solution.py:337
  93.7 11.3 %collective-permute-start.20 = (bf16[256,512]{1,0:T(8,128)(2,1)S(1)}, bf16[256,512]{1,0:T(8,128)(2,1)S(1)}, u32[]{:S(2)}, u32[]{:S(2)}) collective-permute-start(bf16[256,512]{1,0:T(8,128)(2,1)S(1)} %shard_map.81.refs_0_), channel_id=1, source_target_pairs={{0,96},{32,0},{64,32},{96,64},{1,97},{33,1},{65,33},{97,65},{2,98}... | collective-permute-start | bytes 786440 | tf_op jit(solution)/shard_map/ppermute | solution.py:337
  94.1 10.9 %collective-permute-start.19 = (bf16[256,512]{1,0:T(8,128)(2,1)S(1)}, bf16[256,512]{1,0:T(8,128)(2,1)S(1)}, u32[]{:S(2)}, u32[]{:S(2)}) collective-permute-start(bf16[256,512]{1,0:T(8,128)(2,1)S(1)} %shard_map.82.refs_1_), channel_id=1, source_target_pairs={{0,32},{32,64},{64,96},{96,0},{1,33},{33,65},{65,97},{97,1},{2,34}... | collective-permute-start | bytes 786440 | tf_op jit(solution)/shard_map/ppermute | solution.py:337
  98.5 11.6 %collective-permute-start.16 = (bf16[256,512]{1,0:T(8,128)(2,1)S(1)}, bf16[256,512]{1,0:T(8,128)(2,1)S(1)}, u32[]{:S(2)}, u32[]{:S(2)}) collective-permute-start(bf16[256,512]{1,0:T(8,128)(2,1)S(1)} %collective-permute-done.15.refs_2_), channel_id=1, source_target_pairs={{0,32},{32,64},{64,96},{96,0},{1,33},{33,65},{65,97},{97,1},{2,34}... | collective-permute-start | bytes 786440 | tf_op jit(solution)/shard_map/ppermute | solution.py:337
  99.4 11.2 %collective-permute-start.18 = (bf16[256,512]{1,0:T(8,128)(2,1)S(1)}, bf16[256,512]{1,0:T(8,128)(2,1)S(1)}, u32[]{:S(2)}, u32[]{:S(2)}) collective-permute-start(bf16[256,512]{1,0:T(8,128)(2,1)S(1)} %collective-permute-done.17.refs_5_), channel_id=1, source_target_pairs={{0,96},{32,0},{64,32},{96,64},{1,97},{33,1},{65,33},{97,65},{2,98}... | collective-permute-start | bytes 786440 | tf_op jit(solution)/shard_map/ppermute | solution.py:337
  111.7 3.5 %collective-permute-start.21 = (bf16[512,1024]{1,0:T(8,128)(2,1)S(1)}, bf16[512,1024]{1,0:T(8,128)(2,1)S(1)}, u32[]{:S(2)}, u32[]{:S(2)}) collective-permute-start(bf16[512,1024]{1,0:T(8,128)(2,1)S(1)} %shard_map.85), channel_id=1, source_target_pairs={{0,4},{4,0},{1,5},{5,1},{2,6},{6,2},{3,7},{7,3},{8,12},{12,8},{9,1... | collective-permute-start | bytes 3145736 | tf_op jit(solution)/shard_map/ppermute | solution.py:342
  115.9 8.7 %collective-permute-start.22 = (bf16[256,512]{1,0:T(8,128)(2,1)S(1)}, bf16[256,512]{1,0:T(8,128)(2,1)S(1)}, u32[]{:S(2)}, u32[]{:S(2)}) collective-permute-start(bf16[256,512]{1,0:T(8,128)(2,1)S(1)} %get-tuple-element.59), channel_id=1, source_target_pairs={{0,8},{8,0},{16,24},{24,16},{1,9},{9,1},{17,25},{25,17},{2,10},{10... | collective-permute-start | bytes 786440 | tf_op jit(solution)/shard_map/ppermute | solution.py:342
  116.4 10.3 %collective-permute-start.24 = (bf16[256,512]{1,0:T(8,128)(2,1)S(1)}, bf16[256,512]{1,0:T(8,128)(2,1)S(1)}, u32[]{:S(2)}, u32[]{:S(2)}) collective-permute-start(bf16[256,512]{1,0:T(8,128)(2,1)S(1)} %get-tuple-element.61), channel_id=1, source_target_pairs={{0,24},{8,16},{16,8},{24,0},{1,25},{9,17},{17,9},{25,1},{2,26},{10... | collective-permute-start | bytes 786440 | tf_op jit(solution)/shard_map/ppermute | solution.py:342
  124.5 6.3 %collective-permute-start.23 = (bf16[128,512]{1,0:T(8,128)(2,1)S(1)}, bf16[128,512]{1,0:T(8,128)(2,1)S(1)}, u32[]{:S(2)}, u32[]{:S(2)}) collective-permute-start(bf16[128,512]{1,0:T(8,128)(2,1)S(1)} %add_convert_fusion.1), channel_id=1, source_target_pairs={{0,24},{8,16},{16,8},{24,0},{1,25},{9,17},{17,9},{25,1},{2,26},{10... | collective-permute-start | bytes 393224 | tf_op jit(solution)/shard_map/ppermute | solution.py:342
  126.7 5.0 %collective-permute-start.25 = (bf16[128,512]{1,0:T(8,128)(2,1)S(1)}, bf16[128,512]{1,0:T(8,128)(2,1)S(1)}, u32[]{:S(2)}, u32[]{:S(2)}) collective-permute-start(bf16[128,512]{1,0:T(8,128)(2,1)S(1)} %add_convert_fusion), channel_id=1, source_target_pairs={{0,8},{8,0},{16,24},{24,16},{1,9},{9,1},{17,25},{25,17},{2,10},{10... | collective-permute-start | bytes 393224 | tf_op jit(solution)/shard_map/ppermute | solution.py:342

commit v6 on v5

--- a/solution.py
+++ b/solution.py
@@ -347,8 +347,12 @@
     where = jnp.stack([yi, zi, ci, hi])
 
     cot = lax.ppermute(out_cotangent, ("y", "head"), [(a * 4 + b, b * 4 + a) for a in range(4) for b in range(4)])
-    cot2 = jnp.stack([cot, swap(cot, "head", 1)])
-    cots = jnp.concatenate([cot2, swap(cot2, "head", 3)])
+    cot1 = swap(cot, "head", 1)
+    cot3 = swap(cot, "head", 3)
+    t = TOK // 2
+    top = swap(cot3[:t], "head", 1)
+    low = swap(cot1[t:], "head", 3)
+    cots = jnp.stack([cot, cot1, jnp.concatenate([top, low]), cot3])
     gain = norm_gain.reshape(1, F)
     beta_rows = beta.T
     m_a, xh_a, xl_a, r_a = local_maps(False, where, key_rows, value_rows, beta_rows)
@@ -403,7 +407,7 @@
 
 def cot_rows(w_ref, cot_ref, k, part):
     d = lax.rem(w_ref[0] - k + 4, 4) ^ w_ref[3]
-    j = d ^ (d >> 1)
+    j = d
     core = half_of(part == 1, w_ref)
     return jnp.concatenate(
         [cot_ref[j, :, pl.ds(pl.multiple_of((2 * n + core) * F, F), F)] for n in range(4)], axis=1

time: 133 us -> 115 us (0.86)
  starting transfers between devices: 63.9 us -> 46.4 us
    ppermute x10 -> x12, starting transfers between devices: 39.4 us -> 17.2 us  [swap(): return lax.ppermute(x, axis, [(i, i ^ k) for i in range(n)])]
    ppermute x15, starting transfers between devices: 22.7 us -> 27.5 us  [shift(): return lax.ppermute(x, axis, [(i, (i + k) % 4) for i in range(4)])]
    ppermute x10 -> x12, waiting for transfers between devices: 16.9 us -> 15.9 us  [swap(): return lax.ppermute(x, axis, [(i, i ^ k) for i in range(n)])]
  transfers between devices with their start and end apart: 26 -> 28, of which waited for: 19 -> 18; matrix products, arithmetic and copies ran while one was open for 1% -> 1% of each run, Pallas kernels for 20% -> 18%
where the time goes in v6:
time: 115 us; the launch traced here: 114 us
  starting transfers between devices  46.4 us (40%)
  waiting for transfers between devices  36.2 us (31%)
  Pallas kernels  28.1 us (24%)
  other arithmetic  2.39 us (2%)
    ppermute x15, starting transfers between devices, shift(): return lax.ppermute(x, axis, [(i, (i + k) % 4) for i in range(4)])  27.5 us
    ppermute x15, waiting for transfers between devices, shift(): return lax.ppermute(x, axis, [(i, (i + k) % 4) for i in range(4)])  20.2 us
    ppermute x12, starting transfers between devices, swap(): return lax.ppermute(x, axis, [(i, i ^ k) for i in range(n)])  17.2 us
    ppermute x12, waiting for transfers between devices, swap(): return lax.ppermute(x, axis, [(i, i ^ k) for i in range(n)])  15.9 us
    pallas_call x2, Pallas kernels, local_maps(): pl.pallas_call(functools.partial(local_kernel, mine), grid_spec=pltpu.Pre...  10.8 us
    pallas_call x10, Pallas kernels, stage(): pl.pallas_call(kernel, in_specs=[pl.BlockSpec(memory_space=pltpu.SMEM)] +...  10.8 us
    pallas_call x2, Pallas kernels, local_reads(): pl.pallas_call(reads_kernel, grid_spec=pltpu.PrefetchScalarGridSpec(num_s...  6.47 us
  transfers between devices with their start and end apart: 28, of which 18 were waited for; matrix products, arithmetic and copies ran while one was open for 1% of the time, Pallas kernels for 18%

profile of v6, /device:TPU:0, one launch (start us, length us, event | category | flops | bytes accessed | tf_op | source)
XLA Modules:
  0.0 114.0 jit_solution(12027201409689865804)
XLA Ops:
  0.7 5.4 %local_maps.3 = (f32[4,128,256]{2,1,0:T(8,128)S(1)}, bf16[4,256,256]{2,1,0:T(8,128)(2,1)S(1)}, bf16[4,256,256]{2,1,0:T(8,128)(2,1)S(1)}, f32[1,8,256]{2,1,0:T(8,128)S(1)}) custom-call(s32[4]{0:T(128)S(1)} %pad_add_fusion.w_ref, bf16[256,1024]{1,0:T(8,128)(2,1)} %k_ref.7, bf16[256,1024]{1,0:T(8,128)(2,1)} %v_ref.3, f32[8,256]{1,0:T(8,128)} %bitcast.16), custom_call_target="tpu_custom_call" | custom-call | tf_op jit(solution)/shard_map/local_maps/pallas_call | solution.py:186
  6.2 1.7 %collective-permute-start.12 = (bf16[256,1024]{1,0:T(8,128)(2,1)}, bf16[256,1024]{1,0:T(8,128)(2,1)S(1)}, u32[]{:S(2)}, u32[]{:S(2)}) collective-permute-start(bf16[256,1024]{1,0:T(8,128)(2,1)} %param.11), channel_id=1, source_target_pairs={{0,0},{1,32},{2,64},{3,96},{32,1},{33,33},{34,65},{35,97},{64,2},{... | collective-permute-start | bytes 1572872 | tf_op jit(solution)/shard_map/ppermute | solution.py:349
  7.9 5.4 %local_maps.2 = (f32[4,128,256]{2,1,0:T(8,128)S(1)}, bf16[4,256,256]{2,1,0:T(8,128)(2,1)S(1)}, bf16[4,256,256]{2,1,0:T(8,128)(2,1)S(1)}, f32[1,8,256]{2,1,0:T(8,128)S(1)}) custom-call(s32[4]{0:T(128)S(1)} %pad_add_fusion.w_ref, bf16[256,1024]{1,0:T(8,128)(2,1)} %k_ref.7, bf16[256,1024]{1,0:T(8,128)(2,1)} %v_ref.3, f32[8,256]{1,0:T(8,128)} %bitcast.17), custom_call_target="tpu_custom_call" | custom-call | tf_op jit(solution)/shard_map/local_maps/pallas_call | solution.py:186
  14.3 2.1 %collective-permute-start.1 = (f16[128,256]{1,0:T(8,128)(2,1)S(1)}, f16[128,256]{1,0:T(8,128)(2,1)S(1)}, u32[]{:S(2)}, u32[]{:S(2)}) collective-permute-start(f16[128,256]{1,0:T(8,128)(2,1)S(1)} %convert_element_type.56), channel_id=1, source_target_pairs={{0,8},{8,16},{16,24},{24,0},{1,9},{9,17},{17,25},{25,1},{2,10},{10... | collective-permute-start | bytes 196616 | tf_op jit(solution)/shard_map/ppermute | solution.py:337
  16.4 3.7 %collective-permute-start.2 = (f16[128,256]{1,0:T(8,128)(2,1)S(1)}, f16[128,256]{1,0:T(8,128)(2,1)S(1)}, u32[]{:S(2)}, u32[]{:S(2)}) collective-permute-start(f16[128,256]{1,0:T(8,128)(2,1)S(1)} %convert_element_type.58), channel_id=1, source_target_pairs={{0,16},{8,24},{16,0},{24,8},{1,17},{9,25},{17,1},{25,9},{2,18},{10... | collective-permute-start | bytes 196616 | tf_op jit(solution)/shard_map/ppermute | solution.py:337
  21.2 2.6 %collective-permute-done.2 = f16[128,256]{1,0:T(8,128)(2,1)S(1)} collective-permute-done((f16[128,256]{1,0:T(8,128)(2,1)S(1)}, f16[128,256]{1,0:T(8,128)(2,1)S(1)}, u32[]{:S(2)}, u32[]{:S(2)}) %collective-permute-start.2) | collective-permute-done | bytes 65568 | tf_op jit(solution)/shard_map/ppermute | solution.py:337
  24.4 1.2 %shard_map.78 = (f32[3,128,256]{2,1,0:T(8,128)S(1)}, f32[128,256]{1,0:T(8,128)S(1)}) custom-call(s32[4]{0:T(128)S(1)} %pad_add_fusion.w_ref, f32[128,256]{1,0:T(8,128)S(1)} %get-tuple-element.40.m0_ref, f32[128,256]{1,0:T(8,128)S(1)} %convert_element_type.57.m1_ref, f32[128,256]{1,0:T(8,128)S(1)} %convert_element_type.59.m2_ref, ...), custom_call_target="tpu_custom_call" | custom-call | tf_op jit(solution)/shard_map/pallas_call | solution.py:271
  25.6 5.7 %collective-permute-start.4 = (f16[128,256]{1,0:T(8,128)(2,1)S(1)}, f16[128,256]{1,0:T(8,128)(2,1)S(1)}, u32[]{:S(2)}, u32[]{:S(2)}) collective-permute-start(f16[128,256]{1,0:T(8,128)(2,1)S(1)} %convert_element_type.62), channel_id=1, source_target_pairs={{0,96},{32,0},{64,32},{96,64},{1,97},{33,1},{65,33},{97,65},{2,98}... | collective-permute-start | bytes 196616 | tf_op jit(solution)/shard_map/ppermute | solution.py:337
  31.3 8.8 %collective-permute-start.14 = (bf16[256,1024]{1,0:T(8,128)(2,1)S(1)}, bf16[256,1024]{1,0:T(8,128)(2,1)S(1)}, u32[]{:S(2)}, u32[]{:S(2)}) collective-permute-start(bf16[256,1024]{1,0:T(8,128)(2,1)S(1)} %collective-permute-done.12), channel_id=1, source_target_pairs={{0,3},{1,2},{2,1},{3,0},{4,7},{5,6},{6,5},{7,4},{8,11},{9,10},{10,... | collective-permute-start | bytes 1572872 | tf_op jit(solution)/shard_map/ppermute | solution.py:342
  41.8 4.1 %collective-permute-done.5 = f16[128,256]{1,0:T(8,128)(2,1)S(1)} collective-permute-done((f16[128,256]{1,0:T(8,128)(2,1)S(1)}, f16[128,256]{1,0:T(8,128)(2,1)S(1)}, u32[]{:S(2)}, u32[]{:S(2)}) %collective-permute-start.5) | collective-permute-done | bytes 65568 | tf_op jit(solution)/shard_map/ppermute | solution.py:337
  47.7 2.2 %collective-permute-start.7 = (f32[128,128]{1,0:T(8,128)S(1)}, f32[128,128]{1,0:T(8,128)S(1)}, u32[]{:S(2)}, u32[]{:S(2)}) collective-permute-start(f32[128,128]{1,0:T(8,128)S(1)} %get-tuple-element.47), channel_id=1, source_target_pairs={{0,8},{8,16},{16,24},{24,0},{1,9},{9,17},{17,25},{25,1},{2,10},{10... | collective-permute-start | bytes 196616 | tf_op jit(solution)/shard_map/ppermute | solution.py:337
  49.9 3.6 %collective-permute-start.8 = (f32[128,128]{1,0:T(8,128)S(1)}, f32[128,128]{1,0:T(8,128)S(1)}, u32[]{:S(2)}, u32[]{:S(2)}) collective-permute-start(f32[128,128]{1,0:T(8,128)S(1)} %get-tuple-element.48), channel_id=1, source_target_pairs={{0,16},{8,24},{16,0},{24,8},{1,17},{9,25},{17,1},{25,9},{2,18},{10... | collective-permute-start | bytes 196616 | tf_op jit(solution)/shard_map/ppermute | solution.py:337
  53.5 1.2 %collective-permute-done.7.s1_ref = f32[128,128]{1,0:T(8,128)S(1)} collective-permute-done((f32[128,128]{1,0:T(8,128)S(1)}, f32[128,128]{1,0:T(8,128)S(1)}, u32[]{:S(2)}, u32[]{:S(2)}) %collective-permute-start.7) | collective-permute-done | bytes 65568 | tf_op jit(solution)/shard_map/ppermute | solution.py:337
  54.6 1.6 %collective-permute-start.9 = (f32[128,128]{1,0:T(8,128)S(1)}, f32[128,128]{1,0:T(8,128)S(1)}, u32[]{:S(2)}, u32[]{:S(2)}) collective-permute-start(f32[128,128]{1,0:T(8,128)S(1)} %get-tuple-element.49), channel_id=1, source_target_pairs={{0,24},{8,0},{16,8},{24,16},{1,25},{9,1},{17,9},{25,17},{2,26},{10... | collective-permute-start | bytes 196616 | tf_op jit(solution)/shard_map/ppermute | solution.py:337
  56.4 2.5 %collective-permute-done.9.s3_ref = f32[128,128]{1,0:T(8,128)S(1)} collective-permute-done((f32[128,128]{1,0:T(8,128)S(1)}, f32[128,128]{1,0:T(8,128)S(1)}, u32[]{:S(2)}, u32[]{:S(2)}) %collective-permute-start.9) | collective-permute-done | bytes 65568 | tf_op jit(solution)/shard_map/ppermute | solution.py:337
  59.6 3.2 %local_reads.2 = (bf16[4,256,128]{2,1,0:T(8,128)(2,1)S(1)}, bf16[4,256,128]{2,1,0:T(8,128)(2,1)S(1)}, f32[4,256,128]{2,1,0:T(8,128)S(1)}) custom-call(s32[4]{0:T(128)S(1)} %pad_add_fusion.w_ref, bf16[256,1024]{1,0:T(8,128)(2,1)} %q_ref.3, bf16[256,1024]{1,0:T(8,128)(2,1)} %k_ref.7, bf16[4,256,256]{2,1,0:T(8,128)(2,1)S(1)} %get-tuple-element.32.xh_ref, ...), custom_call_target="tpu_custom_call" | custom-call | tf_op jit(solution)/shard_map/local_reads/pallas_call | solution.py:240
  62.8 3.2 %local_reads.3 = (bf16[4,256,128]{2,1,0:T(8,128)(2,1)S(1)}, bf16[4,256,128]{2,1,0:T(8,128)(2,1)S(1)}, f32[4,256,128]{2,1,0:T(8,128)S(1)}) custom-call(s32[4]{0:T(128)S(1)} %pad_add_fusion.w_ref, bf16[256,1024]{1,0:T(8,128)(2,1)} %q_ref.3, bf16[256,1024]{1,0:T(8,128)(2,1)} %k_ref.7, bf16[4,256,256]{2,1,0:T(8,128)(2,1)S(1)} %get-tuple-element.50.xh_ref, ...), custom_call_target="tpu_custom_call" | custom-call | tf_op jit(solution)/shard_map/local_reads/pallas_call | solution.py:240
  68.1 3.3 %collective-permute-start.19 = (bf16[256,512]{1,0:T(8,128)(2,1)S(1)}, bf16[256,512]{1,0:T(8,128)(2,1)S(1)}, u32[]{:S(2)}, u32[]{:S(2)}) collective-permute-start(bf16[256,512]{1,0:T(8,128)(2,1)S(1)} %shard_map.82.refs_1_), channel_id=1, source_target_pairs={{0,96},{32,0},{64,32},{96,64},{1,97},{33,1},{65,33},{97,65},{2,98}... | collective-permute-start | bytes 786440 | tf_op jit(solution)/shard_map/ppermute | solution.py:337
  71.4 1.7 %collective-permute-start.15 = (bf16[128,1024]{1,0:T(8,128)(2,1)S(1)}, bf16[128,1024]{1,0:T(8,128)(2,1)S(1)}, u32[]{:S(2)}, u32[]{:S(2)}) collective-permute-start(bf16[128,1024]{1,0:T(8,128)(2,1)S(1)} %slice.40), channel_id=1, source_target_pairs={{0,1},{1,0},{2,3},{3,2},{4,5},{5,4},{6,7},{7,6},{8,9},{9,8},{10,11... | collective-permute-start | bytes 786440 | tf_op jit(solution)/shard_map/ppermute | solution.py:342
  73.5 1.4 %collective-permute-start.22 = (bf16[256,512]{1,0:T(8,128)(2,1)S(1)}, bf16[256,512]{1,0:T(8,128)(2,1)S(1)}, u32[]{:S(2)}, u32[]{:S(2)}) collective-permute-start(bf16[256,512]{1,0:T(8,128)(2,1)S(1)} %shard_map.81.refs_0_), channel_id=1, source_target_pairs={{0,96},{32,0},{64,32},{96,64},{1,97},{33,1},{65,33},{97,65},{2,98}... | collective-permute-start | bytes 786440 | tf_op jit(solution)/shard_map/ppermute | solution.py:337
  74.9 1.4 %collective-permute-done.17.refs_2_ = bf16[256,512]{1,0:T(8,128)(2,1)S(1)} collective-permute-done((bf16[256,512]{1,0:T(8,128)(2,1)S(1)}, bf16[256,512]{1,0:T(8,128)(2,1)S(1)}, u32[]{:S(2)}, u32[]{:S(2)}) %collective-permute-start.17) | collective-permute-done | bytes 262176 | tf_op jit(solution)/shard_map/ppermute | solution.py:337
  77.3 2.6 %collective-permute-done.15 = bf16[128,1024]{1,0:T(8,128)(2,1)S(1)} collective-permute-done((bf16[128,1024]{1,0:T(8,128)(2,1)S(1)}, bf16[128,1024]{1,0:T(8,128)(2,1)S(1)}, u32[]{:S(2)}, u32[]{:S(2)}) %collective-permute-start.15) | collective-permute-done | bytes 262176 | tf_op jit(solution)/shard_map/ppermute | solution.py:342
  80.8 2.4 %collective-permute-done.16 = bf16[128,1024]{1,0:T(8,128)(2,1)S(1)} collective-permute-done((bf16[128,1024]{1,0:T(8,128)(2,1)S(1)}, bf16[128,1024]{1,0:T(8,128)(2,1)S(1)}, u32[]{:S(2)}, u32[]{:S(2)}) %collective-permute-start.16) | collective-permute-done | bytes 262176 | tf_op jit(solution)/shard_map/ppermute | solution.py:342
  83.5 3.0 %collective-permute-done.21.refs_3_ = bf16[256,512]{1,0:T(8,128)(2,1)S(1)} collective-permute-done((bf16[256,512]{1,0:T(8,128)(2,1)S(1)}, bf16[256,512]{1,0:T(8,128)(2,1)S(1)}, u32[]{:S(2)}, u32[]{:S(2)}) %collective-permute-start.21) | collective-permute-done | bytes 262176 | tf_op jit(solution)/shard_map/ppermute | solution.py:337
  86.5 2.4 %shard_map.83 = (f32[512,1024]{1,0:T(8,128)S(1)}, f32[512,1024]{1,0:T(8,128)S(1)}) custom-call(s32[4]{0:T(128)S(1)} %pad_add_fusion.w_ref, bf16[4,256,1024]{2,1,0:T(8,128)(2,1)S(1)} %pad_maximum_fusion.cot_ref, bf16[256,512]{1,0:T(8,128)(2,1)S(1)} %shard_map.81.refs_0_, bf16[256,512]{1,0:T(8,128)(2,1)S(1)} %shard_map.82.refs_1_, ...), custom_call_target="tpu_custom_call" | custom-call | tf_op jit(solution)/shard_map/pallas_call | solution.py:271
  88.9 3.2 %collective-permute-done.18.b_ref = bf16[256,512]{1,0:T(8,128)(2,1)S(1)} collective-permute-done((bf16[256,512]{1,0:T(8,128)(2,1)S(1)}, bf16[256,512]{1,0:T(8,128)(2,1)S(1)}, u32[]{:S(2)}, u32[]{:S(2)}) %collective-permute-start.18) | collective-permute-done | bytes 262176 | tf_op jit(solution)/shard_map/ppermute | solution.py:337
  94.4 1.5 %collective-permute-done.23.got_ref = bf16[512,1024]{1,0:T(8,128)(2,1)S(1)} collective-permute-done((bf16[512,1024]{1,0:T(8,128)(2,1)S(1)}, bf16[512,1024]{1,0:T(8,128)(2,1)S(1)}, u32[]{:S(2)}, u32[]{:S(2)}) %collective-permute-start.23) | collective-permute-done | bytes 1048608 | tf_op jit(solution)/shard_map/ppermute | solution.py:342
  96.8 2.8 %collective-permute-start.26 = (bf16[256,512]{1,0:T(8,128)(2,1)S(1)}, bf16[256,512]{1,0:T(8,128)(2,1)S(1)}, u32[]{:S(2)}, u32[]{:S(2)}) collective-permute-start(bf16[256,512]{1,0:T(8,128)(2,1)S(1)} %get-tuple-element.61), channel_id=1, source_target_pairs={{0,24},{8,16},{16,8},{24,0},{1,25},{9,17},{17,9},{25,1},{2,26},{10... | collective-permute-start | bytes 786440 | tf_op jit(solution)/shard_map/ppermute | solution.py:342
  100.6 4.5 %collective-permute-done.24 = bf16[256,512]{1,0:T(8,128)(2,1)S(1)} collective-permute-done((bf16[256,512]{1,0:T(8,128)(2,1)S(1)}, bf16[256,512]{1,0:T(8,128)(2,1)S(1)}, u32[]{:S(2)}, u32[]{:S(2)}) %collective-permute-start.24) | collective-permute-done | bytes 262176 | tf_op jit(solution)/shard_map/ppermute | solution.py:342
  105.1 2.9 %collective-permute-start.25 = (bf16[128,512]{1,0:T(8,128)(2,1)S(1)}, bf16[128,512]{1,0:T(8,128)(2,1)S(1)}, u32[]{:S(2)}, u32[]{:S(2)}) collective-permute-start(bf16[128,512]{1,0:T(8,128)(2,1)S(1)} %add_convert_fusion.1), channel_id=1, source_target_pairs={{0,24},{8,16},{16,8},{24,0},{1,25},{9,17},{17,9},{25,1},{2,26},{10... | collective-permute-start | bytes 393224 | tf_op jit(solution)/shard_map/ppermute | solution.py:342
  108.1 3.2 %collective-permute-done.25 = bf16[128,512]{1,0:T(8,128)(2,1)S(1)} collective-permute-done((bf16[128,512]{1,0:T(8,128)(2,1)S(1)}, bf16[128,512]{1,0:T(8,128)(2,1)S(1)}, u32[]{:S(2)}, u32[]{:S(2)}) %collective-permute-start.25) | collective-permute-done | bytes 131104 | tf_op jit(solution)/shard_map/ppermute | solution.py:342
  111.4 1.7 %collective-permute-done.27 = bf16[128,512]{1,0:T(8,128)(2,1)S(1)} collective-permute-done((bf16[128,512]{1,0:T(8,128)(2,1)S(1)}, bf16[128,512]{1,0:T(8,128)(2,1)S(1)}, u32[]{:S(2)}, u32[]{:S(2)}) %collective-permute-start.27) | collective-permute-done | bytes 131104 | tf_op jit(solution)/shard_map/ppermute | solution.py:342
  (61 shorter events, 16.9 us)
Async XLA Ops:
  6.1 7.2 %collective-permute-start = (f32[4,128,256]{2,1,0:T(8,128)S(1)}, f32[4,128,256]{2,1,0:T(8,128)S(1)}, u32[]{:S(2)}, u32[]{:S(2)}) collective-permute-start(f32[4,128,256]{2,1,0:T(8,128)S(1)} %get-tuple-element.35), channel_id=1, source_target_pairs={{0,4},{4,0},{1,5},{5,1},{2,6},{6,2},{3,7},{7,3},{8,12},{12,8},{9,1... | collective-permute-start | bytes 1572872 | tf_op jit(solution)/shard_map/ppermute | solution.py:342
  6.2 25.1 %collective-permute-start.12 = (bf16[256,1024]{1,0:T(8,128)(2,1)}, bf16[256,1024]{1,0:T(8,128)(2,1)S(1)}, u32[]{:S(2)}, u32[]{:S(2)}) collective-permute-start(bf16[256,1024]{1,0:T(8,128)(2,1)} %param.11), channel_id=1, source_target_pairs={{0,0},{1,32},{2,64},{3,96},{32,1},{33,33},{34,65},{35,97},{64,2},{... | collective-permute-start | bytes 1572872 | tf_op jit(solution)/shard_map/ppermute | solution.py:349
  14.3 7.0 %collective-permute-start.1 = (f16[128,256]{1,0:T(8,128)(2,1)S(1)}, f16[128,256]{1,0:T(8,128)(2,1)S(1)}, u32[]{:S(2)}, u32[]{:S(2)}) collective-permute-start(f16[128,256]{1,0:T(8,128)(2,1)S(1)} %convert_element_type.56), channel_id=1, source_target_pairs={{0,8},{8,16},{16,24},{24,0},{1,9},{9,17},{17,25},{25,1},{2,10},{10... | collective-permute-start | bytes 196616 | tf_op jit(solution)/shard_map/ppermute | solution.py:337
  16.4 7.4 %collective-permute-start.2 = (f16[128,256]{1,0:T(8,128)(2,1)S(1)}, f16[128,256]{1,0:T(8,128)(2,1)S(1)}, u32[]{:S(2)}, u32[]{:S(2)}) collective-permute-start(f16[128,256]{1,0:T(8,128)(2,1)S(1)} %convert_element_type.58), channel_id=1, source_target_pairs={{0,16},{8,24},{16,0},{24,8},{1,17},{9,25},{17,1},{25,9},{2,18},{10... | collective-permute-start | bytes 196616 | tf_op jit(solution)/shard_map/ppermute | solution.py:337
  20.1 4.3 %collective-permute-start.3 = (f16[128,256]{1,0:T(8,128)(2,1)S(1)}, f16[128,256]{1,0:T(8,128)(2,1)S(1)}, u32[]{:S(2)}, u32[]{:S(2)}) collective-permute-start(f16[128,256]{1,0:T(8,128)(2,1)S(1)} %convert_element_type.60), channel_id=1, source_target_pairs={{0,24},{8,0},{16,8},{24,16},{1,25},{9,1},{17,9},{25,17},{2,26},{10... | collective-permute-start | bytes 196616 | tf_op jit(solution)/shard_map/ppermute | solution.py:337
  21.1 41.7 %collective-permute-start.10 = (f32[4,128,256]{2,1,0:T(8,128)S(1)}, f32[4,128,256]{2,1,0:T(8,128)S(1)}, u32[]{:S(2)}, u32[]{:S(2)}) collective-permute-start(f32[4,128,256]{2,1,0:T(8,128)S(1)} %get-tuple-element.39.own_ref), channel_id=1, source_target_pairs={{0,4},{4,0},{1,5},{5,1},{2,6},{6,2},{3,7},{7,3},{8,12},{12,8},{9,1... | collective-permute-start | bytes 1572872 | tf_op jit(solution)/shard_map/ppermute | solution.py:342
  25.6 15.4 %collective-permute-start.4 = (f16[128,256]{1,0:T(8,128)(2,1)S(1)}, f16[128,256]{1,0:T(8,128)(2,1)S(1)}, u32[]{:S(2)}, u32[]{:S(2)}) collective-permute-start(f16[128,256]{1,0:T(8,128)(2,1)S(1)} %convert_element_type.62), channel_id=1, source_target_pairs={{0,96},{32,0},{64,32},{96,64},{1,97},{33,1},{65,33},{97,65},{2,98}... | collective-permute-start | bytes 196616 | tf_op jit(solution)/shard_map/ppermute | solution.py:337
  31.3 40.0 %collective-permute-start.14 = (bf16[256,1024]{1,0:T(8,128)(2,1)S(1)}, bf16[256,1024]{1,0:T(8,128)(2,1)S(1)}, u32[]{:S(2)}, u32[]{:S(2)}) collective-permute-start(bf16[256,1024]{1,0:T(8,128)(2,1)S(1)} %collective-permute-done.12), channel_id=1, source_target_pairs={{0,3},{1,2},{2,1},{3,0},{4,7},{5,6},{6,5},{7,4},{8,11},{9,10},{10,... | collective-permute-start | bytes 1572872 | tf_op jit(solution)/shard_map/ppermute | solution.py:342
  40.1 33.0 %collective-permute-start.13 = (bf16[256,1024]{1,0:T(8,128)(2,1)S(1)}, bf16[256,1024]{1,0:T(8,128)(2,1)S(1)}, u32[]{:S(2)}, u32[]{:S(2)}) collective-permute-start(bf16[256,1024]{1,0:T(8,128)(2,1)S(1)} %collective-permute-done.12), channel_id=1, source_target_pairs={{0,1},{1,0},{2,3},{3,2},{4,5},{5,4},{6,7},{7,6},{8,9},{9,8},{10,11... | collective-permute-start | bytes 1572872 | tf_op jit(solution)/shard_map/ppermute | solution.py:342
  40.1 5.8 %collective-permute-start.5 = (f16[128,256]{1,0:T(8,128)(2,1)S(1)}, f16[128,256]{1,0:T(8,128)(2,1)S(1)}, u32[]{:S(2)}, u32[]{:S(2)}) collective-permute-start(f16[128,256]{1,0:T(8,128)(2,1)S(1)} %convert_element_type.62), channel_id=1, source_target_pairs={{0,64},{32,96},{64,0},{96,32},{1,65},{33,97},{65,1},{97,33},{2,66}... | collective-permute-start | bytes 196616 | tf_op jit(solution)/shard_map/ppermute | solution.py:337
  41.0 5.6 %collective-permute-start.6 = (f16[128,256]{1,0:T(8,128)(2,1)S(1)}, f16[128,256]{1,0:T(8,128)(2,1)S(1)}, u32[]{:S(2)}, u32[]{:S(2)}) collective-permute-start(f16[128,256]{1,0:T(8,128)(2,1)S(1)} %convert_element_type.62), channel_id=1, source_target_pairs={{0,32},{32,64},{64,96},{96,0},{1,33},{33,65},{65,97},{97,1},{2,34}... | collective-permute-start | bytes 196616 | tf_op jit(solution)/shard_map/ppermute | solution.py:337
  47.7 6.9 %collective-permute-start.7 = (f32[128,128]{1,0:T(8,128)S(1)}, f32[128,128]{1,0:T(8,128)S(1)}, u32[]{:S(2)}, u32[]{:S(2)}) collective-permute-start(f32[128,128]{1,0:T(8,128)S(1)} %get-tuple-element.47), channel_id=1, source_target_pairs={{0,8},{8,16},{16,24},{24,0},{1,9},{9,17},{17,25},{25,1},{2,10},{10... | collective-permute-start | bytes 196616 | tf_op jit(solution)/shard_map/ppermute | solution.py:337
  49.9 6.5 %collective-permute-start.8 = (f32[128,128]{1,0:T(8,128)S(1)}, f32[128,128]{1,0:T(8,128)S(1)}, u32[]{:S(2)}, u32[]{:S(2)}) collective-permute-start(f32[128,128]{1,0:T(8,128)S(1)} %get-tuple-element.48), channel_id=1, source_target_pairs={{0,16},{8,24},{16,0},{24,8},{1,17},{9,25},{17,1},{25,9},{2,18},{10... | collective-permute-start | bytes 196616 | tf_op jit(solution)/shard_map/ppermute | solution.py:337
  54.6 4.3 %collective-permute-start.9 = (f32[128,128]{1,0:T(8,128)S(1)}, f32[128,128]{1,0:T(8,128)S(1)}, u32[]{:S(2)}, u32[]{:S(2)}) collective-permute-start(f32[128,128]{1,0:T(8,128)S(1)} %get-tuple-element.49), channel_id=1, source_target_pairs={{0,24},{8,0},{16,8},{24,16},{1,25},{9,1},{17,9},{25,17},{2,26},{10... | collective-permute-start | bytes 196616 | tf_op jit(solution)/shard_map/ppermute | solution.py:337
  59.5 7.7 %collective-permute-start.11 = (f32[4,128,128]{2,1,0:T(8,128)S(1)}, f32[4,128,128]{2,1,0:T(8,128)S(1)}, u32[]{:S(2)}, u32[]{:S(2)}) collective-permute-start(f32[4,128,128]{2,1,0:T(8,128)S(1)} %shard_map.80.s_ref), channel_id=1, source_target_pairs={{0,4},{4,0},{1,5},{5,1},{2,6},{6,2},{3,7},{7,3},{8,12},{12,8},{9,1... | collective-permute-start | bytes 786440 | tf_op jit(solution)/shard_map/ppermute | solution.py:342
  59.6 6.5 %copy-start = (f32[128]{0:T(128)S(1)}, f32[128]{0:T(128)}, u32[]{:S(2)}) copy-start(f32[128]{0:T(128)} %param.10) | copy-start | bytes 1540
  67.0 9.2 %collective-permute-start.17 = (bf16[256,512]{1,0:T(8,128)(2,1)S(1)}, bf16[256,512]{1,0:T(8,128)(2,1)S(1)}, u32[]{:S(2)}, u32[]{:S(2)}) collective-permute-start(bf16[256,512]{1,0:T(8,128)(2,1)S(1)} %shard_map.81.refs_0_), channel_id=1, source_target_pairs={{0,32},{32,64},{64,96},{96,0},{1,33},{33,65},{65,97},{97,1},{2,34}... | collective-permute-start | bytes 786440 | tf_op jit(solution)/shard_map/ppermute | solution.py:337
  68.1 9.0 %collective-permute-start.19 = (bf16[256,512]{1,0:T(8,128)(2,1)S(1)}, bf16[256,512]{1,0:T(8,128)(2,1)S(1)}, u32[]{:S(2)}, u32[]{:S(2)}) collective-permute-start(bf16[256,512]{1,0:T(8,128)(2,1)S(1)} %shard_map.82.refs_1_), channel_id=1, source_target_pairs={{0,96},{32,0},{64,32},{96,64},{1,97},{33,1},{65,33},{97,65},{2,98}... | collective-permute-start | bytes 786440 | tf_op jit(solution)/shard_map/ppermute | solution.py:337
  71.4 8.6 %collective-permute-start.15 = (bf16[128,1024]{1,0:T(8,128)(2,1)S(1)}, bf16[128,1024]{1,0:T(8,128)(2,1)S(1)}, u32[]{:S(2)}, u32[]{:S(2)}) collective-permute-start(bf16[128,1024]{1,0:T(8,128)(2,1)S(1)} %slice.40), channel_id=1, source_target_pairs={{0,1},{1,0},{2,3},{3,2},{4,5},{5,4},{6,7},{7,6},{8,9},{9,8},{10,11... | collective-permute-start | bytes 786440 | tf_op jit(solution)/shard_map/ppermute | solution.py:342
  73.1 10.0 %collective-permute-start.16 = (bf16[128,1024]{1,0:T(8,128)(2,1)S(1)}, bf16[128,1024]{1,0:T(8,128)(2,1)S(1)}, u32[]{:S(2)}, u32[]{:S(2)}) collective-permute-start(bf16[128,1024]{1,0:T(8,128)(2,1)S(1)} %slice.41), channel_id=1, source_target_pairs={{0,3},{1,2},{2,1},{3,0},{4,7},{5,6},{6,5},{7,4},{8,11},{9,10},{10,... | collective-permute-start | bytes 786440 | tf_op jit(solution)/shard_map/ppermute | solution.py:342
  73.5 10.0 %collective-permute-start.22 = (bf16[256,512]{1,0:T(8,128)(2,1)S(1)}, bf16[256,512]{1,0:T(8,128)(2,1)S(1)}, u32[]{:S(2)}, u32[]{:S(2)}) collective-permute-start(bf16[256,512]{1,0:T(8,128)(2,1)S(1)} %shard_map.81.refs_0_), channel_id=1, source_target_pairs={{0,96},{32,0},{64,32},{96,64},{1,97},{33,1},{65,33},{97,65},{2,98}... | collective-permute-start | bytes 786440 | tf_op jit(solution)/shard_map/ppermute | solution.py:337
  76.2 10.3 %collective-permute-start.21 = (bf16[256,512]{1,0:T(8,128)(2,1)S(1)}, bf16[256,512]{1,0:T(8,128)(2,1)S(1)}, u32[]{:S(2)}, u32[]{:S(2)}) collective-permute-start(bf16[256,512]{1,0:T(8,128)(2,1)S(1)} %shard_map.82.refs_1_), channel_id=1, source_target_pairs={{0,32},{32,64},{64,96},{96,0},{1,33},{33,65},{65,97},{97,1},{2,34}... | collective-permute-start | bytes 786440 | tf_op jit(solution)/shard_map/ppermute | solution.py:337
  77.1 15.0 %collective-permute-start.18 = (bf16[256,512]{1,0:T(8,128)(2,1)S(1)}, bf16[256,512]{1,0:T(8,128)(2,1)S(1)}, u32[]{:S(2)}, u32[]{:S(2)}) collective-permute-start(bf16[256,512]{1,0:T(8,128)(2,1)S(1)} %collective-permute-done.17.refs_2_), channel_id=1, source_target_pairs={{0,32},{32,64},{64,96},{96,0},{1,33},{33,65},{65,97},{97,1},{2,34}... | collective-permute-start | bytes 786440 | tf_op jit(solution)/shard_map/ppermute | solution.py:337
  79.9 12.2 %collective-permute-start.20 = (bf16[256,512]{1,0:T(8,128)(2,1)S(1)}, bf16[256,512]{1,0:T(8,128)(2,1)S(1)}, u32[]{:S(2)}, u32[]{:S(2)}) collective-permute-start(bf16[256,512]{1,0:T(8,128)(2,1)S(1)} %collective-permute-done.19.refs_5_), channel_id=1, source_target_pairs={{0,96},{32,0},{64,32},{96,64},{1,97},{33,1},{65,33},{97,65},{2,98}... | collective-permute-start | bytes 786440 | tf_op jit(solution)/shard_map/ppermute | solution.py:337
  93.2 2.7 %collective-permute-start.23 = (bf16[512,1024]{1,0:T(8,128)(2,1)S(1)}, bf16[512,1024]{1,0:T(8,128)(2,1)S(1)}, u32[]{:S(2)}, u32[]{:S(2)}) collective-permute-start(bf16[512,1024]{1,0:T(8,128)(2,1)S(1)} %shard_map.85), channel_id=1, source_target_pairs={{0,4},{4,0},{1,5},{5,1},{2,6},{6,2},{3,7},{7,3},{8,12},{12,8},{9,1... | collective-permute-start | bytes 3145736 | tf_op jit(solution)/shard_map/ppermute | solution.py:342
  96.6 8.4 %collective-permute-start.24 = (bf16[256,512]{1,0:T(8,128)(2,1)S(1)}, bf16[256,512]{1,0:T(8,128)(2,1)S(1)}, u32[]{:S(2)}, u32[]{:S(2)}) collective-permute-start(bf16[256,512]{1,0:T(8,128)(2,1)S(1)} %get-tuple-element.59), channel_id=1, source_target_pairs={{0,8},{8,0},{16,24},{24,16},{1,9},{9,1},{17,25},{25,17},{2,10},{10... | collective-permute-start | bytes 786440 | tf_op jit(solution)/shard_map/ppermute | solution.py:342
  96.8 11.2 %collective-permute-start.26 = (bf16[256,512]{1,0:T(8,128)(2,1)S(1)}, bf16[256,512]{1,0:T(8,128)(2,1)S(1)}, u32[]{:S(2)}, u32[]{:S(2)}) collective-permute-start(bf16[256,512]{1,0:T(8,128)(2,1)S(1)} %get-tuple-element.61), channel_id=1, source_target_pairs={{0,24},{8,16},{16,8},{24,0},{1,25},{9,17},{17,9},{25,1},{2,26},{10... | collective-permute-start | bytes 786440 | tf_op jit(solution)/shard_map/ppermute | solution.py:342
  105.1 6.3 %collective-permute-start.25 = (bf16[128,512]{1,0:T(8,128)(2,1)S(1)}, bf16[128,512]{1,0:T(8,128)(2,1)S(1)}, u32[]{:S(2)}, u32[]{:S(2)}) collective-permute-start(bf16[128,512]{1,0:T(8,128)(2,1)S(1)} %add_convert_fusion.1), channel_id=1, source_target_pairs={{0,24},{8,16},{16,8},{24,0},{1,25},{9,17},{17,9},{25,1},{2,26},{10... | collective-permute-start | bytes 393224 | tf_op jit(solution)/shard_map/ppermute | solution.py:342
  108.0 5.0 %collective-permute-start.27 = (bf16[128,512]{1,0:T(8,128)(2,1)S(1)}, bf16[128,512]{1,0:T(8,128)(2,1)S(1)}, u32[]{:S(2)}, u32[]{:S(2)}) collective-permute-start(bf16[128,512]{1,0:T(8,128)(2,1)S(1)} %add_convert_fusion), channel_id=1, source_target_pairs={{0,8},{8,0},{16,24},{24,16},{1,9},{9,1},{17,25},{25,17},{2,10},{10... | collective-permute-start | bytes 393224 | tf_op jit(solution)/shard_map/ppermute | solution.py:342
